TPU v7x, 32 devices: a whole 2x2x4 slice. The times are simulated.
32 devices in a mesh: grp: 2 (over y), kxy: 8 (over z, x), kz: 2 (over core).
Axes of the slice: x: 2, y: 2, z: 4, core: 2. Of those that a mesh axis runs over, the one named last changes fastest.
Arguments:
- start_rotation: float32 [512, 2, 128, 128], P(('grp', 'kxy', 'kz')), parts along dimension 0, may hold values from -0.06 to 1.06
- correlations: float32 [512, 2, 2, 128, 128], P(('grp', 'kxy', 'kz')), parts along dimension 0, may hold values from -1.15 to 1.15
- neighbours: int32 [512, 2], P(('grp', 'kxy', 'kz')), parts along dimension 0, may hold values from 0 to 255, as said below
Outputs:
- rotation: float32 [512, 2, 128, 128], P(('grp', 'kxy', 'kz')), parts along dimension 0
- gradient: float32 [512, 2, 128, 128], P(('grp', 'kxy', 'kz')), parts along dimension 0
- centres: float32 [4, 128], P('grp'), parts along dimension 0
There are 2 independent parts, one for each index of `grp`. A program takes and returns all parts, laid end to end along the dimension named above; each array names one. Nothing has to cross between parts.
Inputs may be any that keep to these rules, and one draw needn't show every extreme that they name: `neighbours`: entry (k, 0) is the index of the k-point one step further along kx on a periodic mesh of 4 kx planes, entry (k, 1) the one one step further along kz. Indices come in blocks of 16, each in an order of its own. Block B holds kx plane B // 4, ky half (B // 2) % 2 and kz slab B % 2; the kx neighbour of a point in block B lies in block (B + 4) mod (16); its kz neighbour lies in block B or in block B - B % 2 + (B + 1) % 2.
All inputs are finite; a program needn't handle non-finite values.
Results may differ from a plain program's by a relative error of at most 0.0003.
Values sent between devices are 32-bit elements; how exact they have to be, the bound alone decides.
No kernel may reach another device: no remote copies, remote signals or barrier semaphores. Data moves between devices by JAX's collectives and lax.ppermute only.
A program may use at most 192 MiB of HBM per device.

v0:
```python
import functools

import jax
import jax.numpy as jnp
from jax import lax
from jax.experimental import pallas as pl
from jax.experimental.pallas import tpu as pltpu
from jax.sharding import PartitionSpec as P

NS_STEPS = 3
RAW = 6
CHUNKS = (4, 4, 2)
VMEM = 48 << 20


def dot(left, right, contract):
    return lax.dot_general(left, right, ((contract), ((), ())), preferred_element_type=jnp.float32)


def split(value):
    high = value.astype(jnp.bfloat16)
    return high, (value - high.astype(jnp.float32)).astype(jnp.bfloat16)


def product(left, right, contract=((1,), (0,))):
    return dot(left[0], right[0], contract) + (
        dot(left[0], right[1], contract) + dot(left[1], right[0], contract)
    )


def both(function, pair):
    return tuple(function(half) for half in pair)


def right_form(half):
    n = half.shape[0]
    return jnp.concatenate([half, jnp.concatenate([-half[:, n:], half[:, :n]], 1)], 0)


def adjoint_right_form(half):
    n = half.shape[0]
    return jnp.concatenate([half, jnp.concatenate([half[:, n:], -half[:, :n]], 1)], 0)


def identity(n):
    rows = lax.broadcasted_iota(jnp.int32, (n, n), 0)
    return (rows == lax.broadcasted_iota(jnp.int32, (n, n), 1)).astype(jnp.float32)


def polar(pairs):
    n = pairs[0][0].shape[0]
    unit = identity(n)
    unit = jnp.concatenate([1.5 * unit, jnp.zeros_like(unit)], 1)
    current = []
    for real, imag in pairs:
        scale = 1.0 / jnp.sqrt(jnp.sum(real * real + imag * imag) / n + 1e-06)
        current.append(jnp.concatenate([real * scale, imag * scale], 1))
    for _ in range(NS_STEPS):
        left = [split(value) for value in current]
        right = [both(right_form, pair) for pair in left]
        gram = [product(a, b, ((1,), (1,))) for a, b in zip(left, right)]
        factor = [split(unit - 0.5 * value) for value in gram]
        current = [product(a, b) for a, b in zip(factor, right)]
    return current


def polar_kernel(start_ref, out_ref):
    n = start_ref.shape[-1]
    count = start_ref.shape[0]
    for i, value in enumerate(polar([(start_ref[i, 0], start_ref[i, 1]) for i in range(count)])):
        out_ref[i, 0] = value[:, :n]
        out_ref[i, 1] = value[:, n:]


def polar_call(start, step):
    block = pl.BlockSpec((step,) + start.shape[1:], lambda g: (g, 0, 0, 0))
    return pl.pallas_call(
        polar_kernel,
        grid=(start.shape[0] // step,),
        in_specs=[block],
        out_specs=block,
        out_shape=jax.ShapeDtypeStruct(start.shape, start.dtype),
        compiler_params=pltpu.CompilerParams(vmem_limit_bytes=VMEM),
        name="polar",
    )(start)


def sandwich_kernel(rotation_ref, correlation_ref, out_ref):
    for i in range(rotation_ref.shape[0]):
        left = split(jnp.concatenate([rotation_ref[i, 0].T, rotation_ref[i, 1].T], 1))
        for d in range(2):
            right = split(jnp.concatenate([correlation_ref[i, d, 0], correlation_ref[i, d, 1]], 1))
            out_ref[d, i] = product(left, both(adjoint_right_form, right))


def sandwich_call(rotation, correlations, step):
    count, _, n, _ = rotation.shape
    return pl.pallas_call(
        sandwich_kernel,
        grid=(count // step,),
        in_specs=[
            pl.BlockSpec((step, 2, n, n), lambda g: (g, 0, 0, 0)),
            pl.BlockSpec((step, 2, 2, n, n), lambda g: (g, 0, 0, 0, 0)),
        ],
        out_specs=pl.BlockSpec((2, step, n, 2 * n), lambda g: (0, g, 0, 0)),
        out_shape=jax.ShapeDtypeStruct((2, count, n, 2 * n), jnp.float32),
        compiler_params=pltpu.CompilerParams(vmem_limit_bytes=VMEM),
        name="sandwich",
    )(rotation, correlations)


def column_terms(rotated, rows_ref, i):
    n = rotated.shape[0]
    unit = identity(n)
    real = jnp.sum(rotated[:, :n] * unit, axis=0, keepdims=True)
    imag = jnp.sum(rotated[:, n:] * unit, axis=0, keepdims=True)
    phase = jnp.arctan2(imag, real)
    modulus = real * real + imag * imag
    weight_real = imag / modulus
    weight_imag = real / modulus
    rows_ref[i, 0:1] = real + phase * weight_real
    rows_ref[i, 1:2] = phase * weight_imag - imag
    rows_ref[i, 2:3] = weight_real
    rows_ref[i, 3:4] = weight_imag
    return phase


def slab_kernel(slots_ref, sandwich_ref, own_ref, received_ref, out_ref, rows_ref, total_ref):
    g = pl.program_id(0)
    step = sandwich_ref.shape[1]
    count, _, n, _ = own_ref.shape

    @pl.when(g == 0)
    def _():
        total_ref[...] = jnp.zeros_like(total_ref)

    total = jnp.zeros((1, n), jnp.float32)
    for i in range(step):
        slot = slots_ref[g * step + i]
        local = slot % count
        remote = slot >= count
        partner = [jnp.where(remote, received_ref[local, p], own_ref[local, p]) for p in range(2)]
        right = both(right_form, split(jnp.concatenate(partner, 1)))
        rotated = product(split(sandwich_ref[0, i]), right)
        out_ref[i] = rotated
        total = total + column_terms(rotated, rows_ref, i)
    total_ref[1:2] = total_ref[1:2] + total


def slab_call(slots, sandwich, own, received, step):
    _, count, n, _ = sandwich.shape
    whole = pl.BlockSpec(own.shape, lambda g, s: (0, 0, 0, 0))
    return pl.pallas_call(
        slab_kernel,
        grid_spec=pltpu.PrefetchScalarGridSpec(
            num_scalar_prefetch=1,
            grid=(count // step,),
            in_specs=[pl.BlockSpec((1, step, n, 2 * n), lambda g, s: (1, g, 0, 0)), whole, whole],
            out_specs=[
                pl.BlockSpec((step, n, 2 * n), lambda g, s: (g, 0, 0)),
                pl.BlockSpec((step, 8, n), lambda g, s: (g, 0, 0)),
                pl.BlockSpec((8, n), lambda g, s: (0, 0)),
            ],
        ),
        out_shape=[
            jax.ShapeDtypeStruct((count, n, 2 * n), jnp.float32),
            jax.ShapeDtypeStruct((count, 8, n), jnp.float32),
            jax.ShapeDtypeStruct((8, n), jnp.float32),
        ],
        compiler_params=pltpu.CompilerParams(vmem_limit_bytes=VMEM),
        name="slab",
    )(slots, sandwich, own, received)


def plane_kernel(order_ref, *refs, step, raw, earlier, carried):
    sandwich_refs, refs = refs[:step], refs[step:]
    partner_ref, refs = refs[0], refs[1:]
    total_refs, refs = refs[:earlier], refs[earlier:]
    out_ref, rows_ref, total_ref = refs[2 * carried :]
    n = partner_ref.shape[-1]
    g = pl.program_id(0)

    @pl.when(g == 0)
    def _():
        total = jnp.zeros_like(total_ref)
        for other in total_refs:
            total = total + other[...]
        total_ref[...] = total

    pairs = [(partner_ref[i, 0], partner_ref[i, 1]) for i in range(step)]
    partners = polar(pairs) if raw else [jnp.concatenate(pair, 1) for pair in pairs]
    total = jnp.zeros((1, n), jnp.float32)
    rotated = [
        product(split(sandwich_refs[i][0, 0]), both(right_form, split(partners[i]))) for i in range(step)
    ]
    for i in range(step):
        out_ref[i] = rotated[i]
        total = total + column_terms(rotated[i], rows_ref, i)
    total_ref[0:1] = total_ref[0:1] + total


def plane_call(order, sandwich, partner, first, earlier, carried, step, raw):
    _, count, n, _ = sandwich.shape
    base = first // step
    own = [
        pl.BlockSpec((1, 1, n, 2 * n), lambda g, s, i=i: (0, s[first + g * step + i], 0, 0)) for i in range(step)
    ]
    small = pl.BlockSpec((8, n), lambda g, s: (0, 0))
    anywhere = pl.BlockSpec(memory_space=pl.ANY)
    aliases = {}
    if carried:
        position = 1 + step + 1 + len(earlier)
        aliases = {position: 0, position + 1: 1}
    return pl.pallas_call(
        functools.partial(plane_kernel, step=step, raw=raw, earlier=len(earlier), carried=bool(carried)),
        grid_spec=pltpu.PrefetchScalarGridSpec(
            num_scalar_prefetch=1,
            grid=(partner.shape[0] // step,),
            in_specs=own
            + [pl.BlockSpec((step, 2, n, n), lambda g, s: (g, 0, 0, 0))]
            + [small] * len(earlier)
            + [anywhere] * len(carried),
            out_specs=[
                pl.BlockSpec((step, n, 2 * n), lambda g, s: (base + g, 0, 0)),
                pl.BlockSpec((step, 8, n), lambda g, s: (base + g, 0, 0)),
                small,
            ],
        ),
        out_shape=[
            jax.ShapeDtypeStruct((count, n, 2 * n), jnp.float32),
            jax.ShapeDtypeStruct((count, 8, n), jnp.float32),
            jax.ShapeDtypeStruct((8, n), jnp.float32),
        ],
        input_output_aliases=aliases,
        compiler_params=pltpu.CompilerParams(vmem_limit_bytes=VMEM),
        name="plane",
    )(order, *([sandwich] * step), partner, *earlier, *carried)


def gradient_kernel(slots_ref, *refs, step, everything):
    totals, refs = refs[:2], refs[2:]
    plane_refs, refs = refs[:step], refs[step:]
    plane_rows, refs = refs[:step], refs[step:]
    slab_ref, slab_rows, out_ref, centres_ref = refs
    n = slab_ref.shape[1]
    centres = (totals[0][0:2] + totals[1][0:2]) / (-2.0 * everything)
    centres_ref[...] = centres
    for i in range(step):
        real = imag = None
        for d, (matrix, rows) in enumerate(((plane_refs[i], plane_rows[i]), (slab_ref, slab_rows))):
            j = 0 if d == 0 else i
            centre = centres[d : d + 1]
            v_real = 2.0 * (rows[j, 0:1] + centre * rows[j, 2:3])
            v_imag = 2.0 * (rows[j, 1:2] + centre * rows[j, 3:4])
            m_real = matrix[j, :, :n]
            m_imag = matrix[j, :, n:]
            y_real = m_real * v_real - m_imag * v_imag
            y_imag = m_real * v_imag + m_imag * v_real
            real = y_real if d == 0 else real + y_real
            imag = y_imag if d == 0 else imag + y_imag
        out_ref[i, 0] = real - real.T
        out_ref[i, 1] = imag + imag.T


def gradient_call(slots, totals, plane, plane_rows, slab, slab_rows, everything, step):
    count, n, _ = slab.shape
    small = pl.BlockSpec((8, n), lambda g, s: (0, 0))
    picked = [
        pl.BlockSpec((1, rows, width), lambda g, s, i=i: (s[g * step + i], 0, 0))
        for rows, width in ((n, 2 * n), (8, n))
        for i in range(step)
    ]
    return pl.pallas_call(
        functools.partial(gradient_kernel, step=step, everything=everything),
        grid_spec=pltpu.PrefetchScalarGridSpec(
            num_scalar_prefetch=1,
            grid=(count // step,),
            in_specs=[small, small]
            + picked
            + [
                pl.BlockSpec((step, n, 2 * n), lambda g, s: (g, 0, 0)),
                pl.BlockSpec((step, 8, n), lambda g, s: (g, 0, 0)),
            ],
            out_specs=[
                pl.BlockSpec((step, 2, n, n), lambda g, s: (g, 0, 0, 0)),
                pl.BlockSpec((2, n), lambda g, s: (0, 0)),
            ],
        ),
        out_shape=[
            jax.ShapeDtypeStruct((count, 2, n, n), jnp.float32),
            jax.ShapeDtypeStruct((2, n), jnp.float32),
        ],
        compiler_params=pltpu.CompilerParams(vmem_limit_bytes=VMEM),
        name="gradient",
    )(slots, *totals, *([plane] * step), *([plane_rows] * step), slab, slab_rows)


def shifted(value, axis, steps):
    count = lax.axis_size(axis)
    return lax.ppermute(value, axis, [(source, (source + steps) % count) for source in range(count)])


def reduce_parts(value):
    count = lax.axis_size("kxy")
    if lax.axis_size("kz") != 2 or count & (count - 1) or count < 2:
        return lax.psum(value, ("kxy", "kz")), jnp.zeros_like(value)
    value = value + shifted(value, "kz", 1)
    distance = 1
    while True:
        other = lax.ppermute(value, "kxy", [(source, source ^ distance) for source in range(count)])
        distance *= 2
        if distance == count:
            return value, other
        value = value + other


def body(start_rotation, correlations, neighbours):
    count = start_rotation.shape[0]
    block_index = lax.axis_index("kxy") * lax.axis_size("kz") + lax.axis_index("kz")
    everything = count * lax.axis_size("kxy") * lax.axis_size("kz")
    plane_slots = neighbours[:, 0] % count
    positions = jnp.arange(count, dtype=jnp.int32)
    order = jnp.max(jnp.where(plane_slots[:, None] == positions[None], positions[:, None], 0), axis=0)
    remote = (neighbours[:, 1] // count != block_index).astype(jnp.int32)
    slab_slots = neighbours[:, 1] % count + count * remote

    received = [shifted(start_rotation[:RAW], "kxy", -2)]
    rotation = polar_call(start_rotation, 4)
    first = RAW
    bounds = []
    for size in CHUNKS:
        bounds.append((first, size))
        received.append(shifted(rotation[first : first + size], "kxy", -2))
        first += size
    from_slab = shifted(rotation, "kz", -1)
    sandwich = sandwich_call(rotation, correlations, 4)
    slab, slab_rows, slab_total = slab_call(slab_slots, sandwich, rotation, from_slab, 4)
    plane, plane_rows, total = plane_call(order, sandwich, received[0], 0, [slab_total], [], 2, True)
    for (first, size), partner in zip(bounds, received[1:]):
        plane, plane_rows, total = plane_call(
            order, sandwich, partner, first, [total], [plane, plane_rows], 2, False
        )
    gradient, centres = gradient_call(
        plane_slots, reduce_parts(total), plane, plane_rows, slab, slab_rows, everything, 4
    )
    return (rotation, gradient, centres)


def solution(mesh):
    in_specs = (
        P(("grp", "kxy", "kz"), None, None, None),
        P(("grp", "kxy", "kz"), None, None, None, None),
        P(("grp", "kxy", "kz"), None),
    )
    out_specs = (
        P(("grp", "kxy", "kz"), None, None, None),
        P(("grp", "kxy", "kz"), None, None, None),
        P("grp", None),
    )
    return jax.shard_map(body, mesh=mesh, in_specs=in_specs, out_specs=out_specs, check_vma=False)
```

profile of v0, /device:TPU:0, one launch (start us, length us, event | category | flops | bytes accessed | tf_op | source)
XLA Modules:
  0.0 84.2 jit_solution(4727489227995380676)
XLA Ops:
  0.6 1.6 %copy-done.2 = f32[16,2,128,128]{3,2,1,0:T(8,128)S(1)} copy-done((f32[16,2,128,128]{3,2,1,0:T(8,128)S(1)}, f32[16,2,128,128]{3,2,1,0:T(8,128)}, u32[]{:S(2)}) %copy-start.2) | copy-done | bytes 2097176
  2.2 11.2 %polar.1.rotation_ref.own_ref = f32[16,2,128,128]{3,2,1,0:T(8,128)} custom-call(f32[16,2,128,128]{3,2,1,0:T(8,128)S(1)} %copy-done.2), custom_call_target="tpu_custom_call" | custom-call | tf_op jit(solution)/shard_map/polar/pallas_call | solution.py:77
  13.8 2.3 %slice.23 = f32[6,2,128,128]{3,2,1,0:T(8,128)} slice(f32[16,2,128,128]{3,2,1,0:T(8,128)} %start_ref.1), slice={[0:6], [0:2], [0:128], [0:128]} | slice | bytes 1572864 | tf_op jit(solution)/shard_map/slice | solution.py:327
  16.1 4.6 %collective-permute-start.3 = (f32[6,2,128,128]{3,2,1,0:T(8,128)}, f32[6,2,128,128]{3,2,1,0:T(8,128)S(1)}, u32[]{:S(2)}, u32[]{:S(2)}) collective-permute-start(f32[6,2,128,128]{3,2,1,0:T(8,128)} %slice.23), channel_id=1, source_target_pairs={{0,12},{2,14},{4,0},{6,2},{8,4},{10,6},{12,8},{14,10},{1,13},{3,15... | collective-permute-start | bytes 2359304 | tf_op jit(solution)/shard_map/ppermute | solution.py:300
  20.7 2.3 %fusion.4 = (f32[4,2,128,128]{3,2,1,0:T(8,128)}, f32[4,2,128,128]{3,2,1,0:T(8,128)}) fusion(f32[16,2,128,128]{3,2,1,0:T(8,128)} %polar.1.rotation_ref.own_ref), kind=kLoop, calls=%fused_computation.19 | loop fusion | bytes 2097152 | tf_op jit(solution)/shard_map/slice | solution.py:333
  23.9 0.8 slice.25
  24.8 5.9 %sandwich.1.sandwich_ref.refs_0_.refs_1_ = f32[2,16,128,256]{3,2,1,0:T(8,128)} custom-call(f32[16,2,128,128]{3,2,1,0:T(8,128)S(1)} %copy-done, f32[16,2,2,128,128]{4,3,2,1,0:T(8,128)} %correlation_ref.1), custom_call_target="tpu_custom_call" | custom-call | tf_op jit(solution)/shard_map/sandwich/pallas_call | solution.py:98
  30.6 1.6 %copy-done.1 = f32[16,2,128,128]{3,2,1,0:T(8,128)S(1)} copy-done((f32[16,2,128,128]{3,2,1,0:T(8,128)S(1)}, f32[16,2,128,128]{3,2,1,0:T(8,128)}, u32[]{:S(2)}) %copy-start.1) | copy-done | bytes 2097176
  32.2 4.8 %slab.1 = (f32[16,128,256]{2,1,0:T(8,128)S(1)}, f32[16,8,128]{2,1,0:T(8,128)S(1)}, f32[8,128]{1,0:T(8,128)S(1)}) custom-call(s32[16]{0:T(128)S(1)} %get-tuple-element.39.slots_ref, f32[2,16,128,256]{3,2,1,0:T(8,128)} %sandwich.1.sandwich_ref.refs_0_.refs_1_, f32[16,2,128,128]{3,2,1,0:T(8,128)S(1)} %copy-done.1, ...), custom_call_target="tpu_custom_call" | custom-call | tf_op jit(solution)/shard_map/slab/pallas_call | solution.py:153
  37.0 1.8 %collective-permute-done.3.refs_2_ = f32[6,2,128,128]{3,2,1,0:T(8,128)S(1)} collective-permute-done((f32[6,2,128,128]{3,2,1,0:T(8,128)}, f32[6,2,128,128]{3,2,1,0:T(8,128)S(1)}, u32[]{:S(2)}, u32[]{:S(2)}) %collective-permute-start.3) | collective-permute-done | bytes 786464 | tf_op jit(solution)/shard_map/ppermute | solution.py:300
  38.9 8.4 %plane.4 = (f32[16,128,256]{2,1,0:T(8,128)S(1)}, f32[16,8,128]{2,1,0:T(8,128)S(1)}, f32[8,128]{1,0:T(8,128)S(1)}) custom-call(s32[16]{0:T(128)S(1)} %select_reduce_fusion.order_ref, f32[2,16,128,256]{3,2,1,0:T(8,128)} %sandwich.1.sandwich_ref.refs_0_.refs_1_, f32[2,16,128,256]{3,2,1,0:T(8,128)} %sandwich.1.sandwich_ref.refs_0_.refs_1_, ...), custom_call_target="tpu_custom_call" | custom-call | tf_op jit(solution)/shard_map/plane/pallas_call | solution.py:214
  47.3 2.8 %collective-permute-done.2.refs_2_ = f32[4,2,128,128]{3,2,1,0:T(8,128)} collective-permute-done((f32[4,2,128,128]{3,2,1,0:T(8,128)}, f32[4,2,128,128]{3,2,1,0:T(8,128)}, u32[]{:S(2)}, u32[]{:S(2)}) %collective-permute-start.2) | collective-permute-done | bytes 524320 | tf_op jit(solution)/shard_map/ppermute | solution.py:300
  50.1 2.4 %plane.5 = (f32[16,128,256]{2,1,0:T(8,128)S(1)}, f32[16,8,128]{2,1,0:T(8,128)S(1)}, f32[8,128]{1,0:T(8,128)S(1)}) custom-call(s32[16]{0:T(128)S(1)} %select_reduce_fusion.order_ref, f32[2,16,128,256]{3,2,1,0:T(8,128)} %sandwich.1.sandwich_ref.refs_0_.refs_1_, ...), custom_call_target="tpu_custom_call", output_to_operand_aliasing={{0}: (5, {}), {1}: (6, {})} | custom-call | tf_op jit(solution)/shard_map/plane/pallas_call | solution.py:214
  52.5 8.8 %collective-permute-done.1.refs_2_ = f32[4,2,128,128]{3,2,1,0:T(8,128)S(1)} collective-permute-done((f32[4,2,128,128]{3,2,1,0:T(8,128)}, f32[4,2,128,128]{3,2,1,0:T(8,128)S(1)}, u32[]{:S(2)}, u32[]{:S(2)}) %collective-permute-start.1) | collective-permute-done | bytes 524320 | tf_op jit(solution)/shard_map/ppermute | solution.py:300
  61.3 2.2 %plane.6 = (f32[16,128,256]{2,1,0:T(8,128)S(1)}, f32[16,8,128]{2,1,0:T(8,128)S(1)}, f32[8,128]{1,0:T(8,128)S(1)}) custom-call(s32[16]{0:T(128)S(1)} %select_reduce_fusion.order_ref, f32[2,16,128,256]{3,2,1,0:T(8,128)} %sandwich.1.sandwich_ref.refs_0_.refs_1_, ...), custom_call_target="tpu_custom_call", output_to_operand_aliasing={{0}: (5, {}), {1}: (6, {})} | custom-call | tf_op jit(solution)/shard_map/plane/pallas_call | solution.py:214
  63.6 2.8 %collective-permute-done.refs_2_ = f32[2,2,128,128]{3,2,1,0:T(8,128)} collective-permute-done((f32[2,2,128,128]{3,2,1,0:T(8,128)}, f32[2,2,128,128]{3,2,1,0:T(8,128)}, u32[]{:S(2)}, u32[]{:S(2)}) %collective-permute-start) | collective-permute-done | bytes 262176 | tf_op jit(solution)/shard_map/ppermute | solution.py:300
  66.4 2.0 %plane.7 = (f32[16,128,256]{2,1,0:T(8,128)S(1)}, f32[16,8,128]{2,1,0:T(8,128)S(1)}, f32[8,128]{1,0:T(8,128)S(1)}) custom-call(s32[16]{0:T(128)S(1)} %select_reduce_fusion.order_ref, f32[2,16,128,256]{3,2,1,0:T(8,128)} %sandwich.1.sandwich_ref.refs_0_.refs_1_, ...), custom_call_target="tpu_custom_call", output_to_operand_aliasing={{0}: (5, {}), {1}: (6, {})} | custom-call | tf_op jit(solution)/shard_map/plane/pallas_call | solution.py:214
  68.4 1.2 %collective-permute-done.5 = f32[8,128]{1,0:T(8,128)S(1)} collective-permute-done((f32[8,128]{1,0:T(8,128)S(1)}, f32[8,128]{1,0:T(8,128)S(1)}, u32[]{:S(2)}, u32[]{:S(2)}) %collective-permute-start.5) | collective-permute-done | bytes 4128 | tf_op jit(solution)/shard_map/ppermute | solution.py:300
  69.6 1.5 %collective-permute-start.6 = (f32[8,128]{1,0:T(8,128)S(1)}, f32[8,128]{1,0:T(8,128)S(1)}, u32[]{:S(2)}, u32[]{:S(2)}) collective-permute-start(f32[8,128]{1,0:T(8,128)S(1)} %add.34), channel_id=1, source_target_pairs={{0,2},{2,0},{4,6},{6,4},{8,10},{10,8},{12,14},{14,12},{1,3},{3,1},... | collective-permute-start | bytes 12296 | tf_op jit(solution)/shard_map/ppermute | solution.py:310
  71.1 2.1 %collective-permute-done.6 = f32[8,128]{1,0:T(8,128)S(1)} collective-permute-done((f32[8,128]{1,0:T(8,128)S(1)}, f32[8,128]{1,0:T(8,128)S(1)}, u32[]{:S(2)}, u32[]{:S(2)}) %collective-permute-start.6) | collective-permute-done | bytes 4128 | tf_op jit(solution)/shard_map/ppermute | solution.py:310
  73.6 3.1 %collective-permute-done.7 = f32[8,128]{1,0:T(8,128)S(1)} collective-permute-done((f32[8,128]{1,0:T(8,128)S(1)}, f32[8,128]{1,0:T(8,128)S(1)}, u32[]{:S(2)}, u32[]{:S(2)}) %collective-permute-start.7) | collective-permute-done | bytes 4128 | tf_op jit(solution)/shard_map/ppermute | solution.py:310
  76.8 2.8 %collective-permute-start.8 = (f32[8,128]{1,0:T(8,128)S(1)}, f32[8,128]{1,0:T(8,128)S(1)}, u32[]{:S(2)}, u32[]{:S(2)}) collective-permute-start(f32[8,128]{1,0:T(8,128)S(1)} %add.36.refs_0_), channel_id=1, source_target_pairs={{0,8},{2,10},{4,12},{6,14},{8,0},{10,2},{12,4},{14,6},{1,9},{3,11}... | collective-permute-start | bytes 12296 | tf_op jit(solution)/shard_map/ppermute | solution.py:310
  79.6 1.7 %collective-permute-done.8.refs_1_ = f32[8,128]{1,0:T(8,128)S(1)} collective-permute-done((f32[8,128]{1,0:T(8,128)S(1)}, f32[8,128]{1,0:T(8,128)S(1)}, u32[]{:S(2)}, u32[]{:S(2)}) %collective-permute-start.8) | collective-permute-done | bytes 4128 | tf_op jit(solution)/shard_map/ppermute | solution.py:310
  81.3 2.9 %gradient.1 = (f32[16,2,128,128]{3,2,1,0:T(8,128)}, f32[2,128]{1,0:T(2,128)}) custom-call(s32[16]{0:T(128)S(1)} %get-tuple-element.40.slots_ref, f32[8,128]{1,0:T(8,128)S(1)} %add.36.refs_0_, f32[8,128]{1,0:T(8,128)S(1)} %collective-permute-done.8.refs_1_, f32[16,128,256]{2,1,0:T(8,128)S(1)} %get-tuple-element.31.refs_2_.refs_3_.refs_4_.refs_5_, ...), custom_call_target="tpu_custom_call" | custom-call | tf_op jit(solution)/shard_map/gradient/pallas_call | solution.py:273
  (19 shorter events, 2.1 us)
Async XLA Ops:
  0.6 1.6 %copy-start.2 = (f32[16,2,128,128]{3,2,1,0:T(8,128)S(1)}, f32[16,2,128,128]{3,2,1,0:T(8,128)}, u32[]{:S(2)}) copy-start(f32[16,2,128,128]{3,2,1,0:T(8,128)} %start_ref.1) | copy-start | bytes 6291460
  13.4 10.5 %copy-start = (f32[16,2,128,128]{3,2,1,0:T(8,128)S(1)}, f32[16,2,128,128]{3,2,1,0:T(8,128)}, u32[]{:S(2)}) copy-start(f32[16,2,128,128]{3,2,1,0:T(8,128)} %polar.1.rotation_ref.own_ref) | copy-start | bytes 6291460
  13.4 11.3 %copy-start.3 = (s32[16,2]{0,1:T(2,128)S(1)}, s32[16,2]{0,1:T(2,128)}, u32[]{:S(2)}) copy-start(s32[16,2]{0,1:T(2,128)} %param.5) | copy-start | bytes 388
  13.4 17.2 %collective-permute-start.4 = (f32[16,2,128,128]{3,2,1,0:T(8,128)}, f32[16,2,128,128]{3,2,1,0:T(8,128)}, u32[]{:S(2)}, u32[]{:S(2)}) collective-permute-start(f32[16,2,128,128]{3,2,1,0:T(8,128)} %polar.1.rotation_ref.own_ref), channel_id=1, source_target_pairs={{0,1},{1,0},{2,3},{3,2},{4,5},{5,4},{6,7},{7,6},{8,9},{9,8},{10,11... | collective-permute-start | bytes 6291464 | tf_op jit(solution)/shard_map/ppermute | solution.py:300
  16.1 22.8 %collective-permute-start.3 = (f32[6,2,128,128]{3,2,1,0:T(8,128)}, f32[6,2,128,128]{3,2,1,0:T(8,128)S(1)}, u32[]{:S(2)}, u32[]{:S(2)}) collective-permute-start(f32[6,2,128,128]{3,2,1,0:T(8,128)} %slice.23), channel_id=1, source_target_pairs={{0,12},{2,14},{4,0},{6,2},{8,4},{10,6},{12,8},{14,10},{1,13},{3,15... | collective-permute-start | bytes 2359304 | tf_op jit(solution)/shard_map/ppermute | solution.py:300
  23.0 27.1 %collective-permute-start.2 = (f32[4,2,128,128]{3,2,1,0:T(8,128)}, f32[4,2,128,128]{3,2,1,0:T(8,128)}, u32[]{:S(2)}, u32[]{:S(2)}) collective-permute-start(f32[4,2,128,128]{3,2,1,0:T(8,128)} %get-tuple-element.37), channel_id=1, source_target_pairs={{0,12},{2,14},{4,0},{6,2},{8,4},{10,6},{12,8},{14,10},{1,13},{3,15... | collective-permute-start | bytes 1572872 | tf_op jit(solution)/shard_map/ppermute | solution.py:300
  23.4 37.9 %collective-permute-start.1 = (f32[4,2,128,128]{3,2,1,0:T(8,128)}, f32[4,2,128,128]{3,2,1,0:T(8,128)S(1)}, u32[]{:S(2)}, u32[]{:S(2)}) collective-permute-start(f32[4,2,128,128]{3,2,1,0:T(8,128)} %get-tuple-element.38), channel_id=1, source_target_pairs={{0,12},{2,14},{4,0},{6,2},{8,4},{10,6},{12,8},{14,10},{1,13},{3,15... | collective-permute-start | bytes 1572872 | tf_op jit(solution)/shard_map/ppermute | solution.py:300
  24.6 41.8 %collective-permute-start = (f32[2,2,128,128]{3,2,1,0:T(8,128)}, f32[2,2,128,128]{3,2,1,0:T(8,128)}, u32[]{:S(2)}, u32[]{:S(2)}) collective-permute-start(f32[2,2,128,128]{3,2,1,0:T(8,128)} %slice.25), channel_id=1, source_target_pairs={{0,12},{2,14},{4,0},{6,2},{8,4},{10,6},{12,8},{14,10},{1,13},{3,15... | collective-permute-start | bytes 786440 | tf_op jit(solution)/shard_map/ppermute | solution.py:300
  30.6 1.6 %copy-start.1 = (f32[16,2,128,128]{3,2,1,0:T(8,128)S(1)}, f32[16,2,128,128]{3,2,1,0:T(8,128)}, u32[]{:S(2)}) copy-start(f32[16,2,128,128]{3,2,1,0:T(8,128)} %polar.1.rotation_ref.own_ref) | copy-start | bytes 6291460
  68.3 1.2 %collective-permute-start.5 = (f32[8,128]{1,0:T(8,128)S(1)}, f32[8,128]{1,0:T(8,128)S(1)}, u32[]{:S(2)}, u32[]{:S(2)}) collective-permute-start(f32[8,128]{1,0:T(8,128)S(1)} %get-tuple-element.30), channel_id=1, source_target_pairs={{0,1},{1,0},{2,3},{3,2},{4,5},{5,4},{6,7},{7,6},{8,9},{9,8},{10,11... | collective-permute-start | bytes 12296 | tf_op jit(solution)/shard_map/ppermute | solution.py:300
  69.6 3.6 %collective-permute-start.6 = (f32[8,128]{1,0:T(8,128)S(1)}, f32[8,128]{1,0:T(8,128)S(1)}, u32[]{:S(2)}, u32[]{:S(2)}) collective-permute-start(f32[8,128]{1,0:T(8,128)S(1)} %add.34), channel_id=1, source_target_pairs={{0,2},{2,0},{4,6},{6,4},{8,10},{10,8},{12,14},{14,12},{1,3},{3,1},... | collective-permute-start | bytes 12296 | tf_op jit(solution)/shard_map/ppermute | solution.py:310
  73.2 3.6 %collective-permute-start.7 = (f32[8,128]{1,0:T(8,128)S(1)}, f32[8,128]{1,0:T(8,128)S(1)}, u32[]{:S(2)}, u32[]{:S(2)}) collective-permute-start(f32[8,128]{1,0:T(8,128)S(1)} %add.35), channel_id=1, source_target_pairs={{0,4},{2,6},{4,0},{6,2},{8,12},{10,14},{12,8},{14,10},{1,5},{3,7},... | collective-permute-start | bytes 12296 | tf_op jit(solution)/shard_map/ppermute | solution.py:310
  76.8 4.5 %collective-permute-start.8 = (f32[8,128]{1,0:T(8,128)S(1)}, f32[8,128]{1,0:T(8,128)S(1)}, u32[]{:S(2)}, u32[]{:S(2)}) collective-permute-start(f32[8,128]{1,0:T(8,128)S(1)} %add.36.refs_0_), channel_id=1, source_target_pairs={{0,8},{2,10},{4,12},{6,14},{8,0},{10,2},{12,4},{14,6},{1,9},{3,11}... | collective-permute-start | bytes 12296 | tf_op jit(solution)/shard_map/ppermute | solution.py:310
where the time goes:
time: 84.6 us; the launch traced here: 84.2 us
  Pallas kernels  39.7 us (47%)
  waiting for transfers between devices  24.4 us (29%)
  starting transfers between devices  10.8 us (13%)
  local copies, waits for them, and re-layouts  8.47 us (10%)
    ppermute x6, waiting for transfers between devices, shifted(): lax.ppermute(value, axis, [(source, (source + steps) % count) for source...  17.5 us
    pallas_call x4, Pallas kernels, plane_call(): pl.pallas_call(functools.partial(plane_kernel, step=step, raw=raw, earlie...  15 us
    pallas_call x1, Pallas kernels, polar_call(): pl.pallas_call(polar_kernel, grid=(start.shape[0] // step,), in_specs=[bl...  11.2 us
    ppermute x3, waiting for transfers between devices, reduce_parts(): lax.ppermute(value, 'kxy', [(source, source ^ distance) for source in ran...  6.94 us
    ppermute x6, starting transfers between devices, shifted(): lax.ppermute(value, axis, [(source, (source + steps) % count) for source...  6.03 us
    pallas_call x1, Pallas kernels, sandwich_call(): pl.pallas_call(sandwich_kernel, grid=(count // step,), in_specs=[pl.Block...  5.86 us
    pallas_call x1, Pallas kernels, slab_call(): pl.pallas_call(slab_kernel, grid_spec=pltpu.PrefetchScalarGridSpec(num_sc...  4.81 us
    ppermute x3, starting transfers between devices, reduce_parts(): lax.ppermute(value, 'kxy', [(source, source ^ distance) for source in ran...  4.78 us
  transfers between devices with their start and end apart: 9, of which 8 were waited for; matrix products, arithmetic and copies ran while one was open for 6% of the time, Pallas kernels for 28%

commit v1 on v0

v1 whole, which is shorter than its diff:
```python
import functools

import jax
import jax.numpy as jnp
from jax import lax
from jax.experimental import pallas as pl
from jax.experimental.pallas import tpu as pltpu
from jax.sharding import PartitionSpec as P

NS_STEPS = 3
RAW = (8,)
CHUNKS = (6, 2)
GROUP = 4
VMEM = 32 << 20


def dot(left, right, contract):
    return lax.dot_general(left, right, ((contract), ((), ())), preferred_element_type=jnp.float32)


def split(value):
    high = value.astype(jnp.bfloat16)
    return high, (value - high.astype(jnp.float32)).astype(jnp.bfloat16)


def product(left, right, contract=((1,), (0,))):
    return dot(left[0], right[0], contract) + (
        dot(left[0], right[1], contract) + dot(left[1], right[0], contract)
    )


def both(function, pair):
    return tuple(function(half) for half in pair)


def right_form(half):
    n = half.shape[0]
    return jnp.concatenate([half, jnp.concatenate([-half[:, n:], half[:, :n]], 1)], 0)


def adjoint_right_form(half):
    n = half.shape[0]
    return jnp.concatenate([half, jnp.concatenate([half[:, n:], -half[:, :n]], 1)], 0)


def identity(n):
    rows = lax.broadcasted_iota(jnp.int32, (n, n), 0)
    return (rows == lax.broadcasted_iota(jnp.int32, (n, n), 1)).astype(jnp.float32)


def polar(pairs):
    n = pairs[0][0].shape[0]
    unit = identity(n)
    unit = jnp.concatenate([1.5 * unit, jnp.zeros_like(unit)], 1)
    current = []
    for real, imag in pairs:
        scale = 1.0 / jnp.sqrt(jnp.sum(real * real + imag * imag) / n + 1e-06)
        current.append(jnp.concatenate([real * scale, imag * scale], 1))
    for _ in range(NS_STEPS):
        left = [split(value) for value in current]
        right = [both(right_form, pair) for pair in left]
        gram = [product(a, b, ((1,), (1,))) for a, b in zip(left, right)]
        factor = [split(unit - 0.5 * value) for value in gram]
        current = [product(a, b) for a, b in zip(factor, right)]
    return current


def polar_kernel(start_ref, *refs, carried, chunks):
    out_refs, chunk_refs = refs[carried : carried + 2], refs[carried + 2 :]
    n = start_ref.shape[-1]
    step = start_ref.shape[0]
    values = polar([(start_ref[i, 0], start_ref[i, 1]) for i in range(step)])

    def store(ref, i, value):
        ref[i, 0] = value[:, :n]
        ref[i, 1] = value[:, n:]

    for i, value in enumerate(values):
        for out_ref in out_refs:
            store(out_ref, i, value)
    slot = 0
    for chunk_ref, size in zip(chunk_refs, chunks):
        for i in range(size):
            pl.when(pl.program_id(0) == slot // step)(
                functools.partial(store, chunk_ref, i, values[slot % step])
            )
            slot += 1


def polar_call(start, first, count, step, carried, chunks):
    shape = start.shape[1:]
    base = first // step
    block = pl.BlockSpec((step,) + shape, lambda g: (base + g, 0, 0, 0))
    return pl.pallas_call(
        functools.partial(polar_kernel, carried=len(carried), chunks=chunks),
        grid=(count // step,),
        in_specs=[block] + [pl.BlockSpec(memory_space=pl.ANY)] * len(carried),
        out_specs=[block, pl.BlockSpec((step,) + shape, lambda g: (g, 0, 0, 0))]
        + [pl.BlockSpec((size,) + shape, lambda g: (0, 0, 0, 0)) for size in chunks],
        out_shape=[jax.ShapeDtypeStruct((size,) + shape, start.dtype) for size in (start.shape[0], count, *chunks)],
        input_output_aliases={1: 0} if carried else {},
        compiler_params=pltpu.CompilerParams(vmem_limit_bytes=VMEM),
        name="polar",
    )(start, *carried)


def take_kernel(start_ref, *refs):
    *out_refs, sems = refs
    copies = []
    first = 0
    for i, out_ref in enumerate(out_refs):
        size = out_ref.shape[0]
        copies.append(pltpu.make_async_copy(start_ref.at[pl.ds(first, size)], out_ref, sems.at[i]))
        copies[-1].start()
        first += size
    for copy in copies:
        copy.wait()


def take_call(start, sizes):
    anywhere = pl.BlockSpec(memory_space=pl.ANY)
    return pl.pallas_call(
        take_kernel,
        in_specs=[anywhere],
        out_specs=[anywhere] * len(sizes),
        out_shape=[jax.ShapeDtypeStruct((size,) + start.shape[1:], start.dtype) for size in sizes],
        scratch_shapes=[pltpu.SemaphoreType.DMA((len(sizes),))],
        name="take",
    )(start)


def sandwich_kernel(rotation_ref, correlation_ref, *out_refs):
    for i in range(rotation_ref.shape[0]):
        left = split(jnp.concatenate([rotation_ref[i, 0].T, rotation_ref[i, 1].T], 1))
        for d in range(2):
            right = split(jnp.concatenate([correlation_ref[i, d, 0], correlation_ref[i, d, 1]], 1))
            out_refs[d][i] = product(left, both(adjoint_right_form, right))


def sandwich_call(rotation, correlations, step):
    count, _, n, _ = rotation.shape
    return pl.pallas_call(
        sandwich_kernel,
        grid=(count // step,),
        in_specs=[
            pl.BlockSpec((step, 2, n, n), lambda g: (g, 0, 0, 0)),
            pl.BlockSpec((step, 2, 2, n, n), lambda g: (g, 0, 0, 0, 0)),
        ],
        out_specs=[pl.BlockSpec((step, n, 2 * n), lambda g: (g, 0, 0))] * 2,
        out_shape=[jax.ShapeDtypeStruct((count, n, 2 * n), jnp.float32)] * 2,
        compiler_params=pltpu.CompilerParams(vmem_limit_bytes=VMEM),
        name="sandwich",
    )(rotation, correlations)


def column_terms(rotated, rows_ref, i):
    n = rotated.shape[0]
    unit = identity(n)
    real = jnp.sum(rotated[:, :n] * unit, axis=0, keepdims=True)
    imag = jnp.sum(rotated[:, n:] * unit, axis=0, keepdims=True)
    phase = jnp.arctan2(imag, real)
    modulus = real * real + imag * imag
    weight_real = imag / modulus
    weight_imag = real / modulus
    rows_ref[i, 0:1] = real + phase * weight_real
    rows_ref[i, 1:2] = phase * weight_imag - imag
    rows_ref[i, 2:3] = weight_real
    rows_ref[i, 3:4] = weight_imag
    return phase


def slab_kernel(slots_ref, before_ref, sandwich_ref, own_ref, *refs, pieces):
    piece_refs, (out_ref, rows_ref, total_ref, received_ref) = refs[:pieces], refs[pieces:]
    count, _, n, _ = own_ref.shape
    first = 0
    for piece_ref in piece_refs:
        received_ref[first : first + piece_ref.shape[0]] = piece_ref[...]
        first += piece_ref.shape[0]

    def group(g, total):
        rotated = []
        for i in range(GROUP):
            slot = slots_ref[g * GROUP + i]
            local = slot % count
            remote = slot >= count
            partner = [jnp.where(remote, received_ref[local, p], own_ref[local, p]) for p in range(2)]
            right = both(right_form, split(jnp.concatenate(partner, 1)))
            rotated.append(product(split(sandwich_ref[g * GROUP + i]), right))
        for i, matrix in enumerate(rotated):
            out_ref[g * GROUP + i] = matrix
            total = total + column_terms(matrix, rows_ref, g * GROUP + i)
        return total

    total_ref[...] = before_ref[...]
    total_ref[1:2] = lax.fori_loop(0, count // GROUP, group, jnp.zeros((1, n), jnp.float32))


def slab_call(slots, total, sandwich, own, pieces):
    count, n, _ = sandwich.shape
    whole = pl.BlockSpec(memory_space=pltpu.VMEM)
    return pl.pallas_call(
        functools.partial(slab_kernel, pieces=len(pieces)),
        in_specs=[pl.BlockSpec(memory_space=pltpu.SMEM)] + [whole] * (3 + len(pieces)),
        out_specs=[whole] * 3,
        out_shape=[
            jax.ShapeDtypeStruct((count, n, 2 * n), jnp.float32),
            jax.ShapeDtypeStruct((count, 8, n), jnp.float32),
            jax.ShapeDtypeStruct((8, n), jnp.float32),
        ],
        scratch_shapes=[pltpu.VMEM(own.shape, own.dtype)],
        compiler_params=pltpu.CompilerParams(vmem_limit_bytes=VMEM),
        name="slab",
    )(slots, total, sandwich, own, *pieces)


def plane_kernel(order_ref, sandwich_ref, partner_ref, *refs, first, raw, earlier, carried):
    total_refs, refs = refs[:earlier], refs[earlier:]
    out_ref, rows_ref, total_ref = refs[2 * carried :]
    count = partner_ref.shape[0]
    total = total_refs[0][...] if earlier else jnp.zeros_like(total_ref)
    for other in total_refs[1:]:
        total = total + other[...]
    phases = jnp.zeros((1, partner_ref.shape[-1]), jnp.float32)
    for begin in range(0, count, GROUP):
        group = range(begin, min(begin + GROUP, count))
        pairs = [(partner_ref[i, 0], partner_ref[i, 1]) for i in group]
        partners = polar(pairs) if raw else [jnp.concatenate(pair, 1) for pair in pairs]
        rotated = [
            product(split(sandwich_ref[order_ref[first + i]]), both(right_form, split(partner)))
            for i, partner in zip(group, partners)
        ]
        for i, matrix in zip(group, rotated):
            out_ref[first + i] = matrix
            phases = phases + column_terms(matrix, rows_ref, first + i)
    total_ref[...] = total
    total_ref[0:1] = total[0:1] + phases


def plane_call(order, sandwich, partner, first, earlier, carried, raw):
    count, n, _ = sandwich.shape
    whole = pl.BlockSpec(memory_space=pltpu.VMEM)
    position = 3 + len(earlier)
    return pl.pallas_call(
        functools.partial(plane_kernel, first=first, raw=raw, earlier=len(earlier), carried=bool(carried)),
        in_specs=[pl.BlockSpec(memory_space=pltpu.SMEM)] + [whole] * (2 + len(earlier) + len(carried)),
        out_specs=[whole] * 3,
        out_shape=[
            jax.ShapeDtypeStruct((count, n, 2 * n), jnp.float32),
            jax.ShapeDtypeStruct((count, 8, n), jnp.float32),
            jax.ShapeDtypeStruct((8, n), jnp.float32),
        ],
        input_output_aliases={position: 0, position + 1: 1} if carried else {},
        compiler_params=pltpu.CompilerParams(vmem_limit_bytes=VMEM),
        name="plane",
    )(order, sandwich, partner, *earlier, *carried)


def gradient_kernel(
    slots_ref, first_ref, second_ref, plane_ref, plane_rows, slab_ref, slab_rows, out_ref, centres_ref, buffer, sems, *, everything
):
    count, n, _ = slab_ref.shape
    centres = (first_ref[0:2] + second_ref[0:2]) / (-2.0 * everything)
    centres_ref[...] = centres
    copies = []
    for i in range(count):
        real = imag = None
        for d, (j, matrix, rows) in enumerate(
            ((slots_ref[i], plane_ref, plane_rows), (i, slab_ref, slab_rows))
        ):
            centre = centres[d : d + 1]
            v_real = 2.0 * (rows[j, 0:1] + centre * rows[j, 2:3])
            v_imag = 2.0 * (rows[j, 1:2] + centre * rows[j, 3:4])
            m_real = matrix[j, :, :n]
            m_imag = matrix[j, :, n:]
            y_real = m_real * v_real - m_imag * v_imag
            y_imag = m_real * v_imag + m_imag * v_real
            real = y_real if d == 0 else real + y_real
            imag = y_imag if d == 0 else imag + y_imag
        buffer[i, 0] = real - real.T
        buffer[i, 1] = imag + imag.T
        copies.append(pltpu.make_async_copy(buffer.at[i], out_ref.at[i], sems.at[i]))
        copies[-1].start()
    for copy in copies:
        copy.wait()


def gradient_call(slots, totals, plane, plane_rows, slab, slab_rows, everything):
    count, n, _ = slab.shape
    whole = pl.BlockSpec(memory_space=pltpu.VMEM)
    return pl.pallas_call(
        functools.partial(gradient_kernel, everything=everything),
        in_specs=[pl.BlockSpec(memory_space=pltpu.SMEM)] + [whole] * 6,
        out_specs=[pl.BlockSpec(memory_space=pl.ANY), whole],
        out_shape=[
            jax.ShapeDtypeStruct((count, 2, n, n), jnp.float32),
            jax.ShapeDtypeStruct((2, n), jnp.float32),
        ],
        scratch_shapes=[pltpu.VMEM((count, 2, n, n), jnp.float32), pltpu.SemaphoreType.DMA((count,))],
        compiler_params=pltpu.CompilerParams(vmem_limit_bytes=VMEM),
        name="gradient",
    )(slots, *totals, plane, plane_rows, slab, slab_rows)


def shifted(value, axis, steps):
    count = lax.axis_size(axis)
    return lax.ppermute(value, axis, [(source, (source + steps) % count) for source in range(count)])


def reduce_parts(value):
    count = lax.axis_size("kxy")
    if lax.axis_size("kz") != 2 or count & (count - 1) or count < 2:
        return lax.psum(value, ("kxy", "kz")), jnp.zeros_like(value)
    value = value + shifted(value, "kz", 1)
    distance = 1
    while True:
        other = lax.ppermute(value, "kxy", [(source, source ^ distance) for source in range(count)])
        distance *= 2
        if distance == count:
            return value, other
        value = value + other


def body(start_rotation, correlations, neighbours):
    count = start_rotation.shape[0]
    block_index = lax.axis_index("kxy") * lax.axis_size("kz") + lax.axis_index("kz")
    everything = count * lax.axis_size("kxy") * lax.axis_size("kz")
    plane_slots = neighbours[:, 0] % count
    positions = jnp.arange(count, dtype=jnp.int32)
    order = jnp.max(jnp.where(plane_slots[:, None] == positions[None], positions[:, None], 0), axis=0)
    remote = (neighbours[:, 1] // count != block_index).astype(jnp.int32)
    slab_slots = neighbours[:, 1] % count + count * remote

    received = []
    first = 0
    for part in take_call(start_rotation, RAW):
        received.append((first, True, shifted(part, "kxy", -2)))
        first += part.shape[0]
    rotation, late, *parts = polar_call(start_rotation, first, count - first, GROUP, [], CHUNKS)
    for part in parts:
        received.append((first, False, shifted(part, "kxy", -2)))
        first += part.shape[0]
    rotation, early = polar_call(start_rotation, 0, sum(RAW), GROUP, [rotation], ())
    from_slab = [shifted(part, "kz", -1) for part in (early, late)]
    for_plane, for_slab = sandwich_call(rotation, correlations, 4)
    total, carried = None, []
    for first, raw, partner in received:
        earlier = [] if total is None else [total]
        plane, plane_rows, total = plane_call(order, for_plane, partner, first, earlier, carried, raw)
        if not carried:
            slab, slab_rows, total = slab_call(slab_slots, total, for_slab, rotation, from_slab)
        carried = [plane, plane_rows]
    gradient, centres = gradient_call(
        plane_slots, reduce_parts(total), plane, plane_rows, slab, slab_rows, everything
    )
    return (rotation, gradient, centres)


def solution(mesh):
    in_specs = (
        P(("grp", "kxy", "kz"), None, None, None),
        P(("grp", "kxy", "kz"), None, None, None, None),
        P(("grp", "kxy", "kz"), None),
    )
    out_specs = (
        P(("grp", "kxy", "kz"), None, None, None),
        P(("grp", "kxy", "kz"), None, None, None),
        P("grp", None),
    )
    return jax.shard_map(body, mesh=mesh, in_specs=in_specs, out_specs=out_specs, check_vma=False)
```

time: 84.6 us -> 101 us (1.19)
  Pallas kernels: 39.7 us -> 61.7 us
  local copies, waits for them, and re-layouts: 8.47 us -> 3.78 us
  waiting for transfers between devices: 24.4 us -> 22.8 us
    pallas_call x7 -> x8, Pallas kernels: 33.8 us -> 59.2 us  [the longest x1 32.9 us: take_call(): pl.pallas_call(take_kernel, in_specs=[anywhere], out_specs=[anywhere] * l...]
    slice x3 -> x0, local copies, waits for them, and re-layouts: 5.29 us -> none  [the longest x2 3.04 us: body(): received.append(shifted(rotation[first:first + size], 'kxy', -2))]
    pallas_call x1, Pallas kernels: 5.86 us -> 2.53 us  [sandwich_call(): pl.pallas_call(sandwich_kernel, grid=(count // step,), in_specs=[pl.Block...]
    ppermute x6, waiting for transfers between devices: 17.5 us -> 15.6 us  [shifted(): lax.ppermute(value, axis, [(source, (source + steps) % count) for source...]
  transfers between devices with their start and end apart: 9 -> 9, of which waited for: 8 -> 7; matrix products, arithmetic and copies ran while one was open for 6% -> 0% of each run, Pallas kernels for 28% -> 25%
where the time goes in v1:
time: 101 us; the launch traced here: 100 us
  Pallas kernels  61.7 us (61%)
  waiting for transfers between devices  22.8 us (23%)
  starting transfers between devices  11.1 us (11%)
  local copies, waits for them, and re-layouts  3.78 us (4%)
    pallas_call x1, Pallas kernels, take_call(): pl.pallas_call(take_kernel, in_specs=[anywhere], out_specs=[anywhere] * l...  32.9 us
    ppermute x6, waiting for transfers between devices, shifted(): lax.ppermute(value, axis, [(source, (source + steps) % count) for source...  15.6 us
    pallas_call x2, Pallas kernels, polar_call(): pl.pallas_call(functools.partial(polar_kernel, carried=len(carried), chun...  12.8 us
    pallas_call x3, Pallas kernels, plane_call(): pl.pallas_call(functools.partial(plane_kernel, first=first, raw=raw, earl...  8.39 us
    ppermute x3, waiting for transfers between devices, reduce_parts(): lax.ppermute(value, 'kxy', [(source, source ^ distance) for source in ran...  7.16 us
    ppermute x6, starting transfers between devices, shifted(): lax.ppermute(value, axis, [(source, (source + steps) % count) for source...  6.58 us
    ppermute x3, starting transfers between devices, reduce_parts(): lax.ppermute(value, 'kxy', [(source, source ^ distance) for source in ran...  4.56 us
    unnamed x8, local copies, waits for them, and re-layouts  3.78 us
  transfers between devices with their start and end apart: 9, of which 7 were waited for; matrix products, arithmetic and copies ran while one was open for 0% of the time, Pallas kernels for 25%

profile of v1, /device:TPU:0, one launch (start us, length us, event | category | flops | bytes accessed | tf_op | source)
XLA Modules:
  0.0 100.3 jit_solution(4960074326313987934)
XLA Ops:
  0.6 32.9 %take.1 = f32[8,2,128,128]{3,2,1,0:T(8,128)} custom-call(f32[16,2,128,128]{3,2,1,0:T(8,128)} %start_ref.5), custom_call_target="tpu_custom_call" | custom-call | tf_op jit(solution)/shard_map/take/pallas_call | solution.py:122
  33.5 5.1 %collective-permute-start.2 = (f32[8,2,128,128]{3,2,1,0:T(8,128)}, f32[8,2,128,128]{3,2,1,0:T(8,128)S(1)}, u32[]{:S(2)}, u32[]{:S(2)}) collective-permute-start(f32[8,2,128,128]{3,2,1,0:T(8,128)} %take.1), channel_id=1, source_target_pairs={{0,12},{2,14},{4,0},{6,2},{8,4},{10,6},{12,8},{14,10},{1,13},{3,15... | collective-permute-start | bytes 3145736 | tf_op jit(solution)/shard_map/ppermute | solution.py:306
  38.6 6.6 %polar.2 = (f32[16,2,128,128]{3,2,1,0:T(8,128)}, f32[8,2,128,128]{3,2,1,0:T(8,128)}, f32[6,2,128,128]{3,2,1,0:T(8,128)}, f32[2,2,128,128]{3,2,1,0:T(8,128)}) custom-call(f32[16,2,128,128]{3,2,1,0:T(8,128)S(1)} %copy-done), custom_call_target="tpu_custom_call" | custom-call | tf_op jit(solution)/shard_map/polar/pallas_call | solution.py:94
  45.2 6.2 %polar.3 = (f32[16,2,128,128]{3,2,1,0:T(8,128)}, f32[8,2,128,128]{3,2,1,0:T(8,128)}) custom-call(f32[16,2,128,128]{3,2,1,0:T(8,128)S(1)} %copy-done, f32[16,2,128,128]{3,2,1,0:T(8,128)} %get-tuple-element.25.refs_0_), custom_call_target="tpu_custom_call", output_to_operand_aliasing={{0}: (1, {})} | custom-call | tf_op jit(solution)/shard_map/polar/pallas_call | solution.py:94
  51.4 0.5 collective-permute-start.4
  51.9 0.4 collective-permute-start.1
  52.4 0.4 collective-permute-start
  52.9 1.6 %copy-done.1 = f32[16,2,128,128]{3,2,1,0:T(8,128)S(1)} copy-done((f32[16,2,128,128]{3,2,1,0:T(8,128)S(1)}, f32[16,2,128,128]{3,2,1,0:T(8,128)}, u32[]{:S(2)}) %copy-start.1) | copy-done | bytes 2097176
  54.5 2.2 %copy-done.2 = f32[16,2,2,128,128]{4,3,2,1,0:T(8,128)S(1)} copy-done((f32[16,2,2,128,128]{4,3,2,1,0:T(8,128)S(1)}, f32[16,2,2,128,128]{4,3,2,1,0:T(8,128)}, u32[]{:S(2)}) %copy-start.2) | copy-done | bytes 4194328
  56.7 2.5 %sandwich.1 = (f32[16,128,256]{2,1,0:T(8,128)S(1)}, f32[16,128,256]{2,1,0:T(8,128)S(1)}) custom-call(f32[16,2,128,128]{3,2,1,0:T(8,128)S(1)} %copy-done.1, f32[16,2,2,128,128]{4,3,2,1,0:T(8,128)S(1)} %copy-done.2), custom_call_target="tpu_custom_call" | custom-call | tf_op jit(solution)/shard_map/sandwich/pallas_call | solution.py:142
  59.3 3.2 %collective-permute-done.2.partner_ref = f32[8,2,128,128]{3,2,1,0:T(8,128)S(1)} collective-permute-done((f32[8,2,128,128]{3,2,1,0:T(8,128)}, f32[8,2,128,128]{3,2,1,0:T(8,128)S(1)}, u32[]{:S(2)}, u32[]{:S(2)}) %collective-permute-start.2) | collective-permute-done | bytes 1048608 | tf_op jit(solution)/shard_map/ppermute | solution.py:306
  62.5 5.8 %plane.3 = (f32[16,128,256]{2,1,0:T(8,128)S(1)}, f32[16,8,128]{2,1,0:T(8,128)S(1)}, f32[8,128]{1,0:T(8,128)S(1)}) custom-call(s32[16]{0:T(128)S(1)} %select_reduce_fusion.order_ref, f32[16,128,256]{2,1,0:T(8,128)S(1)} %get-tuple-element.27.sandwich_ref, f32[8,2,128,128]{3,2,1,0:T(8,128)S(1)} %collective-permute-done.2.partner_ref), custom_call_target="tpu_custom_call" | custom-call | tf_op jit(solution)/shard_map/plane/pallas_call | solution.py:243
  68.4 2.5 %slab.1 = (f32[16,128,256]{2,1,0:T(8,128)S(1)}, f32[16,8,128]{2,1,0:T(8,128)S(1)}, f32[8,128]{1,0:T(8,128)S(1)}) custom-call(s32[16]{0:T(128)S(1)} %get-tuple-element.47.slots_ref, f32[8,128]{1,0:T(8,128)S(1)} %get-tuple-element.30.before_ref, f32[16,128,256]{2,1,0:T(8,128)S(1)} %get-tuple-element.31.sandwich_ref, f32[16,2,128,128]{3,2,1,0:T(8,128)S(1)} %copy-done.1, ...), custom_call_target="tpu_custom_call" | custom-call | tf_op jit(solution)/shard_map/slab/pallas_call | solution.py:201
  70.9 8.5 %collective-permute-done.1.partner_ref = f32[6,2,128,128]{3,2,1,0:T(8,128)} collective-permute-done((f32[6,2,128,128]{3,2,1,0:T(8,128)}, f32[6,2,128,128]{3,2,1,0:T(8,128)}, u32[]{:S(2)}, u32[]{:S(2)}) %collective-permute-start.1) | collective-permute-done | bytes 786464 | tf_op jit(solution)/shard_map/ppermute | solution.py:306
  79.4 1.7 %plane.4 = (f32[16,128,256]{2,1,0:T(8,128)S(1)}, f32[16,8,128]{2,1,0:T(8,128)S(1)}, f32[8,128]{1,0:T(8,128)S(1)}) custom-call(s32[16]{0:T(128)S(1)} %select_reduce_fusion.order_ref, f32[16,128,256]{2,1,0:T(8,128)S(1)} %get-tuple-element.27.sandwich_ref, ...), custom_call_target="tpu_custom_call", output_to_operand_aliasing={{0}: (4, {}), {1}: (5, {})} | custom-call | tf_op jit(solution)/shard_map/plane/pallas_call | solution.py:243
  81.0 2.8 %collective-permute-done.partner_ref = f32[2,2,128,128]{3,2,1,0:T(8,128)S(1)} collective-permute-done((f32[2,2,128,128]{3,2,1,0:T(8,128)}, f32[2,2,128,128]{3,2,1,0:T(8,128)S(1)}, u32[]{:S(2)}, u32[]{:S(2)}) %collective-permute-start) | collective-permute-done | bytes 262176 | tf_op jit(solution)/shard_map/ppermute | solution.py:306
  83.8 0.9 plane.5
  84.8 1.2 %collective-permute-done.5 = f32[8,128]{1,0:T(8,128)S(1)} collective-permute-done((f32[8,128]{1,0:T(8,128)S(1)}, f32[8,128]{1,0:T(8,128)S(1)}, u32[]{:S(2)}, u32[]{:S(2)}) %collective-permute-start.5) | collective-permute-done | bytes 4128 | tf_op jit(solution)/shard_map/ppermute | solution.py:306
  85.9 1.5 %collective-permute-start.6 = (f32[8,128]{1,0:T(8,128)S(1)}, f32[8,128]{1,0:T(8,128)S(1)}, u32[]{:S(2)}, u32[]{:S(2)}) collective-permute-start(f32[8,128]{1,0:T(8,128)S(1)} %add.34), channel_id=1, source_target_pairs={{0,2},{2,0},{4,6},{6,4},{8,10},{10,8},{12,14},{14,12},{1,3},{3,1},... | collective-permute-start | bytes 12296 | tf_op jit(solution)/shard_map/ppermute | solution.py:316
  87.4 2.1 %collective-permute-done.6 = f32[8,128]{1,0:T(8,128)S(1)} collective-permute-done((f32[8,128]{1,0:T(8,128)S(1)}, f32[8,128]{1,0:T(8,128)S(1)}, u32[]{:S(2)}, u32[]{:S(2)}) %collective-permute-start.6) | collective-permute-done | bytes 4128 | tf_op jit(solution)/shard_map/ppermute | solution.py:316
  89.9 3.3 %collective-permute-done.7 = f32[8,128]{1,0:T(8,128)S(1)} collective-permute-done((f32[8,128]{1,0:T(8,128)S(1)}, f32[8,128]{1,0:T(8,128)S(1)}, u32[]{:S(2)}, u32[]{:S(2)}) %collective-permute-start.7) | collective-permute-done | bytes 4128 | tf_op jit(solution)/shard_map/ppermute | solution.py:316
  93.2 2.7 %collective-permute-start.8 = (f32[8,128]{1,0:T(8,128)S(1)}, f32[8,128]{1,0:T(8,128)S(1)}, u32[]{:S(2)}, u32[]{:S(2)}) collective-permute-start(f32[8,128]{1,0:T(8,128)S(1)} %add.36.first_ref), channel_id=1, source_target_pairs={{0,8},{2,10},{4,12},{6,14},{8,0},{10,2},{12,4},{14,6},{1,9},{3,11}... | collective-permute-start | bytes 12296 | tf_op jit(solution)/shard_map/ppermute | solution.py:316
  95.9 1.8 %collective-permute-done.8.second_ref = f32[8,128]{1,0:T(8,128)S(1)} collective-permute-done((f32[8,128]{1,0:T(8,128)S(1)}, f32[8,128]{1,0:T(8,128)S(1)}, u32[]{:S(2)}, u32[]{:S(2)}) %collective-permute-start.8) | collective-permute-done | bytes 4128 | tf_op jit(solution)/shard_map/ppermute | solution.py:316
  97.7 2.7 %gradient.1 = (f32[16,2,128,128]{3,2,1,0:T(8,128)}, f32[2,128]{1,0:T(2,128)}) custom-call(s32[16]{0:T(128)S(1)} %get-tuple-element.48.slots_ref, f32[8,128]{1,0:T(8,128)S(1)} %add.36.first_ref, f32[8,128]{1,0:T(8,128)S(1)} %collective-permute-done.8.second_ref, f32[16,128,256]{2,1,0:T(8,128)S(1)} %get-tuple-element.41.plane_ref, ...), custom_call_target="tpu_custom_call" | custom-call | tf_op jit(solution)/shard_map/gradient/pallas_call | solution.py:290
  (17 shorter events, 0.6 us)
Async XLA Ops:
  0.6 38.0 %copy-start = (f32[16,2,128,128]{3,2,1,0:T(8,128)S(1)}, f32[16,2,128,128]{3,2,1,0:T(8,128)}, u32[]{:S(2)}) copy-start(f32[16,2,128,128]{3,2,1,0:T(8,128)} %start_ref.5) | copy-start | bytes 6291460
  33.5 29.0 %collective-permute-start.2 = (f32[8,2,128,128]{3,2,1,0:T(8,128)}, f32[8,2,128,128]{3,2,1,0:T(8,128)S(1)}, u32[]{:S(2)}, u32[]{:S(2)}) collective-permute-start(f32[8,2,128,128]{3,2,1,0:T(8,128)} %take.1), channel_id=1, source_target_pairs={{0,12},{2,14},{4,0},{6,2},{8,4},{10,6},{12,8},{14,10},{1,13},{3,15... | collective-permute-start | bytes 3145736 | tf_op jit(solution)/shard_map/ppermute | solution.py:306
  45.2 7.6 %copy-start.3 = (s32[16,2]{0,1:T(2,128)S(1)}, s32[16,2]{0,1:T(2,128)}, u32[]{:S(2)}) copy-start(s32[16,2]{0,1:T(2,128)} %param.5) | copy-start | bytes 388
  51.4 16.9 %collective-permute-start.3 = (f32[8,2,128,128]{3,2,1,0:T(8,128)}, f32[8,2,128,128]{3,2,1,0:T(8,128)S(1)}, u32[]{:S(2)}, u32[]{:S(2)}) collective-permute-start(f32[8,2,128,128]{3,2,1,0:T(8,128)} %get-tuple-element.32), channel_id=1, source_target_pairs={{0,1},{1,0},{2,3},{3,2},{4,5},{5,4},{6,7},{7,6},{8,9},{9,8},{10,11... | collective-permute-start | bytes 3145736 | tf_op jit(solution)/shard_map/ppermute | solution.py:306
  51.4 16.9 %collective-permute-start.4 = (f32[8,2,128,128]{3,2,1,0:T(8,128)}, f32[8,2,128,128]{3,2,1,0:T(8,128)S(1)}, u32[]{:S(2)}, u32[]{:S(2)}) collective-permute-start(f32[8,2,128,128]{3,2,1,0:T(8,128)} %get-tuple-element.33), channel_id=1, source_target_pairs={{0,1},{1,0},{2,3},{3,2},{4,5},{5,4},{6,7},{7,6},{8,9},{9,8},{10,11... | collective-permute-start | bytes 3145736 | tf_op jit(solution)/shard_map/ppermute | solution.py:306
  51.9 27.4 %collective-permute-start.1 = (f32[6,2,128,128]{3,2,1,0:T(8,128)}, f32[6,2,128,128]{3,2,1,0:T(8,128)}, u32[]{:S(2)}, u32[]{:S(2)}) collective-permute-start(f32[6,2,128,128]{3,2,1,0:T(8,128)} %get-tuple-element.29), channel_id=1, source_target_pairs={{0,12},{2,14},{4,0},{6,2},{8,4},{10,6},{12,8},{14,10},{1,13},{3,15... | collective-permute-start | bytes 2359304 | tf_op jit(solution)/shard_map/ppermute | solution.py:306
  52.4 31.4 %collective-permute-start = (f32[2,2,128,128]{3,2,1,0:T(8,128)}, f32[2,2,128,128]{3,2,1,0:T(8,128)S(1)}, u32[]{:S(2)}, u32[]{:S(2)}) collective-permute-start(f32[2,2,128,128]{3,2,1,0:T(8,128)} %get-tuple-element.28), channel_id=1, source_target_pairs={{0,12},{2,14},{4,0},{6,2},{8,4},{10,6},{12,8},{14,10},{1,13},{3,15... | collective-permute-start | bytes 786440 | tf_op jit(solution)/shard_map/ppermute | solution.py:306
  52.9 1.6 %copy-start.1 = (f32[16,2,128,128]{3,2,1,0:T(8,128)S(1)}, f32[16,2,128,128]{3,2,1,0:T(8,128)}, u32[]{:S(2)}) copy-start(f32[16,2,128,128]{3,2,1,0:T(8,128)} %get-tuple-element.22.rotation_ref.own_ref) | copy-start | bytes 6291460
  54.5 2.2 %copy-start.2 = (f32[16,2,2,128,128]{4,3,2,1,0:T(8,128)S(1)}, f32[16,2,2,128,128]{4,3,2,1,0:T(8,128)}, u32[]{:S(2)}) copy-start(f32[16,2,2,128,128]{4,3,2,1,0:T(8,128)} %correlation_ref.1) | copy-start | bytes 12582916
  84.7 1.2 %collective-permute-start.5 = (f32[8,128]{1,0:T(8,128)S(1)}, f32[8,128]{1,0:T(8,128)S(1)}, u32[]{:S(2)}, u32[]{:S(2)}) collective-permute-start(f32[8,128]{1,0:T(8,128)S(1)} %get-tuple-element.40), channel_id=1, source_target_pairs={{0,1},{1,0},{2,3},{3,2},{4,5},{5,4},{6,7},{7,6},{8,9},{9,8},{10,11... | collective-permute-start | bytes 12296 | tf_op jit(solution)/shard_map/ppermute | solution.py:306
  85.9 3.6 %collective-permute-start.6 = (f32[8,128]{1,0:T(8,128)S(1)}, f32[8,128]{1,0:T(8,128)S(1)}, u32[]{:S(2)}, u32[]{:S(2)}) collective-permute-start(f32[8,128]{1,0:T(8,128)S(1)} %add.34), channel_id=1, source_target_pairs={{0,2},{2,0},{4,6},{6,4},{8,10},{10,8},{12,14},{14,12},{1,3},{3,1},... | collective-permute-start | bytes 12296 | tf_op jit(solution)/shard_map/ppermute | solution.py:316
  89.5 3.6 %collective-permute-start.7 = (f32[8,128]{1,0:T(8,128)S(1)}, f32[8,128]{1,0:T(8,128)S(1)}, u32[]{:S(2)}, u32[]{:S(2)}) collective-permute-start(f32[8,128]{1,0:T(8,128)S(1)} %add.35), channel_id=1, source_target_pairs={{0,4},{2,6},{4,0},{6,2},{8,12},{10,14},{12,8},{14,10},{1,5},{3,7},... | collective-permute-start | bytes 12296 | tf_op jit(solution)/shard_map/ppermute | solution.py:316
  93.2 4.5 %collective-permute-start.8 = (f32[8,128]{1,0:T(8,128)S(1)}, f32[8,128]{1,0:T(8,128)S(1)}, u32[]{:S(2)}, u32[]{:S(2)}) collective-permute-start(f32[8,128]{1,0:T(8,128)S(1)} %add.36.first_ref), channel_id=1, source_target_pairs={{0,8},{2,10},{4,12},{6,14},{8,0},{10,2},{12,4},{14,6},{1,9},{3,11}... | collective-permute-start | bytes 12296 | tf_op jit(solution)/shard_map/ppermute | solution.py:316

commit v2 on v1

--- a/solution.py
+++ b/solution.py
@@ -8,7 +8,7 @@
 from jax.sharding import PartitionSpec as P
 
 NS_STEPS = 3
-RAW = (8,)
+RAW = 8
 CHUNKS = (6, 2)
 GROUP = 4
 VMEM = 32 << 20
@@ -104,27 +104,20 @@
     )(start, *carried)
 
 
-def take_kernel(start_ref, *refs):
-    *out_refs, sems = refs
-    copies = []
-    first = 0
-    for i, out_ref in enumerate(out_refs):
-        size = out_ref.shape[0]
-        copies.append(pltpu.make_async_copy(start_ref.at[pl.ds(first, size)], out_ref, sems.at[i]))
-        copies[-1].start()
-        first += size
-    for copy in copies:
-        copy.wait()
-
-
-def take_call(start, sizes):
-    anywhere = pl.BlockSpec(memory_space=pl.ANY)
+def take_kernel(start_ref, out_ref, sem):
+    copy = pltpu.make_async_copy(start_ref.at[pl.ds(0, out_ref.shape[0])], out_ref, sem)
+    copy.start()
+    copy.wait()
+
+
+def take_call(start, size):
     return pl.pallas_call(
         take_kernel,
-        in_specs=[anywhere],
-        out_specs=[anywhere] * len(sizes),
-        out_shape=[jax.ShapeDtypeStruct((size,) + start.shape[1:], start.dtype) for size in sizes],
-        scratch_shapes=[pltpu.SemaphoreType.DMA((len(sizes),))],
+        in_specs=[pl.BlockSpec(memory_space=pltpu.HBM)],
+        out_specs=pl.BlockSpec(memory_space=pltpu.VMEM),
+        out_shape=jax.ShapeDtypeStruct((size,) + start.shape[1:], start.dtype),
+        scratch_shapes=[pltpu.SemaphoreType.DMA],
+        compiler_params=pltpu.CompilerParams(vmem_limit_bytes=VMEM),
         name="take",
     )(start)
 
@@ -153,24 +146,51 @@
     )(rotation, correlations)
 
 
-def column_terms(rotated, rows_ref, i):
+def column_terms(rotated):
     n = rotated.shape[0]
     unit = identity(n)
     real = jnp.sum(rotated[:, :n] * unit, axis=0, keepdims=True)
     imag = jnp.sum(rotated[:, n:] * unit, axis=0, keepdims=True)
     phase = jnp.arctan2(imag, real)
     modulus = real * real + imag * imag
-    weight_real = imag / modulus
-    weight_imag = real / modulus
-    rows_ref[i, 0:1] = real + phase * weight_real
-    rows_ref[i, 1:2] = phase * weight_imag - imag
-    rows_ref[i, 2:3] = weight_real
-    rows_ref[i, 3:4] = weight_imag
-    return phase
-
-
-def slab_kernel(slots_ref, before_ref, sandwich_ref, own_ref, *refs, pieces):
-    piece_refs, (out_ref, rows_ref, total_ref, received_ref) = refs[:pieces], refs[pieces:]
+    w_real = imag / modulus
+    w_imag = real / modulus
+    return phase, (real + phase * w_real, phase * w_imag - imag, w_real, w_imag)
+
+
+def store_rows(rows_ref, i, rows):
+    for r, row in enumerate(rows):
+        rows_ref[i, r : r + 1] = row
+
+
+def load_rows(rows_ref, i):
+    return [rows_ref[i, r : r + 1] for r in range(4)]
+
+
+def scaled(matrix, v_real, v_imag):
+    n = matrix.shape[0]
+    real, imag = matrix[:, :n], matrix[:, n:]
+    return real * v_real - imag * v_imag, real * v_imag + imag * v_real
+
+
+def combine(parts_ref, slot, matrices, rows):
+    real, imag = (
+        sum(pair) for pair in zip(*(scaled(m, 2.0 * r[0], 2.0 * r[1]) for m, r in zip(matrices, rows)))
+    )
+    parts_ref[slot, 0] = real - real.T
+    parts_ref[slot, 1] = imag + imag.T
+    for d in range(2):
+        real, imag = scaled(matrices[d], 2.0 * rows[d][2], 2.0 * rows[d][3])
+        parts_ref[slot, 2 + 4 * d] = real
+        parts_ref[slot, 3 + 4 * d] = imag
+        parts_ref[slot, 4 + 4 * d] = real.T
+        parts_ref[slot, 5 + 4 * d] = imag.T
+
+
+def slab_kernel(
+    order_ref, slots_ref, before_ref, plane_ref, plane_rows, sandwich_ref, own_ref, *refs, pieces
+):
+    piece_refs, (out_ref, rows_ref, parts_ref, total_ref, received_ref) = refs[:pieces], refs[pieces:]
     count, _, n, _ = own_ref.shape
     first = 0
     for piece_ref in piece_refs:
@@ -188,39 +208,48 @@
             rotated.append(product(split(sandwich_ref[g * GROUP + i]), right))
         for i, matrix in enumerate(rotated):
             out_ref[g * GROUP + i] = matrix
-            total = total + column_terms(matrix, rows_ref, g * GROUP + i)
+            phase, rows = column_terms(matrix)
+            store_rows(rows_ref, g * GROUP + i, rows)
+            total = total + phase
         return total
 
     total_ref[...] = before_ref[...]
     total_ref[1:2] = lax.fori_loop(0, count // GROUP, group, jnp.zeros((1, n), jnp.float32))
 
-
-def slab_call(slots, total, sandwich, own, pieces):
+    @pl.loop(0, plane_ref.shape[0])
+    def _(slot):
+        k = order_ref[slot]
+        combine(
+            parts_ref,
+            slot,
+            (plane_ref[slot], out_ref[k]),
+            (load_rows(plane_rows, slot), load_rows(rows_ref, k)),
+        )
+
+
+def slab_call(order, slots, total, plane, plane_rows, sandwich, own, pieces):
     count, n, _ = sandwich.shape
     whole = pl.BlockSpec(memory_space=pltpu.VMEM)
+    scalars = pl.BlockSpec(memory_space=pltpu.SMEM)
     return pl.pallas_call(
         functools.partial(slab_kernel, pieces=len(pieces)),
-        in_specs=[pl.BlockSpec(memory_space=pltpu.SMEM)] + [whole] * (3 + len(pieces)),
-        out_specs=[whole] * 3,
+        in_specs=[scalars] * 2 + [whole] * (5 + len(pieces)),
+        out_specs=[whole] * 4,
         out_shape=[
             jax.ShapeDtypeStruct((count, n, 2 * n), jnp.float32),
             jax.ShapeDtypeStruct((count, 8, n), jnp.float32),
+            jax.ShapeDtypeStruct((count - CHUNKS[-1], 10, n, n), jnp.float32),
             jax.ShapeDtypeStruct((8, n), jnp.float32),
         ],
         scratch_shapes=[pltpu.VMEM(own.shape, own.dtype)],
         compiler_params=pltpu.CompilerParams(vmem_limit_bytes=VMEM),
         name="slab",
-    )(slots, total, sandwich, own, *pieces)
-
-
-def plane_kernel(order_ref, sandwich_ref, partner_ref, *refs, first, raw, earlier, carried):
-    total_refs, refs = refs[:earlier], refs[earlier:]
-    out_ref, rows_ref, total_ref = refs[2 * carried :]
+    )(order, slots, total, plane, plane_rows, sandwich, own, *pieces)
+
+
+def plane_products(order_ref, sandwich_ref, partner_ref, first, raw, finish):
     count = partner_ref.shape[0]
-    total = total_refs[0][...] if earlier else jnp.zeros_like(total_ref)
-    for other in total_refs[1:]:
-        total = total + other[...]
-    phases = jnp.zeros((1, partner_ref.shape[-1]), jnp.float32)
+    total = jnp.zeros((1, partner_ref.shape[-1]), jnp.float32)
     for begin in range(0, count, GROUP):
         group = range(begin, min(begin + GROUP, count))
         pairs = [(partner_ref[i, 0], partner_ref[i, 1]) for i in group]
@@ -230,66 +259,111 @@
             for i, partner in zip(group, partners)
         ]
         for i, matrix in zip(group, rotated):
-            out_ref[first + i] = matrix
-            phases = phases + column_terms(matrix, rows_ref, first + i)
-    total_ref[...] = total
-    total_ref[0:1] = total[0:1] + phases
-
-
-def plane_call(order, sandwich, partner, first, earlier, carried, raw):
-    count, n, _ = sandwich.shape
+            phase, rows = column_terms(matrix)
+            finish(i, matrix, rows)
+            total = total + phase
+    return total
+
+
+def plane_kernel(order_ref, sandwich_ref, partner_ref, *refs, first, raw, before):
+    before_refs, (out_ref, rows_ref, total_ref) = refs[:before], refs[before:]
+
+    def finish(i, matrix, rows):
+        out_ref[i] = matrix
+        store_rows(rows_ref, i, rows)
+
+    total = plane_products(order_ref, sandwich_ref, partner_ref, first, raw, finish)
+    total_ref[...] = before_refs[0][...] if before else jnp.zeros_like(total_ref)
+    total_ref[0:1] = total_ref[0:1] + total
+
+
+def plane_call(order, sandwich, partner, first, before, raw):
+    size, _, n, _ = partner.shape
     whole = pl.BlockSpec(memory_space=pltpu.VMEM)
-    position = 3 + len(earlier)
-    return pl.pallas_call(
-        functools.partial(plane_kernel, first=first, raw=raw, earlier=len(earlier), carried=bool(carried)),
-        in_specs=[pl.BlockSpec(memory_space=pltpu.SMEM)] + [whole] * (2 + len(earlier) + len(carried)),
+    return pl.pallas_call(
+        functools.partial(plane_kernel, first=first, raw=raw, before=len(before)),
+        in_specs=[pl.BlockSpec(memory_space=pltpu.SMEM)] + [whole] * (2 + len(before)),
         out_specs=[whole] * 3,
         out_shape=[
-            jax.ShapeDtypeStruct((count, n, 2 * n), jnp.float32),
-            jax.ShapeDtypeStruct((count, 8, n), jnp.float32),
+            jax.ShapeDtypeStruct((size, n, 2 * n), jnp.float32),
+            jax.ShapeDtypeStruct((size, 8, n), jnp.float32),
             jax.ShapeDtypeStruct((8, n), jnp.float32),
         ],
-        input_output_aliases={position: 0, position + 1: 1} if carried else {},
         compiler_params=pltpu.CompilerParams(vmem_limit_bytes=VMEM),
         name="plane",
-    )(order, sandwich, partner, *earlier, *carried)
+    )(order, sandwich, partner, *before)
+
+
+def middle_kernel(
+    order_ref, sandwich_ref, partner_ref, before_ref, slab_ref, slab_rows, _, parts_ref, total_ref, *, first
+):
+    def finish(i, matrix, rows):
+        k = order_ref[first + i]
+        combine(parts_ref, first + i, (matrix, slab_ref[k]), (rows, load_rows(slab_rows, k)))
+
+    total = plane_products(order_ref, sandwich_ref, partner_ref, first, False, finish)
+    total_ref[...] = before_ref[...]
+    total_ref[0:1] = total_ref[0:1] + total
+
+
+def middle_call(order, sandwich, partner, first, total, slab, slab_rows, parts):
+    whole = pl.BlockSpec(memory_space=pltpu.VMEM)
+    return pl.pallas_call(
+        functools.partial(middle_kernel, first=first),
+        in_specs=[pl.BlockSpec(memory_space=pltpu.SMEM)] + [whole] * 6,
+        out_specs=[whole] * 2,
+        out_shape=[
+            jax.ShapeDtypeStruct(parts.shape, parts.dtype),
+            jax.ShapeDtypeStruct(total.shape, total.dtype),
+        ],
+        input_output_aliases={6: 0},
+        compiler_params=pltpu.CompilerParams(vmem_limit_bytes=VMEM),
+        name="middle",
+    )(order, sandwich, partner, total, slab, slab_rows, parts)
 
 
 def gradient_kernel(
-    slots_ref, first_ref, second_ref, plane_ref, plane_rows, slab_ref, slab_rows, out_ref, centres_ref, buffer, sems, *, everything
+    order_ref, first_ref, second_ref, parts_ref, plane_ref, plane_rows, slab_ref, slab_rows, out_ref, centres_ref, buffer, sems, *, everything
 ):
     count, n, _ = slab_ref.shape
+    done = parts_ref.shape[0]
     centres = (first_ref[0:2] + second_ref[0:2]) / (-2.0 * everything)
     centres_ref[...] = centres
+    across = [centres[d : d + 1] for d in range(2)]
+    down = [jnp.broadcast_to(row, (n, n)).T for row in across]
     copies = []
-    for i in range(count):
-        real = imag = None
-        for d, (j, matrix, rows) in enumerate(
-            ((slots_ref[i], plane_ref, plane_rows), (i, slab_ref, slab_rows))
+
+    def send(slot, real, imag):
+        buffer[slot, 0] = real
+        buffer[slot, 1] = imag
+        copies.append(pltpu.make_async_copy(buffer.at[slot], out_ref.at[order_ref[slot]], sems.at[slot]))
+        copies[-1].start()
+
+    for slot in range(done, count):
+        k = order_ref[slot]
+        real = imag = jnp.zeros((n, n), jnp.float32)
+        for d, (matrix, rows) in enumerate(
+            ((plane_ref[slot - done], load_rows(plane_rows, slot - done)), (slab_ref[k], load_rows(slab_rows, k)))
         ):
-            centre = centres[d : d + 1]
-            v_real = 2.0 * (rows[j, 0:1] + centre * rows[j, 2:3])
-            v_imag = 2.0 * (rows[j, 1:2] + centre * rows[j, 3:4])
-            m_real = matrix[j, :, :n]
-            m_imag = matrix[j, :, n:]
-            y_real = m_real * v_real - m_imag * v_imag
-            y_imag = m_real * v_imag + m_imag * v_real
-            real = y_real if d == 0 else real + y_real
-            imag = y_imag if d == 0 else imag + y_imag
-        buffer[i, 0] = real - real.T
-        buffer[i, 1] = imag + imag.T
-        copies.append(pltpu.make_async_copy(buffer.at[i], out_ref.at[i], sems.at[i]))
-        copies[-1].start()
+            pair = scaled(matrix, 2.0 * (rows[0] + across[d] * rows[2]), 2.0 * (rows[1] + across[d] * rows[3]))
+            real, imag = real + pair[0], imag + pair[1]
+        send(slot, real - real.T, imag + imag.T)
+    for slot in range(done):
+        real, imag = parts_ref[slot, 0], parts_ref[slot, 1]
+        for d in range(2):
+            real = real + (parts_ref[slot, 2 + 4 * d] * across[d] - parts_ref[slot, 4 + 4 * d] * down[d])
+            imag = imag + (parts_ref[slot, 3 + 4 * d] * across[d] + parts_ref[slot, 5 + 4 * d] * down[d])
+        send(slot, real, imag)
     for copy in copies:
         copy.wait()
 
 
-def gradient_call(slots, totals, plane, plane_rows, slab, slab_rows, everything):
+def gradient_call(order, totals, parts, plane, plane_rows, slab, slab_rows, everything):
     count, n, _ = slab.shape
     whole = pl.BlockSpec(memory_space=pltpu.VMEM)
     return pl.pallas_call(
         functools.partial(gradient_kernel, everything=everything),
-        in_specs=[pl.BlockSpec(memory_space=pltpu.SMEM)] + [whole] * 6,
+        in_specs=[pl.BlockSpec(memory_space=pltpu.SMEM)] + [whole] * 7,
         out_specs=[pl.BlockSpec(memory_space=pl.ANY), whole],
         out_shape=[
             jax.ShapeDtypeStruct((count, 2, n, n), jnp.float32),
@@ -298,7 +372,7 @@
         scratch_shapes=[pltpu.VMEM((count, 2, n, n), jnp.float32), pltpu.SemaphoreType.DMA((count,))],
         compiler_params=pltpu.CompilerParams(vmem_limit_bytes=VMEM),
         name="gradient",
-    )(slots, *totals, plane, plane_rows, slab, slab_rows)
+    )(order, *totals, parts, plane, plane_rows, slab, slab_rows)
 
 
 def shifted(value, axis, steps):
@@ -308,12 +382,17 @@
 
 def reduce_parts(value):
     count = lax.axis_size("kxy")
-    if lax.axis_size("kz") != 2 or count & (count - 1) or count < 2:
+    if lax.axis_size("kz") != 2 or count & (count - 1) or count < 4:
         return lax.psum(value, ("kxy", "kz")), jnp.zeros_like(value)
-    value = value + shifted(value, "kz", 1)
-    distance = 1
+
+    def swapped(value, bits, core):
+        pairs = [(2 * s + c, 2 * (s ^ bits) + (c ^ core)) for s in range(count) for c in range(2)]
+        return lax.ppermute(value, ("kxy", "kz"), pairs)
+
+    value = value + swapped(value, 0, 1) + (swapped(value, 1, 0) + swapped(value, 1, 1))
+    distance = 2
     while True:
-        other = lax.ppermute(value, "kxy", [(source, source ^ distance) for source in range(count)])
+        other = swapped(value, distance, 0)
         distance *= 2
         if distance == count:
             return value, other
@@ -330,27 +409,23 @@
     remote = (neighbours[:, 1] // count != block_index).astype(jnp.int32)
     slab_slots = neighbours[:, 1] % count + count * remote
 
-    received = []
-    first = 0
-    for part in take_call(start_rotation, RAW):
-        received.append((first, True, shifted(part, "kxy", -2)))
-        first += part.shape[0]
-    rotation, late, *parts = polar_call(start_rotation, first, count - first, GROUP, [], CHUNKS)
-    for part in parts:
-        received.append((first, False, shifted(part, "kxy", -2)))
-        first += part.shape[0]
-    rotation, early = polar_call(start_rotation, 0, sum(RAW), GROUP, [rotation], ())
+    partners = [shifted(take_call(start_rotation, RAW), "kxy", -2)]
+    rotation, late, *parts = polar_call(start_rotation, RAW, count - RAW, GROUP, [], CHUNKS)
+    partners += [shifted(part, "kxy", -2) for part in parts]
+    rotation, early = polar_call(start_rotation, 0, RAW, GROUP, [rotation], ())
     from_slab = [shifted(part, "kz", -1) for part in (early, late)]
-    for_plane, for_slab = sandwich_call(rotation, correlations, 4)
-    total, carried = None, []
-    for first, raw, partner in received:
-        earlier = [] if total is None else [total]
-        plane, plane_rows, total = plane_call(order, for_plane, partner, first, earlier, carried, raw)
-        if not carried:
-            slab, slab_rows, total = slab_call(slab_slots, total, for_slab, rotation, from_slab)
-        carried = [plane, plane_rows]
+    for_plane, for_slab = sandwich_call(rotation, correlations, GROUP)
+    plane, plane_rows, total = plane_call(order, for_plane, partners[0], 0, [], True)
+    slab, slab_rows, parts, total = slab_call(
+        order, slab_slots, total, plane, plane_rows, for_slab, rotation, from_slab
+    )
+    first = RAW
+    for partner in partners[1:-1]:
+        parts, total = middle_call(order, for_plane, partner, first, total, slab, slab_rows, parts)
+        first += partner.shape[0]
+    plane, plane_rows, total = plane_call(order, for_plane, partners[-1], first, [total], False)
     gradient, centres = gradient_call(
-        plane_slots, reduce_parts(total), plane, plane_rows, slab, slab_rows, everything
+        order, reduce_parts(total), parts, plane, plane_rows, slab, slab_rows, everything
     )
     return (rotation, gradient, centres)
 

time: 101 us -> 69.4 us (0.69)
  Pallas kernels: 61.7 us -> 32.7 us
  waiting for transfers between devices: 22.8 us -> 18.4 us
  local copies, waits for them, and re-layouts: 3.78 us -> 5.37 us
    pallas_call x4, Pallas kernels: 41.3 us -> 9.66 us  [the longest x2 7.4 us: plane_call(): pl.pallas_call(functools.partial(plane_kernel, first=first, raw=raw, befo...]
    ppermute x6 -> x5, waiting for transfers between devices: 15.6 us -> 11.5 us  [shifted(): lax.ppermute(value, axis, [(source, (source + steps) % count) for source...]
    unnamed x8 -> x10, local copies, waits for them, and re-layouts: 3.78 us -> 5.37 us
    pallas_call x1, Pallas kernels: 2.49 us -> 4.07 us  [slab_call(): pl.pallas_call(functools.partial(slab_kernel, pieces=len(pieces)), in_spe...]
    pallas_call x1, Pallas kernels: 2.66 us -> 3.71 us  [gradient_call(): pl.pallas_call(functools.partial(gradient_kernel, everything=everything),...]
    ppermute x3 -> x5, starting transfers between devices: 4.56 us -> 5.06 us  [swapped(): return lax.ppermute(value, ('kxy', 'kz'), pairs)]
    ppermute x3 -> x5, waiting for transfers between devices: 7.16 us -> 6.89 us  [swapped(): return lax.ppermute(value, ('kxy', 'kz'), pairs)]
    ppermute x6 -> x5, starting transfers between devices: 6.58 us -> 6.51 us  [shifted(): lax.ppermute(value, axis, [(source, (source + steps) % count) for source...]
  transfers between devices with their start and end apart: 9 -> 10, of which waited for: 7 -> 7; matrix products, arithmetic and copies ran while one was open for 0% -> 0% of each run, Pallas kernels for 25% -> 41%
where the time goes in v2:
time: 69.4 us; the launch traced here: 69.1 us
  Pallas kernels  32.7 us (47%)
  waiting for transfers between devices  18.4 us (27%)
  starting transfers between devices  11.6 us (17%)
  local copies, waits for them, and re-layouts  5.37 us (8%)
  between operations  0.9 us (1%)
    pallas_call x2, Pallas kernels, polar_call(): pl.pallas_call(functools.partial(polar_kernel, carried=len(carried), chun...  12.8 us
    ppermute x5, waiting for transfers between devices, shifted(): lax.ppermute(value, axis, [(source, (source + steps) % count) for source...  11.5 us
    pallas_call x2, Pallas kernels, plane_call(): pl.pallas_call(functools.partial(plane_kernel, first=first, raw=raw, befo...  7.4 us
    ppermute x5, waiting for transfers between devices, swapped(): return lax.ppermute(value, ('kxy', 'kz'), pairs)  6.89 us
    ppermute x5, starting transfers between devices, shifted(): lax.ppermute(value, axis, [(source, (source + steps) % count) for source...  6.51 us
    unnamed x10, local copies, waits for them, and re-layouts  5.37 us
    ppermute x5, starting transfers between devices, swapped(): return lax.ppermute(value, ('kxy', 'kz'), pairs)  5.06 us
    pallas_call x1, Pallas kernels, slab_call(): pl.pallas_call(functools.partial(slab_kernel, pieces=len(pieces)), in_spe...  4.07 us
  transfers between devices with their start and end apart: 10, of which 7 were waited for; matrix products, arithmetic and copies ran while one was open for 0% of the time, Pallas kernels for 41%

profile of v2, /device:TPU:0, one launch (start us, length us, event | category | flops | bytes accessed | tf_op | source)
XLA Modules:
  0.0 69.1 jit_solution(16791401480260203975)
XLA Ops:
  0.6 1.6 %copy-done.2 = f32[16,2,128,128]{3,2,1,0:T(8,128)S(1)} copy-done((f32[16,2,128,128]{3,2,1,0:T(8,128)S(1)}, f32[16,2,128,128]{3,2,1,0:T(8,128)}, u32[]{:S(2)}) %copy-start.2) | copy-done | bytes 2097176
  2.3 5.1 %collective-permute-start.2 = (f32[8,2,128,128]{3,2,1,0:T(8,128)S(1)}, f32[8,2,128,128]{3,2,1,0:T(8,128)}, u32[]{:S(2)}, u32[]{:S(2)}) collective-permute-start(f32[8,2,128,128]{3,2,1,0:T(8,128)S(1)} %take.1), channel_id=1, source_target_pairs={{0,12},{2,14},{4,0},{6,2},{8,4},{10,6},{12,8},{14,10},{1,13},{3,15... | collective-permute-start | bytes 3145736 | tf_op jit(solution)/shard_map/ppermute | solution.py:380
  7.4 6.6 %polar.2 = (f32[16,2,128,128]{3,2,1,0:T(8,128)}, f32[8,2,128,128]{3,2,1,0:T(8,128)}, f32[6,2,128,128]{3,2,1,0:T(8,128)}, f32[2,2,128,128]{3,2,1,0:T(8,128)}) custom-call(f32[16,2,128,128]{3,2,1,0:T(8,128)S(1)} %copy-done.2), custom_call_target="tpu_custom_call" | custom-call | tf_op jit(solution)/shard_map/polar/pallas_call | solution.py:94
  14.0 6.2 %polar.3 = (f32[16,2,128,128]{3,2,1,0:T(8,128)}, f32[8,2,128,128]{3,2,1,0:T(8,128)}) custom-call(f32[16,2,128,128]{3,2,1,0:T(8,128)S(1)} %copy-done.2, f32[16,2,128,128]{3,2,1,0:T(8,128)} %get-tuple-element.25.refs_0_), custom_call_target="tpu_custom_call", output_to_operand_aliasing={{0}: (1, {})} | custom-call | tf_op jit(solution)/shard_map/polar/pallas_call | solution.py:94
  20.2 0.5 collective-permute-start.4
  20.7 0.4 collective-permute-start.1
  21.2 0.4 collective-permute-start
  21.7 1.6 %copy-done = f32[16,2,128,128]{3,2,1,0:T(8,128)S(1)} copy-done((f32[16,2,128,128]{3,2,1,0:T(8,128)S(1)}, f32[16,2,128,128]{3,2,1,0:T(8,128)}, u32[]{:S(2)}) %copy-start) | copy-done | bytes 2097176
  23.3 2.2 %copy-done.3 = f32[16,2,2,128,128]{4,3,2,1,0:T(8,128)S(1)} copy-done((f32[16,2,2,128,128]{4,3,2,1,0:T(8,128)S(1)}, f32[16,2,2,128,128]{4,3,2,1,0:T(8,128)}, u32[]{:S(2)}) %copy-start.3) | copy-done | bytes 4194328
  25.5 2.5 %sandwich.1 = (f32[16,128,256]{2,1,0:T(8,128)S(1)}, f32[16,128,256]{2,1,0:T(8,128)S(1)}) custom-call(f32[16,2,128,128]{3,2,1,0:T(8,128)S(1)} %copy-done, f32[16,2,2,128,128]{4,3,2,1,0:T(8,128)S(1)} %copy-done.3), custom_call_target="tpu_custom_call" | custom-call | tf_op jit(solution)/shard_map/sandwich/pallas_call | solution.py:135
  28.1 2.9 %collective-permute-done.2.partner_ref = f32[8,2,128,128]{3,2,1,0:T(8,128)} collective-permute-done((f32[8,2,128,128]{3,2,1,0:T(8,128)S(1)}, f32[8,2,128,128]{3,2,1,0:T(8,128)}, u32[]{:S(2)}, u32[]{:S(2)}) %collective-permute-start.2) | collective-permute-done | bytes 1048608 | tf_op jit(solution)/shard_map/ppermute | solution.py:380
  31.0 6.5 %plane.2 = (f32[8,128,256]{2,1,0:T(8,128)S(1)}, f32[8,8,128]{2,1,0:T(8,128)S(1)}, f32[8,128]{1,0:T(8,128)S(1)}) custom-call(s32[16]{0:T(128)S(1)} %select_reduce_fusion.order_ref, f32[16,128,256]{2,1,0:T(8,128)S(1)} %get-tuple-element.27.sandwich_ref, f32[8,2,128,128]{3,2,1,0:T(8,128)} %collective-permute-done.2.partner_ref), custom_call_target="tpu_custom_call" | custom-call | tf_op jit(solution)/shard_map/plane/pallas_call | solution.py:283
  37.5 4.1 %slab.1 = (f32[16,128,256]{2,1,0:T(8,128)S(1)}, f32[16,8,128]{2,1,0:T(8,128)S(1)}, f32[14,10,128,128]{3,2,1,0:T(8,128)S(1)}, f32[8,128]{1,0:T(8,128)S(1)}) custom-call(s32[16]{0:T(128)S(1)} %select_reduce_fusion.order_ref, s32[16]{0:T(128)S(1)} %fusion.slots_ref, f32[8,128]{1,0:T(8,128)S(1)} %get-tuple-element.30.before_ref, ...), custom_call_target="tpu_custom_call" | custom-call | tf_op jit(solution)/shard_map/slab/pallas_call | solution.py:234
  41.6 6.3 %collective-permute-done.1.partner_ref = f32[6,2,128,128]{3,2,1,0:T(8,128)} collective-permute-done((f32[6,2,128,128]{3,2,1,0:T(8,128)}, f32[6,2,128,128]{3,2,1,0:T(8,128)}, u32[]{:S(2)}, u32[]{:S(2)}) %collective-permute-start.1) | collective-permute-done | bytes 786464 | tf_op jit(solution)/shard_map/ppermute | solution.py:380
  47.9 2.2 %middle.1 = (f32[14,10,128,128]{3,2,1,0:T(8,128)S(1)}, f32[8,128]{1,0:T(8,128)S(1)}) custom-call(s32[16]{0:T(128)S(1)} %select_reduce_fusion.order_ref, f32[16,128,256]{2,1,0:T(8,128)S(1)} %get-tuple-element.27.sandwich_ref, f32[6,2,128,128]{3,2,1,0:T(8,128)} %collective-permute-done.1.partner_ref, ...), custom_call_target="tpu_custom_call", output_to_operand_aliasing={{0}: (6, {})} | custom-call | tf_op jit(solution)/shard_map/middle/pallas_call | solution.py:311
  50.1 2.3 %collective-permute-done.partner_ref = f32[2,2,128,128]{3,2,1,0:T(8,128)S(1)} collective-permute-done((f32[2,2,128,128]{3,2,1,0:T(8,128)}, f32[2,2,128,128]{3,2,1,0:T(8,128)S(1)}, u32[]{:S(2)}, u32[]{:S(2)}) %collective-permute-start) | collective-permute-done | bytes 262176 | tf_op jit(solution)/shard_map/ppermute | solution.py:380
  52.4 0.9 %plane.3 = (f32[2,128,256]{2,1,0:T(8,128)S(1)}, f32[2,8,128]{2,1,0:T(8,128)S(1)}, f32[8,128]{1,0:T(8,128)S(1)}) custom-call(s32[16]{0:T(128)S(1)} %select_reduce_fusion.order_ref, f32[16,128,256]{2,1,0:T(8,128)S(1)} %get-tuple-element.27.sandwich_ref, f32[2,2,128,128]{3,2,1,0:T(8,128)S(1)} %collective-permute-done.partner_ref, ...), custom_call_target="tpu_custom_call" | custom-call | tf_op jit(solution)/shard_map/plane/pallas_call | solution.py:283
  53.4 1.5 %collective-permute-start.6 = (f32[8,128]{1,0:T(8,128)S(1)}, f32[8,128]{1,0:T(8,128)S(1)}, u32[]{:S(2)}, u32[]{:S(2)}) collective-permute-start(f32[8,128]{1,0:T(8,128)S(1)} %get-tuple-element.41), channel_id=1, source_target_pairs={{0,2},{1,3},{2,0},{3,1},{4,6},{5,7},{6,4},{7,5},{8,10},{9,11},{10,... | collective-permute-start | bytes 12296 | tf_op jit(solution)/shard_map/ppermute | solution.py:390
  55.2 1.2 %collective-permute-done.7 = f32[8,128]{1,0:T(8,128)S(1)} collective-permute-done((f32[8,128]{1,0:T(8,128)S(1)}, f32[8,128]{1,0:T(8,128)S(1)}, u32[]{:S(2)}, u32[]{:S(2)}) %collective-permute-start.7) | collective-permute-done | bytes 4128 | tf_op jit(solution)/shard_map/ppermute | solution.py:390
  56.4 0.7 collective-permute-done.6
  57.5 3.3 %collective-permute-done.8 = f32[8,128]{1,0:T(8,128)S(1)} collective-permute-done((f32[8,128]{1,0:T(8,128)S(1)}, f32[8,128]{1,0:T(8,128)S(1)}, u32[]{:S(2)}, u32[]{:S(2)}) %collective-permute-start.8) | collective-permute-done | bytes 4128 | tf_op jit(solution)/shard_map/ppermute | solution.py:390
  60.7 2.7 %collective-permute-start.9 = (f32[8,128]{1,0:T(8,128)S(1)}, f32[8,128]{1,0:T(8,128)S(1)}, u32[]{:S(2)}, u32[]{:S(2)}) collective-permute-start(f32[8,128]{1,0:T(8,128)S(1)} %add.37.first_ref), channel_id=1, source_target_pairs={{0,8},{1,9},{2,10},{3,11},{4,12},{5,13},{6,14},{7,15},{8,0},{9,1},... | collective-permute-start | bytes 12296 | tf_op jit(solution)/shard_map/ppermute | solution.py:390
  63.4 1.8 %collective-permute-done.9.second_ref = f32[8,128]{1,0:T(8,128)S(1)} collective-permute-done((f32[8,128]{1,0:T(8,128)S(1)}, f32[8,128]{1,0:T(8,128)S(1)}, u32[]{:S(2)}, u32[]{:S(2)}) %collective-permute-start.9) | collective-permute-done | bytes 4128 | tf_op jit(solution)/shard_map/ppermute | solution.py:390
  65.2 3.7 %gradient.1 = (f32[16,2,128,128]{3,2,1,0:T(8,128)}, f32[2,128]{1,0:T(2,128)}) custom-call(s32[16]{0:T(128)S(1)} %select_reduce_fusion.order_ref, f32[8,128]{1,0:T(8,128)S(1)} %add.37.first_ref, f32[8,128]{1,0:T(8,128)S(1)} %collective-permute-done.9.second_ref, f32[14,10,128,128]{3,2,1,0:T(8,128)S(1)} %get-tuple-element.42.parts_ref, ...), custom_call_target="tpu_custom_call" | custom-call | tf_op jit(solution)/shard_map/gradient/pallas_call | solution.py:364
  (20 shorter events, 1.1 us)
Async XLA Ops:
  0.6 1.6 %copy-start.2 = (f32[16,2,128,128]{3,2,1,0:T(8,128)S(1)}, f32[16,2,128,128]{3,2,1,0:T(8,128)}, u32[]{:S(2)}) copy-start(f32[16,2,128,128]{3,2,1,0:T(8,128)} %start_ref.5) | copy-start | bytes 6291460
  2.3 28.7 %collective-permute-start.2 = (f32[8,2,128,128]{3,2,1,0:T(8,128)S(1)}, f32[8,2,128,128]{3,2,1,0:T(8,128)}, u32[]{:S(2)}, u32[]{:S(2)}) collective-permute-start(f32[8,2,128,128]{3,2,1,0:T(8,128)S(1)} %take.1), channel_id=1, source_target_pairs={{0,12},{2,14},{4,0},{6,2},{8,4},{10,6},{12,8},{14,10},{1,13},{3,15... | collective-permute-start | bytes 3145736 | tf_op jit(solution)/shard_map/ppermute | solution.py:380
  14.0 7.6 %copy-start.4 = (s32[16,2]{0,1:T(2,128)S(1)}, s32[16,2]{0,1:T(2,128)}, u32[]{:S(2)}) copy-start(s32[16,2]{0,1:T(2,128)} %param.5) | copy-start | bytes 388
  20.2 17.3 %collective-permute-start.3 = (f32[8,2,128,128]{3,2,1,0:T(8,128)}, f32[8,2,128,128]{3,2,1,0:T(8,128)S(1)}, u32[]{:S(2)}, u32[]{:S(2)}) collective-permute-start(f32[8,2,128,128]{3,2,1,0:T(8,128)} %get-tuple-element.34), channel_id=1, source_target_pairs={{0,1},{1,0},{2,3},{3,2},{4,5},{5,4},{6,7},{7,6},{8,9},{9,8},{10,11... | collective-permute-start | bytes 3145736 | tf_op jit(solution)/shard_map/ppermute | solution.py:380
  20.2 17.3 %collective-permute-start.4 = (f32[8,2,128,128]{3,2,1,0:T(8,128)}, f32[8,2,128,128]{3,2,1,0:T(8,128)S(1)}, u32[]{:S(2)}, u32[]{:S(2)}) collective-permute-start(f32[8,2,128,128]{3,2,1,0:T(8,128)} %get-tuple-element.35), channel_id=1, source_target_pairs={{0,1},{1,0},{2,3},{3,2},{4,5},{5,4},{6,7},{7,6},{8,9},{9,8},{10,11... | collective-permute-start | bytes 3145736 | tf_op jit(solution)/shard_map/ppermute | solution.py:380
  20.7 27.2 %collective-permute-start.1 = (f32[6,2,128,128]{3,2,1,0:T(8,128)}, f32[6,2,128,128]{3,2,1,0:T(8,128)}, u32[]{:S(2)}, u32[]{:S(2)}) collective-permute-start(f32[6,2,128,128]{3,2,1,0:T(8,128)} %get-tuple-element.29), channel_id=1, source_target_pairs={{0,12},{2,14},{4,0},{6,2},{8,4},{10,6},{12,8},{14,10},{1,13},{3,15... | collective-permute-start | bytes 2359304 | tf_op jit(solution)/shard_map/ppermute | solution.py:380
  21.2 31.2 %collective-permute-start = (f32[2,2,128,128]{3,2,1,0:T(8,128)}, f32[2,2,128,128]{3,2,1,0:T(8,128)S(1)}, u32[]{:S(2)}, u32[]{:S(2)}) collective-permute-start(f32[2,2,128,128]{3,2,1,0:T(8,128)} %get-tuple-element.28), channel_id=1, source_target_pairs={{0,12},{2,14},{4,0},{6,2},{8,4},{10,6},{12,8},{14,10},{1,13},{3,15... | collective-permute-start | bytes 786440 | tf_op jit(solution)/shard_map/ppermute | solution.py:380
  21.7 1.6 %copy-start = (f32[16,2,128,128]{3,2,1,0:T(8,128)S(1)}, f32[16,2,128,128]{3,2,1,0:T(8,128)}, u32[]{:S(2)}) copy-start(f32[16,2,128,128]{3,2,1,0:T(8,128)} %get-tuple-element.22.rotation_ref.own_ref) | copy-start | bytes 6291460
  23.3 2.2 %copy-start.3 = (f32[16,2,2,128,128]{4,3,2,1,0:T(8,128)S(1)}, f32[16,2,2,128,128]{4,3,2,1,0:T(8,128)}, u32[]{:S(2)}) copy-start(f32[16,2,2,128,128]{4,3,2,1,0:T(8,128)} %correlation_ref.1) | copy-start | bytes 12582916
  28.0 9.5 %copy-start.1 = (f32[16,2,128,128]{3,2,1,0:T(8,128)S(1)}, f32[16,2,128,128]{3,2,1,0:T(8,128)}, u32[]{:S(2)}) copy-start(f32[16,2,128,128]{3,2,1,0:T(8,128)} %get-tuple-element.22.rotation_ref.own_ref) | copy-start | bytes 6291460
  53.3 3.1 %collective-permute-start.7 = (f32[8,128]{1,0:T(8,128)S(1)}, f32[8,128]{1,0:T(8,128)S(1)}, u32[]{:S(2)}, u32[]{:S(2)}) collective-permute-start(f32[8,128]{1,0:T(8,128)S(1)} %get-tuple-element.41), channel_id=1, source_target_pairs={{0,3},{1,2},{2,1},{3,0},{4,7},{5,6},{6,5},{7,4},{8,11},{9,10},{10,... | collective-permute-start | bytes 12296 | tf_op jit(solution)/shard_map/ppermute | solution.py:390
  53.4 3.6 %collective-permute-start.6 = (f32[8,128]{1,0:T(8,128)S(1)}, f32[8,128]{1,0:T(8,128)S(1)}, u32[]{:S(2)}, u32[]{:S(2)}) collective-permute-start(f32[8,128]{1,0:T(8,128)S(1)} %get-tuple-element.41), channel_id=1, source_target_pairs={{0,2},{1,3},{2,0},{3,1},{4,6},{5,7},{6,4},{7,5},{8,10},{9,11},{10,... | collective-permute-start | bytes 12296 | tf_op jit(solution)/shard_map/ppermute | solution.py:390
  54.9 2.1 %collective-permute-start.5 = (f32[8,128]{1,0:T(8,128)S(1)}, f32[8,128]{1,0:T(8,128)S(1)}, u32[]{:S(2)}, u32[]{:S(2)}) collective-permute-start(f32[8,128]{1,0:T(8,128)S(1)} %get-tuple-element.41), channel_id=1, source_target_pairs={{0,1},{1,0},{2,3},{3,2},{4,5},{5,4},{6,7},{7,6},{8,9},{9,8},{10,11... | collective-permute-start | bytes 12296 | tf_op jit(solution)/shard_map/ppermute | solution.py:390
  57.0 3.7 %collective-permute-start.8 = (f32[8,128]{1,0:T(8,128)S(1)}, f32[8,128]{1,0:T(8,128)S(1)}, u32[]{:S(2)}, u32[]{:S(2)}) collective-permute-start(f32[8,128]{1,0:T(8,128)S(1)} %add_add_fusion), channel_id=1, source_target_pairs={{0,4},{1,5},{2,6},{3,7},{4,0},{5,1},{6,2},{7,3},{8,12},{9,13},{10,... | collective-permute-start | bytes 12296 | tf_op jit(solution)/shard_map/ppermute | solution.py:390
  60.7 4.5 %collective-permute-start.9 = (f32[8,128]{1,0:T(8,128)S(1)}, f32[8,128]{1,0:T(8,128)S(1)}, u32[]{:S(2)}, u32[]{:S(2)}) collective-permute-start(f32[8,128]{1,0:T(8,128)S(1)} %add.37.first_ref), channel_id=1, source_target_pairs={{0,8},{1,9},{2,10},{3,11},{4,12},{5,13},{6,14},{7,15},{8,0},{9,1},... | collective-permute-start | bytes 12296 | tf_op jit(solution)/shard_map/ppermute | solution.py:390

commit v3 on v2

--- a/solution.py
+++ b/solution.py
@@ -11,7 +11,7 @@
 RAW = 8
 CHUNKS = (6, 2)
 GROUP = 4
-VMEM = 32 << 20
+VMEM = 16 << 20
 
 
 def dot(left, right, contract):
@@ -101,7 +101,7 @@
         input_output_aliases={1: 0} if carried else {},
         compiler_params=pltpu.CompilerParams(vmem_limit_bytes=VMEM),
         name="polar",
-    )(start, *carried)
+    )(pltpu.with_memory_space_constraint(start, pltpu.HBM), *carried)
 
 
 def take_kernel(start_ref, out_ref, sem):
@@ -119,7 +119,7 @@
         scratch_shapes=[pltpu.SemaphoreType.DMA],
         compiler_params=pltpu.CompilerParams(vmem_limit_bytes=VMEM),
         name="take",
-    )(start)
+    )(pltpu.with_memory_space_constraint(start, pltpu.HBM))
 
 
 def sandwich_kernel(rotation_ref, correlation_ref, *out_refs):
@@ -173,18 +173,18 @@
     return real * v_real - imag * v_imag, real * v_imag + imag * v_real
 
 
-def combine(parts_ref, slot, matrices, rows):
+def combine(parts_ref, k, matrices, rows):
     real, imag = (
         sum(pair) for pair in zip(*(scaled(m, 2.0 * r[0], 2.0 * r[1]) for m, r in zip(matrices, rows)))
     )
-    parts_ref[slot, 0] = real - real.T
-    parts_ref[slot, 1] = imag + imag.T
+    parts_ref[k, 0] = real - real.T
+    parts_ref[k, 1] = imag + imag.T
     for d in range(2):
         real, imag = scaled(matrices[d], 2.0 * rows[d][2], 2.0 * rows[d][3])
-        parts_ref[slot, 2 + 4 * d] = real
-        parts_ref[slot, 3 + 4 * d] = imag
-        parts_ref[slot, 4 + 4 * d] = real.T
-        parts_ref[slot, 5 + 4 * d] = imag.T
+        parts_ref[k, 2 + 4 * d] = real
+        parts_ref[k, 3 + 4 * d] = imag
+        parts_ref[k, 4 + 4 * d] = real.T
+        parts_ref[k, 5 + 4 * d] = imag.T
 
 
 def slab_kernel(
@@ -221,7 +221,7 @@
         k = order_ref[slot]
         combine(
             parts_ref,
-            slot,
+            k,
             (plane_ref[slot], out_ref[k]),
             (load_rows(plane_rows, slot), load_rows(rows_ref, k)),
         )
@@ -238,7 +238,7 @@
         out_shape=[
             jax.ShapeDtypeStruct((count, n, 2 * n), jnp.float32),
             jax.ShapeDtypeStruct((count, 8, n), jnp.float32),
-            jax.ShapeDtypeStruct((count - CHUNKS[-1], 10, n, n), jnp.float32),
+            jax.ShapeDtypeStruct((count, 10, n, n), jnp.float32),
             jax.ShapeDtypeStruct((8, n), jnp.float32),
         ],
         scratch_shapes=[pltpu.VMEM(own.shape, own.dtype)],
@@ -247,7 +247,7 @@
     )(order, slots, total, plane, plane_rows, sandwich, own, *pieces)
 
 
-def plane_products(order_ref, sandwich_ref, partner_ref, first, raw, finish):
+def plane_products(partner_ref, picked, raw, finish):
     count = partner_ref.shape[0]
     total = jnp.zeros((1, partner_ref.shape[-1]), jnp.float32)
     for begin in range(0, count, GROUP):
@@ -255,8 +255,7 @@
         pairs = [(partner_ref[i, 0], partner_ref[i, 1]) for i in group]
         partners = polar(pairs) if raw else [jnp.concatenate(pair, 1) for pair in pairs]
         rotated = [
-            product(split(sandwich_ref[order_ref[first + i]]), both(right_form, split(partner)))
-            for i, partner in zip(group, partners)
+            product(split(picked(i)), both(right_form, split(partner))) for i, partner in zip(group, partners)
         ]
         for i, matrix in zip(group, rotated):
             phase, rows = column_terms(matrix)
@@ -265,24 +264,22 @@
     return total
 
 
-def plane_kernel(order_ref, sandwich_ref, partner_ref, *refs, first, raw, before):
-    before_refs, (out_ref, rows_ref, total_ref) = refs[:before], refs[before:]
-
+def plane_kernel(order_ref, sandwich_ref, partner_ref, before_ref, out_ref, rows_ref, total_ref, *, first):
     def finish(i, matrix, rows):
-        out_ref[i] = matrix
-        store_rows(rows_ref, i, rows)
-
-    total = plane_products(order_ref, sandwich_ref, partner_ref, first, raw, finish)
-    total_ref[...] = before_refs[0][...] if before else jnp.zeros_like(total_ref)
+        out_ref[first + i] = matrix
+        store_rows(rows_ref, first + i, rows)
+
+    total = plane_products(partner_ref, lambda i: sandwich_ref[order_ref[first + i]], True, finish)
+    total_ref[...] = before_ref[...]
     total_ref[0:1] = total_ref[0:1] + total
 
 
-def plane_call(order, sandwich, partner, first, before, raw):
+def plane_call(order, sandwich, partner, first, total):
     size, _, n, _ = partner.shape
     whole = pl.BlockSpec(memory_space=pltpu.VMEM)
     return pl.pallas_call(
-        functools.partial(plane_kernel, first=first, raw=raw, before=len(before)),
-        in_specs=[pl.BlockSpec(memory_space=pltpu.SMEM)] + [whole] * (2 + len(before)),
+        functools.partial(plane_kernel, first=first),
+        in_specs=[pl.BlockSpec(memory_space=pltpu.SMEM)] + [whole] * 3,
         out_specs=[whole] * 3,
         out_shape=[
             jax.ShapeDtypeStruct((size, n, 2 * n), jnp.float32),
@@ -291,30 +288,36 @@
         ],
         compiler_params=pltpu.CompilerParams(vmem_limit_bytes=VMEM),
         name="plane",
-    )(order, sandwich, partner, *before)
+    )(order, sandwich, partner, total)
 
 
 def middle_kernel(
-    order_ref, sandwich_ref, partner_ref, before_ref, slab_ref, slab_rows, _, parts_ref, total_ref, *, first
+    order_ref, sandwich_ref, partner_ref, before_ref, slab_ref, slab_rows, _, parts_ref, total_ref, last_ref, *, first
 ):
+    size = partner_ref.shape[0]
+    for i in range(last_ref.shape[0]):
+        last_ref[i] = sandwich_ref[order_ref[first + size + i]]
+
     def finish(i, matrix, rows):
         k = order_ref[first + i]
-        combine(parts_ref, first + i, (matrix, slab_ref[k]), (rows, load_rows(slab_rows, k)))
-
-    total = plane_products(order_ref, sandwich_ref, partner_ref, first, False, finish)
+        combine(parts_ref, k, (matrix, slab_ref[k]), (rows, load_rows(slab_rows, k)))
+
+    total = plane_products(partner_ref, lambda i: sandwich_ref[order_ref[first + i]], False, finish)
     total_ref[...] = before_ref[...]
     total_ref[0:1] = total_ref[0:1] + total
 
 
-def middle_call(order, sandwich, partner, first, total, slab, slab_rows, parts):
+def middle_call(order, sandwich, partner, first, total, slab, slab_rows, parts, last):
+    _, n, width = sandwich.shape
     whole = pl.BlockSpec(memory_space=pltpu.VMEM)
     return pl.pallas_call(
         functools.partial(middle_kernel, first=first),
         in_specs=[pl.BlockSpec(memory_space=pltpu.SMEM)] + [whole] * 6,
-        out_specs=[whole] * 2,
+        out_specs=[whole] * 3,
         out_shape=[
             jax.ShapeDtypeStruct(parts.shape, parts.dtype),
             jax.ShapeDtypeStruct(total.shape, total.dtype),
+            jax.ShapeDtypeStruct((last, n, width), sandwich.dtype),
         ],
         input_output_aliases={6: 0},
         compiler_params=pltpu.CompilerParams(vmem_limit_bytes=VMEM),
@@ -322,57 +325,103 @@
     )(order, sandwich, partner, total, slab, slab_rows, parts)
 
 
-def gradient_kernel(
-    order_ref, first_ref, second_ref, parts_ref, plane_ref, plane_rows, slab_ref, slab_rows, out_ref, centres_ref, buffer, sems, *, everything
-):
-    count, n, _ = slab_ref.shape
-    done = parts_ref.shape[0]
+def last_kernel(sandwich_ref, partner_ref, before_ref, out_ref, rows_ref, total_ref):
+    def finish(i, matrix, rows):
+        out_ref[i] = matrix
+        store_rows(rows_ref, i, rows)
+
+    total = plane_products(partner_ref, lambda i: sandwich_ref[i], False, finish)
+    total_ref[...] = before_ref[...]
+    total_ref[0:1] = total_ref[0:1] + total
+
+
+def last_call(sandwich, partner, total):
+    size, n, width = sandwich.shape
+    whole = pl.BlockSpec(memory_space=pltpu.VMEM)
+    return pl.pallas_call(
+        last_kernel,
+        in_specs=[whole] * 3,
+        out_specs=[whole] * 3,
+        out_shape=[
+            jax.ShapeDtypeStruct((size, n, width), jnp.float32),
+            jax.ShapeDtypeStruct((size, 8, n), jnp.float32),
+            jax.ShapeDtypeStruct(total.shape, total.dtype),
+        ],
+        compiler_params=pltpu.CompilerParams(vmem_limit_bytes=VMEM),
+        name="last",
+    )(sandwich, partner, total)
+
+
+def combine_kernel(order_ref, plane_ref, plane_rows, slab_ref, slab_rows, _, parts_ref, *, first):
+    for i in range(plane_ref.shape[0]):
+        k = order_ref[first + i]
+        combine(
+            parts_ref, k, (plane_ref[i], slab_ref[k]), (load_rows(plane_rows, i), load_rows(slab_rows, k))
+        )
+
+
+def combine_call(order, plane, plane_rows, slab, slab_rows, parts, first):
+    whole = pl.BlockSpec(memory_space=pltpu.VMEM)
+    return pl.pallas_call(
+        functools.partial(combine_kernel, first=first),
+        in_specs=[pl.BlockSpec(memory_space=pltpu.SMEM)] + [whole] * 5,
+        out_specs=whole,
+        out_shape=jax.ShapeDtypeStruct(parts.shape, parts.dtype),
+        input_output_aliases={5: 0},
+        compiler_params=pltpu.CompilerParams(vmem_limit_bytes=VMEM),
+        name="combine",
+    )(order, plane, plane_rows, slab, slab_rows, parts)
+
+
+def gradient_kernel(first_ref, second_ref, parts_ref, out_ref, centres_ref, buffer, small, sems, small_sem, *, everything):
+    count, _, n, _ = buffer.shape
     centres = (first_ref[0:2] + second_ref[0:2]) / (-2.0 * everything)
-    centres_ref[...] = centres
+    small[...] = centres
+    small_copy = pltpu.make_async_copy(small, centres_ref, small_sem)
+    small_copy.start()
     across = [centres[d : d + 1] for d in range(2)]
     down = [jnp.broadcast_to(row, (n, n)).T for row in across]
-    copies = []
-
-    def send(slot, real, imag):
-        buffer[slot, 0] = real
-        buffer[slot, 1] = imag
-        copies.append(pltpu.make_async_copy(buffer.at[slot], out_ref.at[order_ref[slot]], sems.at[slot]))
-        copies[-1].start()
-
-    for slot in range(done, count):
-        k = order_ref[slot]
-        real = imag = jnp.zeros((n, n), jnp.float32)
-        for d, (matrix, rows) in enumerate(
-            ((plane_ref[slot - done], load_rows(plane_rows, slot - done)), (slab_ref[k], load_rows(slab_rows, k)))
-        ):
-            pair = scaled(matrix, 2.0 * (rows[0] + across[d] * rows[2]), 2.0 * (rows[1] + across[d] * rows[3]))
-            real, imag = real + pair[0], imag + pair[1]
-        send(slot, real - real.T, imag + imag.T)
-    for slot in range(done):
-        real, imag = parts_ref[slot, 0], parts_ref[slot, 1]
+
+    def copy_out(k):
+        return pltpu.make_async_copy(buffer.at[k], out_ref.at[k], sems.at[k])
+
+    @pl.loop(0, count)
+    def _(k):
+        real, imag = parts_ref[k, 0], parts_ref[k, 1]
         for d in range(2):
-            real = real + (parts_ref[slot, 2 + 4 * d] * across[d] - parts_ref[slot, 4 + 4 * d] * down[d])
-            imag = imag + (parts_ref[slot, 3 + 4 * d] * across[d] + parts_ref[slot, 5 + 4 * d] * down[d])
-        send(slot, real, imag)
-    for copy in copies:
-        copy.wait()
-
-
-def gradient_call(order, totals, parts, plane, plane_rows, slab, slab_rows, everything):
-    count, n, _ = slab.shape
+            real = real + (parts_ref[k, 2 + 4 * d] * across[d] - parts_ref[k, 4 + 4 * d] * down[d])
+            imag = imag + (parts_ref[k, 3 + 4 * d] * across[d] + parts_ref[k, 5 + 4 * d] * down[d])
+        buffer[k, 0] = real
+        buffer[k, 1] = imag
+        copy_out(k).start()
+
+    small_copy.wait()
+
+    @pl.loop(0, count)
+    def _(k):
+        copy_out(k).wait()
+
+
+def gradient_call(totals, parts, everything):
+    count, _, n, _ = parts.shape
     whole = pl.BlockSpec(memory_space=pltpu.VMEM)
     return pl.pallas_call(
         functools.partial(gradient_kernel, everything=everything),
-        in_specs=[pl.BlockSpec(memory_space=pltpu.SMEM)] + [whole] * 7,
-        out_specs=[pl.BlockSpec(memory_space=pl.ANY), whole],
+        in_specs=[whole] * 3,
+        out_specs=[pl.BlockSpec(memory_space=pl.ANY)] * 2,
         out_shape=[
             jax.ShapeDtypeStruct((count, 2, n, n), jnp.float32),
             jax.ShapeDtypeStruct((2, n), jnp.float32),
         ],
-        scratch_shapes=[pltpu.VMEM((count, 2, n, n), jnp.float32), pltpu.SemaphoreType.DMA((count,))],
+        scratch_shapes=[
+            pltpu.VMEM((count, 2, n, n), jnp.float32),
+            pltpu.VMEM((2, n), jnp.float32),
+            pltpu.SemaphoreType.DMA((count,)),
+            pltpu.SemaphoreType.DMA,
+        ],
         compiler_params=pltpu.CompilerParams(vmem_limit_bytes=VMEM),
         name="gradient",
-    )(order, *totals, parts, plane, plane_rows, slab, slab_rows)
+    )(*totals, parts)
 
 
 def shifted(value, axis, steps):
@@ -390,13 +439,11 @@
         return lax.ppermute(value, ("kxy", "kz"), pairs)
 
     value = value + swapped(value, 0, 1) + (swapped(value, 1, 0) + swapped(value, 1, 1))
-    distance = 2
-    while True:
-        other = swapped(value, distance, 0)
-        distance *= 2
-        if distance == count:
-            return value, other
-        value = value + other
+    distance = count // 2
+    while distance > 2:
+        value = value + swapped(value, distance, 1)
+        distance //= 2
+    return value, swapped(value, distance, 1)
 
 
 def body(start_rotation, correlations, neighbours):
@@ -415,18 +462,18 @@
     rotation, early = polar_call(start_rotation, 0, RAW, GROUP, [rotation], ())
     from_slab = [shifted(part, "kz", -1) for part in (early, late)]
     for_plane, for_slab = sandwich_call(rotation, correlations, GROUP)
-    plane, plane_rows, total = plane_call(order, for_plane, partners[0], 0, [], True)
+    total = jnp.zeros((8, rotation.shape[-1]), jnp.float32)
+    plane, plane_rows, total = plane_call(order, for_plane, partners[0], 0, total)
     slab, slab_rows, parts, total = slab_call(
         order, slab_slots, total, plane, plane_rows, for_slab, rotation, from_slab
     )
-    first = RAW
-    for partner in partners[1:-1]:
-        parts, total = middle_call(order, for_plane, partner, first, total, slab, slab_rows, parts)
-        first += partner.shape[0]
-    plane, plane_rows, total = plane_call(order, for_plane, partners[-1], first, [total], False)
-    gradient, centres = gradient_call(
-        order, reduce_parts(total), parts, plane, plane_rows, slab, slab_rows, everything
-    )
+    parts, total, for_last = middle_call(
+        order, for_plane, partners[1], RAW, total, slab, slab_rows, parts, CHUNKS[-1]
+    )
+    plane, plane_rows, total = last_call(for_last, partners[2], total)
+    totals = reduce_parts(total)
+    parts = combine_call(order, plane, plane_rows, slab, slab_rows, parts, count - CHUNKS[-1])
+    gradient, centres = gradient_call(totals, parts, everything)
     return (rotation, gradient, centres)
 
 

time: 69.4 us -> 65.3 us (0.941)
  waiting for transfers between devices: 18.4 us -> 14.3 us
  local copies, waits for them, and re-layouts: 5.37 us -> 3.79 us
  Pallas kernels: 32.7 us -> 34.2 us
    ppermute x5, waiting for transfers between devices: 11.5 us -> 9.36 us  [shifted(): lax.ppermute(value, axis, [(source, (source + steps) % count) for source...]
    pallas_call x1, Pallas kernels: 3.71 us -> 1.59 us  [gradient_call(): pl.pallas_call(functools.partial(gradient_kernel, everything=everything),...]
    pallas_call x2, Pallas kernels: 12.8 us -> 14.8 us  [polar_call(): pl.pallas_call(functools.partial(polar_kernel, carried=len(carried), chun...]
    ppermute x5, waiting for transfers between devices: 6.89 us -> 4.93 us  [swapped(): return lax.ppermute(value, ('kxy', 'kz'), pairs)]
    unnamed x10 -> x8, local copies, waits for them, and re-layouts: 5.37 us -> 3.78 us
    pallas_call x1, Pallas kernels: 0.08 us -> 1.24 us  [take_call(): pl.pallas_call(take_kernel, in_specs=[pl.BlockSpec(memory_space=pltpu.HBM...]
    pallas_call x2 -> x3, Pallas kernels: 7.4 us -> 7.68 us  [the longest x1 6.53 us: plane_call(): pl.pallas_call(functools.partial(plane_kernel, first=first), in_specs=[pl...]
  transfers between devices with their start and end apart: 10 -> 10, of which waited for: 7 -> 7; matrix products, arithmetic and copies ran while one was open for 0% -> 0% of each run, Pallas kernels for 41% -> 48%
where the time goes in v3:
time: 65.3 us; the launch traced here: 65 us
  Pallas kernels  34.2 us (52%)
  waiting for transfers between devices  14.3 us (22%)
  starting transfers between devices  11.7 us (18%)
  local copies, waits for them, and re-layouts  3.79 us (6%)
  between operations  0.9 us (1%)
    pallas_call x2, Pallas kernels, polar_call(): pl.pallas_call(functools.partial(polar_kernel, carried=len(carried), chun...  14.8 us
    ppermute x5, waiting for transfers between devices, shifted(): lax.ppermute(value, axis, [(source, (source + steps) % count) for source...  9.36 us
    pallas_call x1, Pallas kernels, plane_call(): pl.pallas_call(functools.partial(plane_kernel, first=first), in_specs=[pl...  6.53 us
    ppermute x5, starting transfers between devices, shifted(): lax.ppermute(value, axis, [(source, (source + steps) % count) for source...  6.52 us
    ppermute x5, starting transfers between devices, swapped(): return lax.ppermute(value, ('kxy', 'kz'), pairs)  5.14 us
    ppermute x5, waiting for transfers between devices, swapped(): return lax.ppermute(value, ('kxy', 'kz'), pairs)  4.93 us
    pallas_call x1, Pallas kernels, slab_call(): pl.pallas_call(functools.partial(slab_kernel, pieces=len(pieces)), in_spe...  4.05 us
    unnamed x8, local copies, waits for them, and re-layouts  3.78 us
  transfers between devices with their start and end apart: 10, of which 7 were waited for; matrix products, arithmetic and copies ran while one was open for 0% of the time, Pallas kernels for 48%

profile of v3, /device:TPU:0, one launch (start us, length us, event | category | flops | bytes accessed | tf_op | source)
XLA Modules:
  0.0 65.0 jit_solution(9234683925890543781)
XLA Ops:
  0.6 1.2 %take.1 = f32[8,2,128,128]{3,2,1,0:T(8,128)S(1)} custom-call(f32[16,2,128,128]{3,2,1,0:T(8,128)} %start_ref.5), custom_call_target="tpu_custom_call" | custom-call | tf_op jit(solution)/shard_map/take/pallas_call | solution.py:114
  1.9 5.1 %collective-permute-start.1 = (f32[8,2,128,128]{3,2,1,0:T(8,128)S(1)}, f32[8,2,128,128]{3,2,1,0:T(8,128)}, u32[]{:S(2)}, u32[]{:S(2)}) collective-permute-start(f32[8,2,128,128]{3,2,1,0:T(8,128)S(1)} %take.1), channel_id=1, source_target_pairs={{0,12},{2,14},{4,0},{6,2},{8,4},{10,6},{12,8},{14,10},{1,13},{3,15... | collective-permute-start | bytes 3145736 | tf_op jit(solution)/shard_map/ppermute | solution.py:429
  7.0 7.6 %polar.2 = (f32[16,2,128,128]{3,2,1,0:T(8,128)}, f32[8,2,128,128]{3,2,1,0:T(8,128)}, f32[6,2,128,128]{3,2,1,0:T(8,128)}, f32[2,2,128,128]{3,2,1,0:T(8,128)}) custom-call(f32[16,2,128,128]{3,2,1,0:T(8,128)} %start_ref.5), custom_call_target="tpu_custom_call" | custom-call | tf_op jit(solution)/shard_map/polar/pallas_call | solution.py:94
  14.6 7.2 %polar.3 = (f32[16,2,128,128]{3,2,1,0:T(8,128)}, f32[8,2,128,128]{3,2,1,0:T(8,128)}) custom-call(f32[16,2,128,128]{3,2,1,0:T(8,128)} %start_ref.5, f32[16,2,128,128]{3,2,1,0:T(8,128)} %get-tuple-element.26.refs_0_), custom_call_target="tpu_custom_call", output_to_operand_aliasing={{0}: (1, {})} | custom-call | tf_op jit(solution)/shard_map/polar/pallas_call | solution.py:94
  21.8 0.5 collective-permute-start.3
  22.8 0.5 collective-permute-start.4
  23.4 1.6 %copy-done = f32[16,2,128,128]{3,2,1,0:T(8,128)S(1)} copy-done((f32[16,2,128,128]{3,2,1,0:T(8,128)S(1)}, f32[16,2,128,128]{3,2,1,0:T(8,128)}, u32[]{:S(2)}) %copy-start) | copy-done | bytes 2097176
  24.9 2.2 %copy-done.2 = f32[16,2,2,128,128]{4,3,2,1,0:T(8,128)S(1)} copy-done((f32[16,2,2,128,128]{4,3,2,1,0:T(8,128)S(1)}, f32[16,2,2,128,128]{4,3,2,1,0:T(8,128)}, u32[]{:S(2)}) %copy-start.2) | copy-done | bytes 4194328
  27.1 2.5 %sandwich.1 = (f32[16,128,256]{2,1,0:T(8,128)S(1)}, f32[16,128,256]{2,1,0:T(8,128)S(1)}) custom-call(f32[16,2,128,128]{3,2,1,0:T(8,128)S(1)} %copy-done, f32[16,2,2,128,128]{4,3,2,1,0:T(8,128)S(1)} %copy-done.2), custom_call_target="tpu_custom_call" | custom-call | tf_op jit(solution)/shard_map/sandwich/pallas_call | solution.py:135
  29.7 0.8 %collective-permute-done.1.partner_ref = f32[8,2,128,128]{3,2,1,0:T(8,128)} collective-permute-done((f32[8,2,128,128]{3,2,1,0:T(8,128)S(1)}, f32[8,2,128,128]{3,2,1,0:T(8,128)}, u32[]{:S(2)}, u32[]{:S(2)}) %collective-permute-start.1) | collective-permute-done | bytes 1048608 | tf_op jit(solution)/shard_map/ppermute | solution.py:429
  30.5 6.5 %plane.1 = (f32[8,128,256]{2,1,0:T(8,128)S(1)}, f32[8,8,128]{2,1,0:T(8,128)S(1)}, f32[8,128]{1,0:T(8,128)S(1)}) custom-call(s32[16]{0:T(128)S(1)} %select_reduce_fusion.order_ref, f32[16,128,256]{2,1,0:T(8,128)S(1)} %get-tuple-element.28.sandwich_ref, f32[8,2,128,128]{3,2,1,0:T(8,128)} %collective-permute-done.1.partner_ref, ...), custom_call_target="tpu_custom_call" | custom-call | tf_op jit(solution)/shard_map/plane/pallas_call | solution.py:280
  37.1 4.0 %slab.1 = (f32[16,128,256]{2,1,0:T(8,128)S(1)}, f32[16,8,128]{2,1,0:T(8,128)S(1)}, f32[16,10,128,128]{3,2,1,0:T(8,128)S(1)}, f32[8,128]{1,0:T(8,128)S(1)}) custom-call(s32[16]{0:T(128)S(1)} %select_reduce_fusion.order_ref, s32[16]{0:T(128)S(1)} %fusion.slots_ref, f32[8,128]{1,0:T(8,128)S(1)} %get-tuple-element.30.before_ref, ...), custom_call_target="tpu_custom_call" | custom-call | tf_op jit(solution)/shard_map/slab/pallas_call | solution.py:234
  41.2 6.3 %collective-permute-done.partner_ref = f32[6,2,128,128]{3,2,1,0:T(8,128)} collective-permute-done((f32[6,2,128,128]{3,2,1,0:T(8,128)}, f32[6,2,128,128]{3,2,1,0:T(8,128)}, u32[]{:S(2)}, u32[]{:S(2)}) %collective-permute-start) | collective-permute-done | bytes 786464 | tf_op jit(solution)/shard_map/ppermute | solution.py:429
  47.5 2.3 %middle.1 = (f32[16,10,128,128]{3,2,1,0:T(8,128)S(1)}, f32[8,128]{1,0:T(8,128)S(1)}, f32[2,128,256]{2,1,0:T(8,128)S(1)}) custom-call(s32[16]{0:T(128)S(1)} %select_reduce_fusion.order_ref, f32[16,128,256]{2,1,0:T(8,128)S(1)} %get-tuple-element.28.sandwich_ref, f32[6,2,128,128]{3,2,1,0:T(8,128)} %collective-permute-done.partner_ref, ...), custom_call_target="tpu_custom_call", output_to_operand_aliasing={{0}: (6, {})} | custom-call | tf_op jit(solution)/shard_map/middle/pallas_call | solution.py:313
  49.8 2.2 %collective-permute-done.4.partner_ref = f32[2,2,128,128]{3,2,1,0:T(8,128)S(1)} collective-permute-done((f32[2,2,128,128]{3,2,1,0:T(8,128)}, f32[2,2,128,128]{3,2,1,0:T(8,128)S(1)}, u32[]{:S(2)}, u32[]{:S(2)}) %collective-permute-start.4) | collective-permute-done | bytes 262176 | tf_op jit(solution)/shard_map/ppermute | solution.py:429
  52.4 1.5 %collective-permute-start.6 = (f32[8,128]{1,0:T(8,128)S(1)}, f32[8,128]{1,0:T(8,128)S(1)}, u32[]{:S(2)}, u32[]{:S(2)}) collective-permute-start(f32[8,128]{1,0:T(8,128)S(1)} %get-tuple-element.43), channel_id=1, source_target_pairs={{0,2},{1,3},{2,0},{3,1},{4,6},{5,7},{6,4},{7,5},{8,10},{9,11},{10,... | collective-permute-start | bytes 12296 | tf_op jit(solution)/shard_map/ppermute | solution.py:439
  54.2 1.2 %collective-permute-done.7 = f32[8,128]{1,0:T(8,128)S(1)} collective-permute-done((f32[8,128]{1,0:T(8,128)S(1)}, f32[8,128]{1,0:T(8,128)S(1)}, u32[]{:S(2)}, u32[]{:S(2)}) %collective-permute-start.7) | collective-permute-done | bytes 4128 | tf_op jit(solution)/shard_map/ppermute | solution.py:439
  55.4 0.7 %collective-permute-done.6 = f32[8,128]{1,0:T(8,128)S(1)} collective-permute-done((f32[8,128]{1,0:T(8,128)S(1)}, f32[8,128]{1,0:T(8,128)S(1)}, u32[]{:S(2)}, u32[]{:S(2)}) %collective-permute-start.6) | collective-permute-done | bytes 4128 | tf_op jit(solution)/shard_map/ppermute | solution.py:439
  56.1 1.4 %collective-permute-start.8 = (f32[8,128]{1,0:T(8,128)S(1)}, f32[8,128]{1,0:T(8,128)S(1)}, u32[]{:S(2)}, u32[]{:S(2)}) collective-permute-start(f32[8,128]{1,0:T(8,128)S(1)} %add_add_fusion), channel_id=1, source_target_pairs={{0,9},{1,8},{2,11},{3,10},{4,13},{5,12},{6,15},{7,14},{8,1},{9,0},... | collective-permute-start | bytes 12296 | tf_op jit(solution)/shard_map/ppermute | solution.py:439
  57.5 2.6 %collective-permute-done.8 = f32[8,128]{1,0:T(8,128)S(1)} collective-permute-done((f32[8,128]{1,0:T(8,128)S(1)}, f32[8,128]{1,0:T(8,128)S(1)}, u32[]{:S(2)}, u32[]{:S(2)}) %collective-permute-start.8) | collective-permute-done | bytes 4128 | tf_op jit(solution)/shard_map/ppermute | solution.py:439
  60.1 1.8 %collective-permute-start.9 = (f32[8,128]{1,0:T(8,128)S(1)}, f32[8,128]{1,0:T(8,128)S(1)}, u32[]{:S(2)}, u32[]{:S(2)}) collective-permute-start(f32[8,128]{1,0:T(8,128)S(1)} %add.37.first_ref), channel_id=1, source_target_pairs={{0,5},{1,4},{2,7},{3,6},{4,1},{5,0},{6,3},{7,2},{8,13},{9,12},{10,... | collective-permute-start | bytes 12296 | tf_op jit(solution)/shard_map/ppermute | solution.py:439
  61.9 0.8 %combine.1.parts_ref = f32[16,10,128,128]{3,2,1,0:T(8,128)S(1)} custom-call(s32[16]{0:T(128)S(1)} %select_reduce_fusion.order_ref, f32[2,128,256]{2,1,0:T(8,128)S(1)} %get-tuple-element.44.plane_ref, f32[2,8,128]{2,1,0:T(8,128)S(1)} %get-tuple-element.45.plane_rows, f32[16,128,256]{2,1,0:T(8,128)S(1)} %get-tuple-element.37.slab_ref, ...), custom_call_target="tpu_custom_call", output_to_operand_aliasing={{}: (5, {})} | custom-call | tf_op jit(solution)/shard_map/combine/pallas_call | solution.py:365
  62.7 0.5 collective-permute-done.9.second_ref
  63.2 1.6 %gradient.1 = (f32[16,2,128,128]{3,2,1,0:T(8,128)}, f32[2,128]{1,0:T(2,128)}) custom-call(f32[8,128]{1,0:T(8,128)S(1)} %add.37.first_ref, f32[8,128]{1,0:T(8,128)S(1)} %collective-permute-done.9.second_ref, f32[16,10,128,128]{3,2,1,0:T(8,128)S(1)} %combine.1.parts_ref), custom_call_target="tpu_custom_call" | custom-call | tf_op jit(solution)/shard_map/gradient/pallas_call | solution.py:408
  (20 shorter events, 1.3 us)
Async XLA Ops:
  1.9 28.7 %collective-permute-start.1 = (f32[8,2,128,128]{3,2,1,0:T(8,128)S(1)}, f32[8,2,128,128]{3,2,1,0:T(8,128)}, u32[]{:S(2)}, u32[]{:S(2)}) collective-permute-start(f32[8,2,128,128]{3,2,1,0:T(8,128)S(1)} %take.1), channel_id=1, source_target_pairs={{0,12},{2,14},{4,0},{6,2},{8,4},{10,6},{12,8},{14,10},{1,13},{3,15... | collective-permute-start | bytes 3145736 | tf_op jit(solution)/shard_map/ppermute | solution.py:429
  14.6 8.7 %copy-start.3 = (s32[16,2]{0,1:T(2,128)S(1)}, s32[16,2]{0,1:T(2,128)}, u32[]{:S(2)}) copy-start(s32[16,2]{0,1:T(2,128)} %param.5) | copy-start | bytes 388
  21.8 15.2 %collective-permute-start.2 = (f32[8,2,128,128]{3,2,1,0:T(8,128)}, f32[8,2,128,128]{3,2,1,0:T(8,128)S(1)}, u32[]{:S(2)}, u32[]{:S(2)}) collective-permute-start(f32[8,2,128,128]{3,2,1,0:T(8,128)} %get-tuple-element.34), channel_id=1, source_target_pairs={{0,1},{1,0},{2,3},{3,2},{4,5},{5,4},{6,7},{7,6},{8,9},{9,8},{10,11... | collective-permute-start | bytes 3145736 | tf_op jit(solution)/shard_map/ppermute | solution.py:429
  21.8 15.3 %collective-permute-start.3 = (f32[8,2,128,128]{3,2,1,0:T(8,128)}, f32[8,2,128,128]{3,2,1,0:T(8,128)S(1)}, u32[]{:S(2)}, u32[]{:S(2)}) collective-permute-start(f32[8,2,128,128]{3,2,1,0:T(8,128)} %get-tuple-element.35), channel_id=1, source_target_pairs={{0,1},{1,0},{2,3},{3,2},{4,5},{5,4},{6,7},{7,6},{8,9},{9,8},{10,11... | collective-permute-start | bytes 3145736 | tf_op jit(solution)/shard_map/ppermute | solution.py:429
  22.3 25.2 %collective-permute-start = (f32[6,2,128,128]{3,2,1,0:T(8,128)}, f32[6,2,128,128]{3,2,1,0:T(8,128)}, u32[]{:S(2)}, u32[]{:S(2)}) collective-permute-start(f32[6,2,128,128]{3,2,1,0:T(8,128)} %get-tuple-element.29), channel_id=1, source_target_pairs={{0,12},{2,14},{4,0},{6,2},{8,4},{10,6},{12,8},{14,10},{1,13},{3,15... | collective-permute-start | bytes 2359304 | tf_op jit(solution)/shard_map/ppermute | solution.py:429
  22.8 29.2 %collective-permute-start.4 = (f32[2,2,128,128]{3,2,1,0:T(8,128)}, f32[2,2,128,128]{3,2,1,0:T(8,128)S(1)}, u32[]{:S(2)}, u32[]{:S(2)}) collective-permute-start(f32[2,2,128,128]{3,2,1,0:T(8,128)} %get-tuple-element.41), channel_id=1, source_target_pairs={{0,12},{2,14},{4,0},{6,2},{8,4},{10,6},{12,8},{14,10},{1,13},{3,15... | collective-permute-start | bytes 786440 | tf_op jit(solution)/shard_map/ppermute | solution.py:429
  23.4 1.6 %copy-start = (f32[16,2,128,128]{3,2,1,0:T(8,128)S(1)}, f32[16,2,128,128]{3,2,1,0:T(8,128)}, u32[]{:S(2)}) copy-start(f32[16,2,128,128]{3,2,1,0:T(8,128)} %get-tuple-element.23.rotation_ref.own_ref) | copy-start | bytes 6291460
  24.9 2.2 %copy-start.2 = (f32[16,2,2,128,128]{4,3,2,1,0:T(8,128)S(1)}, f32[16,2,2,128,128]{4,3,2,1,0:T(8,128)}, u32[]{:S(2)}) copy-start(f32[16,2,2,128,128]{4,3,2,1,0:T(8,128)} %correlation_ref.1) | copy-start | bytes 12582916
  29.7 7.4 %copy-start.1 = (f32[16,2,128,128]{3,2,1,0:T(8,128)S(1)}, f32[16,2,128,128]{3,2,1,0:T(8,128)}, u32[]{:S(2)}) copy-start(f32[16,2,128,128]{3,2,1,0:T(8,128)} %get-tuple-element.23.rotation_ref.own_ref) | copy-start | bytes 6291460
  52.3 3.1 %collective-permute-start.7 = (f32[8,128]{1,0:T(8,128)S(1)}, f32[8,128]{1,0:T(8,128)S(1)}, u32[]{:S(2)}, u32[]{:S(2)}) collective-permute-start(f32[8,128]{1,0:T(8,128)S(1)} %get-tuple-element.43), channel_id=1, source_target_pairs={{0,3},{1,2},{2,1},{3,0},{4,7},{5,6},{6,5},{7,4},{8,11},{9,10},{10,... | collective-permute-start | bytes 12296 | tf_op jit(solution)/shard_map/ppermute | solution.py:439
  52.4 3.6 %collective-permute-start.6 = (f32[8,128]{1,0:T(8,128)S(1)}, f32[8,128]{1,0:T(8,128)S(1)}, u32[]{:S(2)}, u32[]{:S(2)}) collective-permute-start(f32[8,128]{1,0:T(8,128)S(1)} %get-tuple-element.43), channel_id=1, source_target_pairs={{0,2},{1,3},{2,0},{3,1},{4,6},{5,7},{6,4},{7,5},{8,10},{9,11},{10,... | collective-permute-start | bytes 12296 | tf_op jit(solution)/shard_map/ppermute | solution.py:439
  53.9 2.1 %collective-permute-start.5 = (f32[8,128]{1,0:T(8,128)S(1)}, f32[8,128]{1,0:T(8,128)S(1)}, u32[]{:S(2)}, u32[]{:S(2)}) collective-permute-start(f32[8,128]{1,0:T(8,128)S(1)} %get-tuple-element.43), channel_id=1, source_target_pairs={{0,1},{1,0},{2,3},{3,2},{4,5},{5,4},{6,7},{7,6},{8,9},{9,8},{10,11... | collective-permute-start | bytes 12296 | tf_op jit(solution)/shard_map/ppermute | solution.py:439
  56.1 4.0 %collective-permute-start.8 = (f32[8,128]{1,0:T(8,128)S(1)}, f32[8,128]{1,0:T(8,128)S(1)}, u32[]{:S(2)}, u32[]{:S(2)}) collective-permute-start(f32[8,128]{1,0:T(8,128)S(1)} %add_add_fusion), channel_id=1, source_target_pairs={{0,9},{1,8},{2,11},{3,10},{4,13},{5,12},{6,15},{7,14},{8,1},{9,0},... | collective-permute-start | bytes 12296 | tf_op jit(solution)/shard_map/ppermute | solution.py:439
  60.1 3.1 %collective-permute-start.9 = (f32[8,128]{1,0:T(8,128)S(1)}, f32[8,128]{1,0:T(8,128)S(1)}, u32[]{:S(2)}, u32[]{:S(2)}) collective-permute-start(f32[8,128]{1,0:T(8,128)S(1)} %add.37.first_ref), channel_id=1, source_target_pairs={{0,5},{1,4},{2,7},{3,6},{4,1},{5,0},{6,3},{7,2},{8,13},{9,12},{10,... | collective-permute-start | bytes 12296 | tf_op jit(solution)/shard_map/ppermute | solution.py:439

commit v4 on v3

--- a/solution.py
+++ b/solution.py
@@ -239,7 +239,7 @@
             jax.ShapeDtypeStruct((count, n, 2 * n), jnp.float32),
             jax.ShapeDtypeStruct((count, 8, n), jnp.float32),
             jax.ShapeDtypeStruct((count, 10, n, n), jnp.float32),
-            jax.ShapeDtypeStruct((8, n), jnp.float32),
+            jax.ShapeDtypeStruct((2, n), jnp.float32),
         ],
         scratch_shapes=[pltpu.VMEM(own.shape, own.dtype)],
         compiler_params=pltpu.CompilerParams(vmem_limit_bytes=VMEM),
@@ -284,7 +284,7 @@
         out_shape=[
             jax.ShapeDtypeStruct((size, n, 2 * n), jnp.float32),
             jax.ShapeDtypeStruct((size, 8, n), jnp.float32),
-            jax.ShapeDtypeStruct((8, n), jnp.float32),
+            jax.ShapeDtypeStruct((2, n), jnp.float32),
         ],
         compiler_params=pltpu.CompilerParams(vmem_limit_bytes=VMEM),
         name="plane",
@@ -375,7 +375,7 @@
 
 def gradient_kernel(first_ref, second_ref, parts_ref, out_ref, centres_ref, buffer, small, sems, small_sem, *, everything):
     count, _, n, _ = buffer.shape
-    centres = (first_ref[0:2] + second_ref[0:2]) / (-2.0 * everything)
+    centres = (first_ref[...] + second_ref[...]) / (-2.0 * everything)
     small[...] = centres
     small_copy = pltpu.make_async_copy(small, centres_ref, small_sem)
     small_copy.start()
@@ -462,7 +462,7 @@
     rotation, early = polar_call(start_rotation, 0, RAW, GROUP, [rotation], ())
     from_slab = [shifted(part, "kz", -1) for part in (early, late)]
     for_plane, for_slab = sandwich_call(rotation, correlations, GROUP)
-    total = jnp.zeros((8, rotation.shape[-1]), jnp.float32)
+    total = jnp.zeros((2, rotation.shape[-1]), jnp.float32)
     plane, plane_rows, total = plane_call(order, for_plane, partners[0], 0, total)
     slab, slab_rows, parts, total = slab_call(
         order, slab_slots, total, plane, plane_rows, for_slab, rotation, from_slab

time: 65.3 us -> 65.2 us (level)
    pallas_call x1, Pallas kernels: 4.05 us -> 4.73 us  [slab_call(): pl.pallas_call(functools.partial(slab_kernel, pieces=len(pieces)), in_spe...]
    pallas_call x1, Pallas kernels: 6.53 us -> 5.84 us  [plane_call(): pl.pallas_call(functools.partial(plane_kernel, first=first), in_specs=[pl...]
where the time goes in v4:
time: 65.2 us; the launch traced here: 64.9 us
  Pallas kernels  34.2 us (52%)
  waiting for transfers between devices  14.2 us (22%)
  starting transfers between devices  11.7 us (18%)
  local copies, waits for them, and re-layouts  3.79 us (6%)
  between operations  0.9 us (1%)
    pallas_call x2, Pallas kernels, polar_call(): pl.pallas_call(functools.partial(polar_kernel, carried=len(carried), chun...  14.8 us
    ppermute x5, waiting for transfers between devices, shifted(): lax.ppermute(value, axis, [(source, (source + steps) % count) for source...  9.39 us
    ppermute x5, starting transfers between devices, shifted(): lax.ppermute(value, axis, [(source, (source + steps) % count) for source...  6.52 us
    pallas_call x1, Pallas kernels, plane_call(): pl.pallas_call(functools.partial(plane_kernel, first=first), in_specs=[pl...  5.84 us
    ppermute x5, starting transfers between devices, swapped(): return lax.ppermute(value, ('kxy', 'kz'), pairs)  5.14 us
    ppermute x5, waiting for transfers between devices, swapped(): return lax.ppermute(value, ('kxy', 'kz'), pairs)  4.82 us
    pallas_call x1, Pallas kernels, slab_call(): pl.pallas_call(functools.partial(slab_kernel, pieces=len(pieces)), in_spe...  4.73 us
    unnamed x8, local copies, waits for them, and re-layouts  3.78 us
  transfers between devices with their start and end apart: 10, of which 7 were waited for; matrix products, arithmetic and copies ran while one was open for 0% of the time, Pallas kernels for 48%

profile of v4, /device:TPU:0, one launch (start us, length us, event | category | flops | bytes accessed | tf_op | source)
XLA Modules:
  0.0 64.9 jit_solution(8192072317709097872)
XLA Ops:
  0.6 1.2 %take.1 = f32[8,2,128,128]{3,2,1,0:T(8,128)S(1)} custom-call(f32[16,2,128,128]{3,2,1,0:T(8,128)} %start_ref.5), custom_call_target="tpu_custom_call" | custom-call | tf_op jit(solution)/shard_map/take/pallas_call | solution.py:114
  1.9 5.1 %collective-permute-start.1 = (f32[8,2,128,128]{3,2,1,0:T(8,128)S(1)}, f32[8,2,128,128]{3,2,1,0:T(8,128)S(1)}, u32[]{:S(2)}, u32[]{:S(2)}) collective-permute-start(f32[8,2,128,128]{3,2,1,0:T(8,128)S(1)} %take.1), channel_id=1, source_target_pairs={{0,12},{2,14},{4,0},{6,2},{8,4},{10,6},{12,8},{14,10},{1,13},{3,15... | collective-permute-start | bytes 3145736 | tf_op jit(solution)/shard_map/ppermute | solution.py:429
  7.0 7.6 %polar.2 = (f32[16,2,128,128]{3,2,1,0:T(8,128)}, f32[8,2,128,128]{3,2,1,0:T(8,128)}, f32[6,2,128,128]{3,2,1,0:T(8,128)}, f32[2,2,128,128]{3,2,1,0:T(8,128)}) custom-call(f32[16,2,128,128]{3,2,1,0:T(8,128)} %start_ref.5), custom_call_target="tpu_custom_call" | custom-call | tf_op jit(solution)/shard_map/polar/pallas_call | solution.py:94
  14.6 7.2 %polar.3 = (f32[16,2,128,128]{3,2,1,0:T(8,128)}, f32[8,2,128,128]{3,2,1,0:T(8,128)}) custom-call(f32[16,2,128,128]{3,2,1,0:T(8,128)} %start_ref.5, f32[16,2,128,128]{3,2,1,0:T(8,128)} %get-tuple-element.26.refs_0_), custom_call_target="tpu_custom_call", output_to_operand_aliasing={{0}: (1, {})} | custom-call | tf_op jit(solution)/shard_map/polar/pallas_call | solution.py:94
  21.8 0.5 collective-permute-start.3
  22.8 0.5 collective-permute-start.4
  23.3 1.6 %copy-done = f32[16,2,128,128]{3,2,1,0:T(8,128)S(1)} copy-done((f32[16,2,128,128]{3,2,1,0:T(8,128)S(1)}, f32[16,2,128,128]{3,2,1,0:T(8,128)}, u32[]{:S(2)}) %copy-start) | copy-done | bytes 2097176
  24.9 2.2 %copy-done.2 = f32[16,2,2,128,128]{4,3,2,1,0:T(8,128)S(1)} copy-done((f32[16,2,2,128,128]{4,3,2,1,0:T(8,128)S(1)}, f32[16,2,2,128,128]{4,3,2,1,0:T(8,128)}, u32[]{:S(2)}) %copy-start.2) | copy-done | bytes 4194328
  27.1 2.5 %sandwich.1 = (f32[16,128,256]{2,1,0:T(8,128)S(1)}, f32[16,128,256]{2,1,0:T(8,128)S(1)}) custom-call(f32[16,2,128,128]{3,2,1,0:T(8,128)S(1)} %copy-done, f32[16,2,2,128,128]{4,3,2,1,0:T(8,128)S(1)} %copy-done.2), custom_call_target="tpu_custom_call" | custom-call | tf_op jit(solution)/shard_map/sandwich/pallas_call | solution.py:135
  29.7 0.9 %collective-permute-done.1.partner_ref = f32[8,2,128,128]{3,2,1,0:T(8,128)S(1)} collective-permute-done((f32[8,2,128,128]{3,2,1,0:T(8,128)S(1)}, f32[8,2,128,128]{3,2,1,0:T(8,128)S(1)}, u32[]{:S(2)}, u32[]{:S(2)}) %collective-permute-start.1) | collective-permute-done | bytes 1048608 | tf_op jit(solution)/shard_map/ppermute | solution.py:429
  30.5 5.8 %plane.1 = (f32[8,128,256]{2,1,0:T(8,128)S(1)}, f32[8,8,128]{2,1,0:T(8,128)S(1)}, f32[2,128]{1,0:T(2,128)S(1)}) custom-call(s32[16]{0:T(128)S(1)} %select_reduce_fusion.order_ref, f32[16,128,256]{2,1,0:T(8,128)S(1)} %get-tuple-element.28.sandwich_ref, f32[8,2,128,128]{3,2,1,0:T(8,128)S(1)} %collective-permute-done.1.partner_ref, ...), custom_call_target="tpu_custom_call" | custom-call | tf_op jit(solution)/shard_map/plane/pallas_call | solution.py:280
  36.4 4.7 %slab.1 = (f32[16,128,256]{2,1,0:T(8,128)S(1)}, f32[16,8,128]{2,1,0:T(8,128)S(1)}, f32[16,10,128,128]{3,2,1,0:T(8,128)S(1)}, f32[2,128]{1,0:T(2,128)S(1)}) custom-call(s32[16]{0:T(128)S(1)} %select_reduce_fusion.order_ref, s32[16]{0:T(128)S(1)} %fusion.slots_ref, f32[2,128]{1,0:T(2,128)S(1)} %get-tuple-element.30.before_ref, ...), custom_call_target="tpu_custom_call" | custom-call | tf_op jit(solution)/shard_map/slab/pallas_call | solution.py:234
  41.2 6.3 %collective-permute-done.partner_ref = f32[6,2,128,128]{3,2,1,0:T(8,128)} collective-permute-done((f32[6,2,128,128]{3,2,1,0:T(8,128)}, f32[6,2,128,128]{3,2,1,0:T(8,128)}, u32[]{:S(2)}, u32[]{:S(2)}) %collective-permute-start) | collective-permute-done | bytes 786464 | tf_op jit(solution)/shard_map/ppermute | solution.py:429
  47.5 2.3 %middle.1 = (f32[16,10,128,128]{3,2,1,0:T(8,128)S(1)}, f32[2,128]{1,0:T(2,128)S(1)}, f32[2,128,256]{2,1,0:T(8,128)S(1)}) custom-call(s32[16]{0:T(128)S(1)} %select_reduce_fusion.order_ref, f32[16,128,256]{2,1,0:T(8,128)S(1)} %get-tuple-element.28.sandwich_ref, f32[6,2,128,128]{3,2,1,0:T(8,128)} %collective-permute-done.partner_ref, ...), custom_call_target="tpu_custom_call", output_to_operand_aliasing={{0}: (6, {})} | custom-call | tf_op jit(solution)/shard_map/middle/pallas_call | solution.py:313
  49.8 2.2 %collective-permute-done.4.partner_ref = f32[2,2,128,128]{3,2,1,0:T(8,128)S(1)} collective-permute-done((f32[2,2,128,128]{3,2,1,0:T(8,128)}, f32[2,2,128,128]{3,2,1,0:T(8,128)S(1)}, u32[]{:S(2)}, u32[]{:S(2)}) %collective-permute-start.4) | collective-permute-done | bytes 262176 | tf_op jit(solution)/shard_map/ppermute | solution.py:429
  52.4 1.5 %collective-permute-start.6 = (f32[2,128]{1,0:T(2,128)S(1)}, f32[2,128]{1,0:T(2,128)S(1)}, u32[]{:S(2)}, u32[]{:S(2)}) collective-permute-start(f32[2,128]{1,0:T(2,128)S(1)} %get-tuple-element.43), channel_id=1, source_target_pairs={{0,2},{1,3},{2,0},{3,1},{4,6},{5,7},{6,4},{7,5},{8,10},{9,11},{10,... | collective-permute-start | bytes 3080 | tf_op jit(solution)/shard_map/ppermute | solution.py:439
  54.2 1.1 %collective-permute-done.7 = f32[2,128]{1,0:T(2,128)S(1)} collective-permute-done((f32[2,128]{1,0:T(2,128)S(1)}, f32[2,128]{1,0:T(2,128)S(1)}, u32[]{:S(2)}, u32[]{:S(2)}) %collective-permute-start.7) | collective-permute-done | bytes 1056 | tf_op jit(solution)/shard_map/ppermute | solution.py:439
  55.4 0.7 %collective-permute-done.6 = f32[2,128]{1,0:T(2,128)S(1)} collective-permute-done((f32[2,128]{1,0:T(2,128)S(1)}, f32[2,128]{1,0:T(2,128)S(1)}, u32[]{:S(2)}, u32[]{:S(2)}) %collective-permute-start.6) | collective-permute-done | bytes 1056 | tf_op jit(solution)/shard_map/ppermute | solution.py:439
  56.0 1.4 %collective-permute-start.8 = (f32[2,128]{1,0:T(2,128)S(1)}, f32[2,128]{1,0:T(2,128)S(1)}, u32[]{:S(2)}, u32[]{:S(2)}) collective-permute-start(f32[2,128]{1,0:T(2,128)S(1)} %add_add_fusion), channel_id=1, source_target_pairs={{0,9},{1,8},{2,11},{3,10},{4,13},{5,12},{6,15},{7,14},{8,1},{9,0},... | collective-permute-start | bytes 3080 | tf_op jit(solution)/shard_map/ppermute | solution.py:439
  57.4 2.6 %collective-permute-done.8 = f32[2,128]{1,0:T(2,128)S(1)} collective-permute-done((f32[2,128]{1,0:T(2,128)S(1)}, f32[2,128]{1,0:T(2,128)S(1)}, u32[]{:S(2)}, u32[]{:S(2)}) %collective-permute-start.8) | collective-permute-done | bytes 1056 | tf_op jit(solution)/shard_map/ppermute | solution.py:439
  60.0 1.8 %collective-permute-start.9 = (f32[2,128]{1,0:T(2,128)S(1)}, f32[2,128]{1,0:T(2,128)S(1)}, u32[]{:S(2)}, u32[]{:S(2)}) collective-permute-start(f32[2,128]{1,0:T(2,128)S(1)} %add.37.first_ref), channel_id=1, source_target_pairs={{0,5},{1,4},{2,7},{3,6},{4,1},{5,0},{6,3},{7,2},{8,13},{9,12},{10,... | collective-permute-start | bytes 3080 | tf_op jit(solution)/shard_map/ppermute | solution.py:439
  61.8 0.8 %combine.1.parts_ref = f32[16,10,128,128]{3,2,1,0:T(8,128)S(1)} custom-call(s32[16]{0:T(128)S(1)} %select_reduce_fusion.order_ref, f32[2,128,256]{2,1,0:T(8,128)S(1)} %get-tuple-element.44.plane_ref, f32[2,8,128]{2,1,0:T(8,128)S(1)} %get-tuple-element.45.plane_rows, f32[16,128,256]{2,1,0:T(8,128)S(1)} %get-tuple-element.37.slab_ref, ...), custom_call_target="tpu_custom_call", output_to_operand_aliasing={{}: (5, {})} | custom-call | tf_op jit(solution)/shard_map/combine/pallas_call | solution.py:365
  62.6 0.5 collective-permute-done.9.second_ref
  63.1 1.6 %gradient.1 = (f32[16,2,128,128]{3,2,1,0:T(8,128)}, f32[2,128]{1,0:T(2,128)}) custom-call(f32[2,128]{1,0:T(2,128)S(1)} %add.37.first_ref, f32[2,128]{1,0:T(2,128)S(1)} %collective-permute-done.9.second_ref, f32[16,10,128,128]{3,2,1,0:T(8,128)S(1)} %combine.1.parts_ref), custom_call_target="tpu_custom_call" | custom-call | tf_op jit(solution)/shard_map/gradient/pallas_call | solution.py:408
  (20 shorter events, 1.3 us)
Async XLA Ops:
  1.9 28.7 %collective-permute-start.1 = (f32[8,2,128,128]{3,2,1,0:T(8,128)S(1)}, f32[8,2,128,128]{3,2,1,0:T(8,128)S(1)}, u32[]{:S(2)}, u32[]{:S(2)}) collective-permute-start(f32[8,2,128,128]{3,2,1,0:T(8,128)S(1)} %take.1), channel_id=1, source_target_pairs={{0,12},{2,14},{4,0},{6,2},{8,4},{10,6},{12,8},{14,10},{1,13},{3,15... | collective-permute-start | bytes 3145736 | tf_op jit(solution)/shard_map/ppermute | solution.py:429
  14.6 8.6 %copy-start.3 = (s32[16,2]{0,1:T(2,128)S(1)}, s32[16,2]{0,1:T(2,128)}, u32[]{:S(2)}) copy-start(s32[16,2]{0,1:T(2,128)} %param.5) | copy-start | bytes 388
  21.8 14.6 %collective-permute-start.2 = (f32[8,2,128,128]{3,2,1,0:T(8,128)}, f32[8,2,128,128]{3,2,1,0:T(8,128)S(1)}, u32[]{:S(2)}, u32[]{:S(2)}) collective-permute-start(f32[8,2,128,128]{3,2,1,0:T(8,128)} %get-tuple-element.34), channel_id=1, source_target_pairs={{0,1},{1,0},{2,3},{3,2},{4,5},{5,4},{6,7},{7,6},{8,9},{9,8},{10,11... | collective-permute-start | bytes 3145736 | tf_op jit(solution)/shard_map/ppermute | solution.py:429
  21.8 14.6 %collective-permute-start.3 = (f32[8,2,128,128]{3,2,1,0:T(8,128)}, f32[8,2,128,128]{3,2,1,0:T(8,128)}, u32[]{:S(2)}, u32[]{:S(2)}) collective-permute-start(f32[8,2,128,128]{3,2,1,0:T(8,128)} %get-tuple-element.35), channel_id=1, source_target_pairs={{0,1},{1,0},{2,3},{3,2},{4,5},{5,4},{6,7},{7,6},{8,9},{9,8},{10,11... | collective-permute-start | bytes 3145736 | tf_op jit(solution)/shard_map/ppermute | solution.py:429
  22.3 25.2 %collective-permute-start = (f32[6,2,128,128]{3,2,1,0:T(8,128)}, f32[6,2,128,128]{3,2,1,0:T(8,128)}, u32[]{:S(2)}, u32[]{:S(2)}) collective-permute-start(f32[6,2,128,128]{3,2,1,0:T(8,128)} %get-tuple-element.29), channel_id=1, source_target_pairs={{0,12},{2,14},{4,0},{6,2},{8,4},{10,6},{12,8},{14,10},{1,13},{3,15... | collective-permute-start | bytes 2359304 | tf_op jit(solution)/shard_map/ppermute | solution.py:429
  22.8 29.2 %collective-permute-start.4 = (f32[2,2,128,128]{3,2,1,0:T(8,128)}, f32[2,2,128,128]{3,2,1,0:T(8,128)S(1)}, u32[]{:S(2)}, u32[]{:S(2)}) collective-permute-start(f32[2,2,128,128]{3,2,1,0:T(8,128)} %get-tuple-element.41), channel_id=1, source_target_pairs={{0,12},{2,14},{4,0},{6,2},{8,4},{10,6},{12,8},{14,10},{1,13},{3,15... | collective-permute-start | bytes 786440 | tf_op jit(solution)/shard_map/ppermute | solution.py:429
  23.3 1.6 %copy-start = (f32[16,2,128,128]{3,2,1,0:T(8,128)S(1)}, f32[16,2,128,128]{3,2,1,0:T(8,128)}, u32[]{:S(2)}) copy-start(f32[16,2,128,128]{3,2,1,0:T(8,128)} %get-tuple-element.23.rotation_ref.own_ref) | copy-start | bytes 6291460
  24.9 2.2 %copy-start.2 = (f32[16,2,2,128,128]{4,3,2,1,0:T(8,128)S(1)}, f32[16,2,2,128,128]{4,3,2,1,0:T(8,128)}, u32[]{:S(2)}) copy-start(f32[16,2,2,128,128]{4,3,2,1,0:T(8,128)} %correlation_ref.1) | copy-start | bytes 12582916
  29.6 6.8 %copy-start.1 = (f32[16,2,128,128]{3,2,1,0:T(8,128)S(1)}, f32[16,2,128,128]{3,2,1,0:T(8,128)}, u32[]{:S(2)}) copy-start(f32[16,2,128,128]{3,2,1,0:T(8,128)} %get-tuple-element.23.rotation_ref.own_ref) | copy-start | bytes 6291460
  52.3 3.1 %collective-permute-start.7 = (f32[2,128]{1,0:T(2,128)S(1)}, f32[2,128]{1,0:T(2,128)S(1)}, u32[]{:S(2)}, u32[]{:S(2)}) collective-permute-start(f32[2,128]{1,0:T(2,128)S(1)} %get-tuple-element.43), channel_id=1, source_target_pairs={{0,3},{1,2},{2,1},{3,0},{4,7},{5,6},{6,5},{7,4},{8,11},{9,10},{10,... | collective-permute-start | bytes 3080 | tf_op jit(solution)/shard_map/ppermute | solution.py:439
  52.4 3.6 %collective-permute-start.6 = (f32[2,128]{1,0:T(2,128)S(1)}, f32[2,128]{1,0:T(2,128)S(1)}, u32[]{:S(2)}, u32[]{:S(2)}) collective-permute-start(f32[2,128]{1,0:T(2,128)S(1)} %get-tuple-element.43), channel_id=1, source_target_pairs={{0,2},{1,3},{2,0},{3,1},{4,6},{5,7},{6,4},{7,5},{8,10},{9,11},{10,... | collective-permute-start | bytes 3080 | tf_op jit(solution)/shard_map/ppermute | solution.py:439
  53.9 2.1 %collective-permute-start.5 = (f32[2,128]{1,0:T(2,128)S(1)}, f32[2,128]{1,0:T(2,128)S(1)}, u32[]{:S(2)}, u32[]{:S(2)}) collective-permute-start(f32[2,128]{1,0:T(2,128)S(1)} %get-tuple-element.43), channel_id=1, source_target_pairs={{0,1},{1,0},{2,3},{3,2},{4,5},{5,4},{6,7},{7,6},{8,9},{9,8},{10,11... | collective-permute-start | bytes 3080 | tf_op jit(solution)/shard_map/ppermute | solution.py:439
  56.0 4.0 %collective-permute-start.8 = (f32[2,128]{1,0:T(2,128)S(1)}, f32[2,128]{1,0:T(2,128)S(1)}, u32[]{:S(2)}, u32[]{:S(2)}) collective-permute-start(f32[2,128]{1,0:T(2,128)S(1)} %add_add_fusion), channel_id=1, source_target_pairs={{0,9},{1,8},{2,11},{3,10},{4,13},{5,12},{6,15},{7,14},{8,1},{9,0},... | collective-permute-start | bytes 3080 | tf_op jit(solution)/shard_map/ppermute | solution.py:439
  60.0 3.1 %collective-permute-start.9 = (f32[2,128]{1,0:T(2,128)S(1)}, f32[2,128]{1,0:T(2,128)S(1)}, u32[]{:S(2)}, u32[]{:S(2)}) collective-permute-start(f32[2,128]{1,0:T(2,128)S(1)} %add.37.first_ref), channel_id=1, source_target_pairs={{0,5},{1,4},{2,7},{3,6},{4,1},{5,0},{6,3},{7,2},{8,13},{9,12},{10,... | collective-permute-start | bytes 3080 | tf_op jit(solution)/shard_map/ppermute | solution.py:439

commit v5 on v4

--- a/solution.py
+++ b/solution.py
@@ -391,9 +391,9 @@
         for d in range(2):
             real = real + (parts_ref[k, 2 + 4 * d] * across[d] - parts_ref[k, 4 + 4 * d] * down[d])
             imag = imag + (parts_ref[k, 3 + 4 * d] * across[d] + parts_ref[k, 5 + 4 * d] * down[d])
-        buffer[k, 0] = real
-        buffer[k, 1] = imag
-        copy_out(k).start()
+        for p, half in enumerate((real, imag)):
+            buffer[k, p] = half
+            pltpu.make_async_copy(buffer.at[k, p], out_ref.at[k, p], sems.at[k]).start()
 
     small_copy.wait()
 

time: 65.2 us -> 65.2 us (level)
  no operation moved by 1% of the time
where the time goes in v5:
time: 65.2 us; the launch traced here: 64.8 us
  Pallas kernels  34.1 us (52%)
  waiting for transfers between devices  14.2 us (22%)
  starting transfers between devices  11.7 us (18%)
  local copies, waits for them, and re-layouts  3.79 us (6%)
  between operations  0.9 us (1%)
    pallas_call x2, Pallas kernels, polar_call(): pl.pallas_call(functools.partial(polar_kernel, carried=len(carried), chun...  14.8 us
    ppermute x5, waiting for transfers between devices, shifted(): lax.ppermute(value, axis, [(source, (source + steps) % count) for source...  9.39 us
    ppermute x5, starting transfers between devices, shifted(): lax.ppermute(value, axis, [(source, (source + steps) % count) for source...  6.52 us
    pallas_call x1, Pallas kernels, plane_call(): pl.pallas_call(functools.partial(plane_kernel, first=first), in_specs=[pl...  5.84 us
    ppermute x5, starting transfers between devices, swapped(): return lax.ppermute(value, ('kxy', 'kz'), pairs)  5.14 us
    ppermute x5, waiting for transfers between devices, swapped(): return lax.ppermute(value, ('kxy', 'kz'), pairs)  4.82 us
    pallas_call x1, Pallas kernels, slab_call(): pl.pallas_call(functools.partial(slab_kernel, pieces=len(pieces)), in_spe...  4.73 us
    unnamed x8, local copies, waits for them, and re-layouts  3.78 us
  transfers between devices with their start and end apart: 10, of which 7 were waited for; matrix products, arithmetic and copies ran while one was open for 0% of the time, Pallas kernels for 48%

profile of v5, /device:TPU:0, one launch (start us, length us, event | category | flops | bytes accessed | tf_op | source)
XLA Modules:
  0.0 64.8 jit_solution(10987493357248623940)
XLA Ops:
  0.6 1.2 %take.1 = f32[8,2,128,128]{3,2,1,0:T(8,128)S(1)} custom-call(f32[16,2,128,128]{3,2,1,0:T(8,128)} %start_ref.5), custom_call_target="tpu_custom_call" | custom-call | tf_op jit(solution)/shard_map/take/pallas_call | solution.py:114
  1.9 5.1 %collective-permute-start.1 = (f32[8,2,128,128]{3,2,1,0:T(8,128)S(1)}, f32[8,2,128,128]{3,2,1,0:T(8,128)S(1)}, u32[]{:S(2)}, u32[]{:S(2)}) collective-permute-start(f32[8,2,128,128]{3,2,1,0:T(8,128)S(1)} %take.1), channel_id=1, source_target_pairs={{0,12},{2,14},{4,0},{6,2},{8,4},{10,6},{12,8},{14,10},{1,13},{3,15... | collective-permute-start | bytes 3145736 | tf_op jit(solution)/shard_map/ppermute | solution.py:429
  7.0 7.6 %polar.2 = (f32[16,2,128,128]{3,2,1,0:T(8,128)}, f32[8,2,128,128]{3,2,1,0:T(8,128)}, f32[6,2,128,128]{3,2,1,0:T(8,128)}, f32[2,2,128,128]{3,2,1,0:T(8,128)}) custom-call(f32[16,2,128,128]{3,2,1,0:T(8,128)} %start_ref.5), custom_call_target="tpu_custom_call" | custom-call | tf_op jit(solution)/shard_map/polar/pallas_call | solution.py:94
  14.6 7.2 %polar.3 = (f32[16,2,128,128]{3,2,1,0:T(8,128)}, f32[8,2,128,128]{3,2,1,0:T(8,128)}) custom-call(f32[16,2,128,128]{3,2,1,0:T(8,128)} %start_ref.5, f32[16,2,128,128]{3,2,1,0:T(8,128)} %get-tuple-element.26.refs_0_), custom_call_target="tpu_custom_call", output_to_operand_aliasing={{0}: (1, {})} | custom-call | tf_op jit(solution)/shard_map/polar/pallas_call | solution.py:94
  21.8 0.5 collective-permute-start.3
  22.8 0.5 collective-permute-start.4
  23.3 1.6 %copy-done = f32[16,2,128,128]{3,2,1,0:T(8,128)S(1)} copy-done((f32[16,2,128,128]{3,2,1,0:T(8,128)S(1)}, f32[16,2,128,128]{3,2,1,0:T(8,128)}, u32[]{:S(2)}) %copy-start) | copy-done | bytes 2097176
  24.9 2.2 %copy-done.2 = f32[16,2,2,128,128]{4,3,2,1,0:T(8,128)S(1)} copy-done((f32[16,2,2,128,128]{4,3,2,1,0:T(8,128)S(1)}, f32[16,2,2,128,128]{4,3,2,1,0:T(8,128)}, u32[]{:S(2)}) %copy-start.2) | copy-done | bytes 4194328
  27.1 2.5 %sandwich.1 = (f32[16,128,256]{2,1,0:T(8,128)S(1)}, f32[16,128,256]{2,1,0:T(8,128)S(1)}) custom-call(f32[16,2,128,128]{3,2,1,0:T(8,128)S(1)} %copy-done, f32[16,2,2,128,128]{4,3,2,1,0:T(8,128)S(1)} %copy-done.2), custom_call_target="tpu_custom_call" | custom-call | tf_op jit(solution)/shard_map/sandwich/pallas_call | solution.py:135
  29.7 0.9 %collective-permute-done.1.partner_ref = f32[8,2,128,128]{3,2,1,0:T(8,128)S(1)} collective-permute-done((f32[8,2,128,128]{3,2,1,0:T(8,128)S(1)}, f32[8,2,128,128]{3,2,1,0:T(8,128)S(1)}, u32[]{:S(2)}, u32[]{:S(2)}) %collective-permute-start.1) | collective-permute-done | bytes 1048608 | tf_op jit(solution)/shard_map/ppermute | solution.py:429
  30.5 5.8 %plane.1 = (f32[8,128,256]{2,1,0:T(8,128)S(1)}, f32[8,8,128]{2,1,0:T(8,128)S(1)}, f32[2,128]{1,0:T(2,128)S(1)}) custom-call(s32[16]{0:T(128)S(1)} %select_reduce_fusion.order_ref, f32[16,128,256]{2,1,0:T(8,128)S(1)} %get-tuple-element.28.sandwich_ref, f32[8,2,128,128]{3,2,1,0:T(8,128)S(1)} %collective-permute-done.1.partner_ref, ...), custom_call_target="tpu_custom_call" | custom-call | tf_op jit(solution)/shard_map/plane/pallas_call | solution.py:280
  36.4 4.7 %slab.1 = (f32[16,128,256]{2,1,0:T(8,128)S(1)}, f32[16,8,128]{2,1,0:T(8,128)S(1)}, f32[16,10,128,128]{3,2,1,0:T(8,128)S(1)}, f32[2,128]{1,0:T(2,128)S(1)}) custom-call(s32[16]{0:T(128)S(1)} %select_reduce_fusion.order_ref, s32[16]{0:T(128)S(1)} %fusion.slots_ref, f32[2,128]{1,0:T(2,128)S(1)} %get-tuple-element.30.before_ref, ...), custom_call_target="tpu_custom_call" | custom-call | tf_op jit(solution)/shard_map/slab/pallas_call | solution.py:234
  41.2 6.3 %collective-permute-done.partner_ref = f32[6,2,128,128]{3,2,1,0:T(8,128)} collective-permute-done((f32[6,2,128,128]{3,2,1,0:T(8,128)}, f32[6,2,128,128]{3,2,1,0:T(8,128)}, u32[]{:S(2)}, u32[]{:S(2)}) %collective-permute-start) | collective-permute-done | bytes 786464 | tf_op jit(solution)/shard_map/ppermute | solution.py:429
  47.5 2.3 %middle.1 = (f32[16,10,128,128]{3,2,1,0:T(8,128)S(1)}, f32[2,128]{1,0:T(2,128)S(1)}, f32[2,128,256]{2,1,0:T(8,128)S(1)}) custom-call(s32[16]{0:T(128)S(1)} %select_reduce_fusion.order_ref, f32[16,128,256]{2,1,0:T(8,128)S(1)} %get-tuple-element.28.sandwich_ref, f32[6,2,128,128]{3,2,1,0:T(8,128)} %collective-permute-done.partner_ref, ...), custom_call_target="tpu_custom_call", output_to_operand_aliasing={{0}: (6, {})} | custom-call | tf_op jit(solution)/shard_map/middle/pallas_call | solution.py:313
  49.8 2.2 %collective-permute-done.4.partner_ref = f32[2,2,128,128]{3,2,1,0:T(8,128)S(1)} collective-permute-done((f32[2,2,128,128]{3,2,1,0:T(8,128)}, f32[2,2,128,128]{3,2,1,0:T(8,128)S(1)}, u32[]{:S(2)}, u32[]{:S(2)}) %collective-permute-start.4) | collective-permute-done | bytes 262176 | tf_op jit(solution)/shard_map/ppermute | solution.py:429
  52.4 1.5 %collective-permute-start.6 = (f32[2,128]{1,0:T(2,128)S(1)}, f32[2,128]{1,0:T(2,128)S(1)}, u32[]{:S(2)}, u32[]{:S(2)}) collective-permute-start(f32[2,128]{1,0:T(2,128)S(1)} %get-tuple-element.43), channel_id=1, source_target_pairs={{0,2},{1,3},{2,0},{3,1},{4,6},{5,7},{6,4},{7,5},{8,10},{9,11},{10,... | collective-permute-start | bytes 3080 | tf_op jit(solution)/shard_map/ppermute | solution.py:439
  54.2 1.1 %collective-permute-done.7 = f32[2,128]{1,0:T(2,128)S(1)} collective-permute-done((f32[2,128]{1,0:T(2,128)S(1)}, f32[2,128]{1,0:T(2,128)S(1)}, u32[]{:S(2)}, u32[]{:S(2)}) %collective-permute-start.7) | collective-permute-done | bytes 1056 | tf_op jit(solution)/shard_map/ppermute | solution.py:439
  55.4 0.7 %collective-permute-done.6 = f32[2,128]{1,0:T(2,128)S(1)} collective-permute-done((f32[2,128]{1,0:T(2,128)S(1)}, f32[2,128]{1,0:T(2,128)S(1)}, u32[]{:S(2)}, u32[]{:S(2)}) %collective-permute-start.6) | collective-permute-done | bytes 1056 | tf_op jit(solution)/shard_map/ppermute | solution.py:439
  56.0 1.4 %collective-permute-start.8 = (f32[2,128]{1,0:T(2,128)S(1)}, f32[2,128]{1,0:T(2,128)S(1)}, u32[]{:S(2)}, u32[]{:S(2)}) collective-permute-start(f32[2,128]{1,0:T(2,128)S(1)} %add_add_fusion), channel_id=1, source_target_pairs={{0,9},{1,8},{2,11},{3,10},{4,13},{5,12},{6,15},{7,14},{8,1},{9,0},... | collective-permute-start | bytes 3080 | tf_op jit(solution)/shard_map/ppermute | solution.py:439
  57.4 2.6 %collective-permute-done.8 = f32[2,128]{1,0:T(2,128)S(1)} collective-permute-done((f32[2,128]{1,0:T(2,128)S(1)}, f32[2,128]{1,0:T(2,128)S(1)}, u32[]{:S(2)}, u32[]{:S(2)}) %collective-permute-start.8) | collective-permute-done | bytes 1056 | tf_op jit(solution)/shard_map/ppermute | solution.py:439
  60.0 1.8 %collective-permute-start.9 = (f32[2,128]{1,0:T(2,128)S(1)}, f32[2,128]{1,0:T(2,128)S(1)}, u32[]{:S(2)}, u32[]{:S(2)}) collective-permute-start(f32[2,128]{1,0:T(2,128)S(1)} %add.37.first_ref), channel_id=1, source_target_pairs={{0,5},{1,4},{2,7},{3,6},{4,1},{5,0},{6,3},{7,2},{8,13},{9,12},{10,... | collective-permute-start | bytes 3080 | tf_op jit(solution)/shard_map/ppermute | solution.py:439
  61.8 0.8 %combine.1.parts_ref = f32[16,10,128,128]{3,2,1,0:T(8,128)S(1)} custom-call(s32[16]{0:T(128)S(1)} %select_reduce_fusion.order_ref, f32[2,128,256]{2,1,0:T(8,128)S(1)} %get-tuple-element.44.plane_ref, f32[2,8,128]{2,1,0:T(8,128)S(1)} %get-tuple-element.45.plane_rows, f32[16,128,256]{2,1,0:T(8,128)S(1)} %get-tuple-element.37.slab_ref, ...), custom_call_target="tpu_custom_call", output_to_operand_aliasing={{}: (5, {})} | custom-call | tf_op jit(solution)/shard_map/combine/pallas_call | solution.py:365
  62.6 0.5 collective-permute-done.9.second_ref
  63.1 1.6 %gradient.1 = (f32[16,2,128,128]{3,2,1,0:T(8,128)}, f32[2,128]{1,0:T(2,128)}) custom-call(f32[2,128]{1,0:T(2,128)S(1)} %add.37.first_ref, f32[2,128]{1,0:T(2,128)S(1)} %collective-permute-done.9.second_ref, f32[16,10,128,128]{3,2,1,0:T(8,128)S(1)} %combine.1.parts_ref), custom_call_target="tpu_custom_call" | custom-call | tf_op jit(solution)/shard_map/gradient/pallas_call | solution.py:408
  (20 shorter events, 1.3 us)
Async XLA Ops:
  1.9 28.7 %collective-permute-start.1 = (f32[8,2,128,128]{3,2,1,0:T(8,128)S(1)}, f32[8,2,128,128]{3,2,1,0:T(8,128)S(1)}, u32[]{:S(2)}, u32[]{:S(2)}) collective-permute-start(f32[8,2,128,128]{3,2,1,0:T(8,128)S(1)} %take.1), channel_id=1, source_target_pairs={{0,12},{2,14},{4,0},{6,2},{8,4},{10,6},{12,8},{14,10},{1,13},{3,15... | collective-permute-start | bytes 3145736 | tf_op jit(solution)/shard_map/ppermute | solution.py:429
  14.6 8.6 %copy-start.3 = (s32[16,2]{0,1:T(2,128)S(1)}, s32[16,2]{0,1:T(2,128)}, u32[]{:S(2)}) copy-start(s32[16,2]{0,1:T(2,128)} %param.5) | copy-start | bytes 388
  21.8 14.6 %collective-permute-start.2 = (f32[8,2,128,128]{3,2,1,0:T(8,128)}, f32[8,2,128,128]{3,2,1,0:T(8,128)S(1)}, u32[]{:S(2)}, u32[]{:S(2)}) collective-permute-start(f32[8,2,128,128]{3,2,1,0:T(8,128)} %get-tuple-element.34), channel_id=1, source_target_pairs={{0,1},{1,0},{2,3},{3,2},{4,5},{5,4},{6,7},{7,6},{8,9},{9,8},{10,11... | collective-permute-start | bytes 3145736 | tf_op jit(solution)/shard_map/ppermute | solution.py:429
  21.8 14.6 %collective-permute-start.3 = (f32[8,2,128,128]{3,2,1,0:T(8,128)}, f32[8,2,128,128]{3,2,1,0:T(8,128)}, u32[]{:S(2)}, u32[]{:S(2)}) collective-permute-start(f32[8,2,128,128]{3,2,1,0:T(8,128)} %get-tuple-element.35), channel_id=1, source_target_pairs={{0,1},{1,0},{2,3},{3,2},{4,5},{5,4},{6,7},{7,6},{8,9},{9,8},{10,11... | collective-permute-start | bytes 3145736 | tf_op jit(solution)/shard_map/ppermute | solution.py:429
  22.3 25.2 %collective-permute-start = (f32[6,2,128,128]{3,2,1,0:T(8,128)}, f32[6,2,128,128]{3,2,1,0:T(8,128)}, u32[]{:S(2)}, u32[]{:S(2)}) collective-permute-start(f32[6,2,128,128]{3,2,1,0:T(8,128)} %get-tuple-element.29), channel_id=1, source_target_pairs={{0,12},{2,14},{4,0},{6,2},{8,4},{10,6},{12,8},{14,10},{1,13},{3,15... | collective-permute-start | bytes 2359304 | tf_op jit(solution)/shard_map/ppermute | solution.py:429
  22.8 29.2 %collective-permute-start.4 = (f32[2,2,128,128]{3,2,1,0:T(8,128)}, f32[2,2,128,128]{3,2,1,0:T(8,128)S(1)}, u32[]{:S(2)}, u32[]{:S(2)}) collective-permute-start(f32[2,2,128,128]{3,2,1,0:T(8,128)} %get-tuple-element.41), channel_id=1, source_target_pairs={{0,12},{2,14},{4,0},{6,2},{8,4},{10,6},{12,8},{14,10},{1,13},{3,15... | collective-permute-start | bytes 786440 | tf_op jit(solution)/shard_map/ppermute | solution.py:429
  23.3 1.6 %copy-start = (f32[16,2,128,128]{3,2,1,0:T(8,128)S(1)}, f32[16,2,128,128]{3,2,1,0:T(8,128)}, u32[]{:S(2)}) copy-start(f32[16,2,128,128]{3,2,1,0:T(8,128)} %get-tuple-element.23.rotation_ref.own_ref) | copy-start | bytes 6291460
  24.9 2.2 %copy-start.2 = (f32[16,2,2,128,128]{4,3,2,1,0:T(8,128)S(1)}, f32[16,2,2,128,128]{4,3,2,1,0:T(8,128)}, u32[]{:S(2)}) copy-start(f32[16,2,2,128,128]{4,3,2,1,0:T(8,128)} %correlation_ref.1) | copy-start | bytes 12582916
  29.6 6.8 %copy-start.1 = (f32[16,2,128,128]{3,2,1,0:T(8,128)S(1)}, f32[16,2,128,128]{3,2,1,0:T(8,128)}, u32[]{:S(2)}) copy-start(f32[16,2,128,128]{3,2,1,0:T(8,128)} %get-tuple-element.23.rotation_ref.own_ref) | copy-start | bytes 6291460
  52.3 3.1 %collective-permute-start.7 = (f32[2,128]{1,0:T(2,128)S(1)}, f32[2,128]{1,0:T(2,128)S(1)}, u32[]{:S(2)}, u32[]{:S(2)}) collective-permute-start(f32[2,128]{1,0:T(2,128)S(1)} %get-tuple-element.43), channel_id=1, source_target_pairs={{0,3},{1,2},{2,1},{3,0},{4,7},{5,6},{6,5},{7,4},{8,11},{9,10},{10,... | collective-permute-start | bytes 3080 | tf_op jit(solution)/shard_map/ppermute | solution.py:439
  52.4 3.6 %collective-permute-start.6 = (f32[2,128]{1,0:T(2,128)S(1)}, f32[2,128]{1,0:T(2,128)S(1)}, u32[]{:S(2)}, u32[]{:S(2)}) collective-permute-start(f32[2,128]{1,0:T(2,128)S(1)} %get-tuple-element.43), channel_id=1, source_target_pairs={{0,2},{1,3},{2,0},{3,1},{4,6},{5,7},{6,4},{7,5},{8,10},{9,11},{10,... | collective-permute-start | bytes 3080 | tf_op jit(solution)/shard_map/ppermute | solution.py:439
  53.9 2.1 %collective-permute-start.5 = (f32[2,128]{1,0:T(2,128)S(1)}, f32[2,128]{1,0:T(2,128)S(1)}, u32[]{:S(2)}, u32[]{:S(2)}) collective-permute-start(f32[2,128]{1,0:T(2,128)S(1)} %get-tuple-element.43), channel_id=1, source_target_pairs={{0,1},{1,0},{2,3},{3,2},{4,5},{5,4},{6,7},{7,6},{8,9},{9,8},{10,11... | collective-permute-start | bytes 3080 | tf_op jit(solution)/shard_map/ppermute | solution.py:439
  56.0 4.0 %collective-permute-start.8 = (f32[2,128]{1,0:T(2,128)S(1)}, f32[2,128]{1,0:T(2,128)S(1)}, u32[]{:S(2)}, u32[]{:S(2)}) collective-permute-start(f32[2,128]{1,0:T(2,128)S(1)} %add_add_fusion), channel_id=1, source_target_pairs={{0,9},{1,8},{2,11},{3,10},{4,13},{5,12},{6,15},{7,14},{8,1},{9,0},... | collective-permute-start | bytes 3080 | tf_op jit(solution)/shard_map/ppermute | solution.py:439
  60.0 3.1 %collective-permute-start.9 = (f32[2,128]{1,0:T(2,128)S(1)}, f32[2,128]{1,0:T(2,128)S(1)}, u32[]{:S(2)}, u32[]{:S(2)}) collective-permute-start(f32[2,128]{1,0:T(2,128)S(1)} %add.37.first_ref), channel_id=1, source_target_pairs={{0,5},{1,4},{2,7},{3,6},{4,1},{5,0},{6,3},{7,2},{8,13},{9,12},{10,... | collective-permute-start | bytes 3080 | tf_op jit(solution)/shard_map/ppermute | solution.py:439

commit v6 on v5

--- a/solution.py
+++ b/solution.py
@@ -439,10 +439,10 @@
         return lax.ppermute(value, ("kxy", "kz"), pairs)
 
     value = value + swapped(value, 0, 1) + (swapped(value, 1, 0) + swapped(value, 1, 1))
-    distance = count // 2
-    while distance > 2:
+    distance = 2
+    while 2 * distance < count:
         value = value + swapped(value, distance, 1)
-        distance //= 2
+        distance *= 2
     return value, swapped(value, distance, 1)
 
 

time: 65.2 us -> 65.2 us (level)
  no operation moved by 1% of the time
where the time goes in v6:
time: 65.2 us; the launch traced here: 64.8 us
  Pallas kernels  34.1 us (52%)
  waiting for transfers between devices  14.3 us (22%)
  starting transfers between devices  11.5 us (18%)
  local copies, waits for them, and re-layouts  3.79 us (6%)
  between operations  0.9 us (1%)
    pallas_call x2, Pallas kernels, polar_call(): pl.pallas_call(functools.partial(polar_kernel, carried=len(carried), chun...  14.8 us
    ppermute x5, waiting for transfers between devices, shifted(): lax.ppermute(value, axis, [(source, (source + steps) % count) for source...  9.39 us
    ppermute x5, starting transfers between devices, shifted(): lax.ppermute(value, axis, [(source, (source + steps) % count) for source...  6.52 us
    pallas_call x1, Pallas kernels, plane_call(): pl.pallas_call(functools.partial(plane_kernel, first=first), in_specs=[pl...  5.84 us
    ppermute x5, starting transfers between devices, swapped(): return lax.ppermute(value, ('kxy', 'kz'), pairs)  5.02 us
    ppermute x5, waiting for transfers between devices, swapped(): return lax.ppermute(value, ('kxy', 'kz'), pairs)  4.94 us
    pallas_call x1, Pallas kernels, slab_call(): pl.pallas_call(functools.partial(slab_kernel, pieces=len(pieces)), in_spe...  4.73 us
    unnamed x8, local copies, waits for them, and re-layouts  3.78 us
  transfers between devices with their start and end apart: 10, of which 7 were waited for; matrix products, arithmetic and copies ran while one was open for 0% of the time, Pallas kernels for 48%

profile of v6, /device:TPU:0, one launch (start us, length us, event | category | flops | bytes accessed | tf_op | source)
XLA Modules:
  0.0 64.8 jit_solution(2764900484871049019)
XLA Ops:
  0.6 1.2 %take.1 = f32[8,2,128,128]{3,2,1,0:T(8,128)S(1)} custom-call(f32[16,2,128,128]{3,2,1,0:T(8,128)} %start_ref.5), custom_call_target="tpu_custom_call" | custom-call | tf_op jit(solution)/shard_map/take/pallas_call | solution.py:114
  1.9 5.1 %collective-permute-start.1 = (f32[8,2,128,128]{3,2,1,0:T(8,128)S(1)}, f32[8,2,128,128]{3,2,1,0:T(8,128)S(1)}, u32[]{:S(2)}, u32[]{:S(2)}) collective-permute-start(f32[8,2,128,128]{3,2,1,0:T(8,128)S(1)} %take.1), channel_id=1, source_target_pairs={{0,12},{2,14},{4,0},{6,2},{8,4},{10,6},{12,8},{14,10},{1,13},{3,15... | collective-permute-start | bytes 3145736 | tf_op jit(solution)/shard_map/ppermute | solution.py:429
  7.0 7.6 %polar.2 = (f32[16,2,128,128]{3,2,1,0:T(8,128)}, f32[8,2,128,128]{3,2,1,0:T(8,128)}, f32[6,2,128,128]{3,2,1,0:T(8,128)}, f32[2,2,128,128]{3,2,1,0:T(8,128)}) custom-call(f32[16,2,128,128]{3,2,1,0:T(8,128)} %start_ref.5), custom_call_target="tpu_custom_call" | custom-call | tf_op jit(solution)/shard_map/polar/pallas_call | solution.py:94
  14.6 7.2 %polar.3 = (f32[16,2,128,128]{3,2,1,0:T(8,128)}, f32[8,2,128,128]{3,2,1,0:T(8,128)}) custom-call(f32[16,2,128,128]{3,2,1,0:T(8,128)} %start_ref.5, f32[16,2,128,128]{3,2,1,0:T(8,128)} %get-tuple-element.26.refs_0_), custom_call_target="tpu_custom_call", output_to_operand_aliasing={{0}: (1, {})} | custom-call | tf_op jit(solution)/shard_map/polar/pallas_call | solution.py:94
  21.8 0.5 collective-permute-start.3
  22.3 0.4 collective-permute-start
  22.8 0.5 collective-permute-start.4
  23.3 1.6 %copy-done = f32[16,2,128,128]{3,2,1,0:T(8,128)S(1)} copy-done((f32[16,2,128,128]{3,2,1,0:T(8,128)S(1)}, f32[16,2,128,128]{3,2,1,0:T(8,128)}, u32[]{:S(2)}) %copy-start) | copy-done | bytes 2097176
  24.9 2.2 %copy-done.2 = f32[16,2,2,128,128]{4,3,2,1,0:T(8,128)S(1)} copy-done((f32[16,2,2,128,128]{4,3,2,1,0:T(8,128)S(1)}, f32[16,2,2,128,128]{4,3,2,1,0:T(8,128)}, u32[]{:S(2)}) %copy-start.2) | copy-done | bytes 4194328
  27.1 2.5 %sandwich.1 = (f32[16,128,256]{2,1,0:T(8,128)S(1)}, f32[16,128,256]{2,1,0:T(8,128)S(1)}) custom-call(f32[16,2,128,128]{3,2,1,0:T(8,128)S(1)} %copy-done, f32[16,2,2,128,128]{4,3,2,1,0:T(8,128)S(1)} %copy-done.2), custom_call_target="tpu_custom_call" | custom-call | tf_op jit(solution)/shard_map/sandwich/pallas_call | solution.py:135
  29.7 0.9 %collective-permute-done.1.partner_ref = f32[8,2,128,128]{3,2,1,0:T(8,128)S(1)} collective-permute-done((f32[8,2,128,128]{3,2,1,0:T(8,128)S(1)}, f32[8,2,128,128]{3,2,1,0:T(8,128)S(1)}, u32[]{:S(2)}, u32[]{:S(2)}) %collective-permute-start.1) | collective-permute-done | bytes 1048608 | tf_op jit(solution)/shard_map/ppermute | solution.py:429
  30.5 5.8 %plane.1 = (f32[8,128,256]{2,1,0:T(8,128)S(1)}, f32[8,8,128]{2,1,0:T(8,128)S(1)}, f32[2,128]{1,0:T(2,128)S(1)}) custom-call(s32[16]{0:T(128)S(1)} %select_reduce_fusion.order_ref, f32[16,128,256]{2,1,0:T(8,128)S(1)} %get-tuple-element.28.sandwich_ref, f32[8,2,128,128]{3,2,1,0:T(8,128)S(1)} %collective-permute-done.1.partner_ref, ...), custom_call_target="tpu_custom_call" | custom-call | tf_op jit(solution)/shard_map/plane/pallas_call | solution.py:280
  36.4 4.7 %slab.1 = (f32[16,128,256]{2,1,0:T(8,128)S(1)}, f32[16,8,128]{2,1,0:T(8,128)S(1)}, f32[16,10,128,128]{3,2,1,0:T(8,128)S(1)}, f32[2,128]{1,0:T(2,128)S(1)}) custom-call(s32[16]{0:T(128)S(1)} %select_reduce_fusion.order_ref, s32[16]{0:T(128)S(1)} %fusion.slots_ref, f32[2,128]{1,0:T(2,128)S(1)} %get-tuple-element.30.before_ref, ...), custom_call_target="tpu_custom_call" | custom-call | tf_op jit(solution)/shard_map/slab/pallas_call | solution.py:234
  41.2 6.3 %collective-permute-done.partner_ref = f32[6,2,128,128]{3,2,1,0:T(8,128)} collective-permute-done((f32[6,2,128,128]{3,2,1,0:T(8,128)}, f32[6,2,128,128]{3,2,1,0:T(8,128)}, u32[]{:S(2)}, u32[]{:S(2)}) %collective-permute-start) | collective-permute-done | bytes 786464 | tf_op jit(solution)/shard_map/ppermute | solution.py:429
  47.5 2.3 %middle.1 = (f32[16,10,128,128]{3,2,1,0:T(8,128)S(1)}, f32[2,128]{1,0:T(2,128)S(1)}, f32[2,128,256]{2,1,0:T(8,128)S(1)}) custom-call(s32[16]{0:T(128)S(1)} %select_reduce_fusion.order_ref, f32[16,128,256]{2,1,0:T(8,128)S(1)} %get-tuple-element.28.sandwich_ref, f32[6,2,128,128]{3,2,1,0:T(8,128)} %collective-permute-done.partner_ref, ...), custom_call_target="tpu_custom_call", output_to_operand_aliasing={{0}: (6, {})} | custom-call | tf_op jit(solution)/shard_map/middle/pallas_call | solution.py:313
  49.8 2.2 %collective-permute-done.4.partner_ref = f32[2,2,128,128]{3,2,1,0:T(8,128)S(1)} collective-permute-done((f32[2,2,128,128]{3,2,1,0:T(8,128)}, f32[2,2,128,128]{3,2,1,0:T(8,128)S(1)}, u32[]{:S(2)}, u32[]{:S(2)}) %collective-permute-start.4) | collective-permute-done | bytes 262176 | tf_op jit(solution)/shard_map/ppermute | solution.py:429
  52.4 1.5 %collective-permute-start.6 = (f32[2,128]{1,0:T(2,128)S(1)}, f32[2,128]{1,0:T(2,128)S(1)}, u32[]{:S(2)}, u32[]{:S(2)}) collective-permute-start(f32[2,128]{1,0:T(2,128)S(1)} %get-tuple-element.43), channel_id=1, source_target_pairs={{0,2},{1,3},{2,0},{3,1},{4,6},{5,7},{6,4},{7,5},{8,10},{9,11},{10,... | collective-permute-start | bytes 3080 | tf_op jit(solution)/shard_map/ppermute | solution.py:439
  54.2 1.1 %collective-permute-done.7 = f32[2,128]{1,0:T(2,128)S(1)} collective-permute-done((f32[2,128]{1,0:T(2,128)S(1)}, f32[2,128]{1,0:T(2,128)S(1)}, u32[]{:S(2)}, u32[]{:S(2)}) %collective-permute-start.7) | collective-permute-done | bytes 1056 | tf_op jit(solution)/shard_map/ppermute | solution.py:439
  55.4 0.7 %collective-permute-done.6 = f32[2,128]{1,0:T(2,128)S(1)} collective-permute-done((f32[2,128]{1,0:T(2,128)S(1)}, f32[2,128]{1,0:T(2,128)S(1)}, u32[]{:S(2)}, u32[]{:S(2)}) %collective-permute-start.6) | collective-permute-done | bytes 1056 | tf_op jit(solution)/shard_map/ppermute | solution.py:439
  56.4 2.7 %collective-permute-done.8 = f32[2,128]{1,0:T(2,128)S(1)} collective-permute-done((f32[2,128]{1,0:T(2,128)S(1)}, f32[2,128]{1,0:T(2,128)S(1)}, u32[]{:S(2)}, u32[]{:S(2)}) %collective-permute-start.8) | collective-permute-done | bytes 1056 | tf_op jit(solution)/shard_map/ppermute | solution.py:439
  59.1 2.7 %collective-permute-start.9 = (f32[2,128]{1,0:T(2,128)S(1)}, f32[2,128]{1,0:T(2,128)S(1)}, u32[]{:S(2)}, u32[]{:S(2)}) collective-permute-start(f32[2,128]{1,0:T(2,128)S(1)} %add.37.first_ref), channel_id=1, source_target_pairs={{0,9},{1,8},{2,11},{3,10},{4,13},{5,12},{6,15},{7,14},{8,1},{9,0},... | collective-permute-start | bytes 3080 | tf_op jit(solution)/shard_map/ppermute | solution.py:439
  61.8 0.8 %combine.1.parts_ref = f32[16,10,128,128]{3,2,1,0:T(8,128)S(1)} custom-call(s32[16]{0:T(128)S(1)} %select_reduce_fusion.order_ref, f32[2,128,256]{2,1,0:T(8,128)S(1)} %get-tuple-element.44.plane_ref, f32[2,8,128]{2,1,0:T(8,128)S(1)} %get-tuple-element.45.plane_rows, f32[16,128,256]{2,1,0:T(8,128)S(1)} %get-tuple-element.37.slab_ref, ...), custom_call_target="tpu_custom_call", output_to_operand_aliasing={{}: (5, {})} | custom-call | tf_op jit(solution)/shard_map/combine/pallas_call | solution.py:365
  62.6 0.5 collective-permute-done.9.second_ref
  63.1 1.6 %gradient.1 = (f32[16,2,128,128]{3,2,1,0:T(8,128)}, f32[2,128]{1,0:T(2,128)}) custom-call(f32[2,128]{1,0:T(2,128)S(1)} %add.37.first_ref, f32[2,128]{1,0:T(2,128)S(1)} %collective-permute-done.9.second_ref, f32[16,10,128,128]{3,2,1,0:T(8,128)S(1)} %combine.1.parts_ref), custom_call_target="tpu_custom_call" | custom-call | tf_op jit(solution)/shard_map/gradient/pallas_call | solution.py:408
  (20 shorter events, 1.3 us)
Async XLA Ops:
  1.9 28.7 %collective-permute-start.1 = (f32[8,2,128,128]{3,2,1,0:T(8,128)S(1)}, f32[8,2,128,128]{3,2,1,0:T(8,128)S(1)}, u32[]{:S(2)}, u32[]{:S(2)}) collective-permute-start(f32[8,2,128,128]{3,2,1,0:T(8,128)S(1)} %take.1), channel_id=1, source_target_pairs={{0,12},{2,14},{4,0},{6,2},{8,4},{10,6},{12,8},{14,10},{1,13},{3,15... | collective-permute-start | bytes 3145736 | tf_op jit(solution)/shard_map/ppermute | solution.py:429
  14.6 8.6 %copy-start.3 = (s32[16,2]{0,1:T(2,128)S(1)}, s32[16,2]{0,1:T(2,128)}, u32[]{:S(2)}) copy-start(s32[16,2]{0,1:T(2,128)} %param.5) | copy-start | bytes 388
  21.8 14.6 %collective-permute-start.2 = (f32[8,2,128,128]{3,2,1,0:T(8,128)}, f32[8,2,128,128]{3,2,1,0:T(8,128)S(1)}, u32[]{:S(2)}, u32[]{:S(2)}) collective-permute-start(f32[8,2,128,128]{3,2,1,0:T(8,128)} %get-tuple-element.34), channel_id=1, source_target_pairs={{0,1},{1,0},{2,3},{3,2},{4,5},{5,4},{6,7},{7,6},{8,9},{9,8},{10,11... | collective-permute-start | bytes 3145736 | tf_op jit(solution)/shard_map/ppermute | solution.py:429
  21.8 14.6 %collective-permute-start.3 = (f32[8,2,128,128]{3,2,1,0:T(8,128)}, f32[8,2,128,128]{3,2,1,0:T(8,128)}, u32[]{:S(2)}, u32[]{:S(2)}) collective-permute-start(f32[8,2,128,128]{3,2,1,0:T(8,128)} %get-tuple-element.35), channel_id=1, source_target_pairs={{0,1},{1,0},{2,3},{3,2},{4,5},{5,4},{6,7},{7,6},{8,9},{9,8},{10,11... | collective-permute-start | bytes 3145736 | tf_op jit(solution)/shard_map/ppermute | solution.py:429
  22.3 25.2 %collective-permute-start = (f32[6,2,128,128]{3,2,1,0:T(8,128)}, f32[6,2,128,128]{3,2,1,0:T(8,128)}, u32[]{:S(2)}, u32[]{:S(2)}) collective-permute-start(f32[6,2,128,128]{3,2,1,0:T(8,128)} %get-tuple-element.29), channel_id=1, source_target_pairs={{0,12},{2,14},{4,0},{6,2},{8,4},{10,6},{12,8},{14,10},{1,13},{3,15... | collective-permute-start | bytes 2359304 | tf_op jit(solution)/shard_map/ppermute | solution.py:429
  22.8 29.2 %collective-permute-start.4 = (f32[2,2,128,128]{3,2,1,0:T(8,128)}, f32[2,2,128,128]{3,2,1,0:T(8,128)S(1)}, u32[]{:S(2)}, u32[]{:S(2)}) collective-permute-start(f32[2,2,128,128]{3,2,1,0:T(8,128)} %get-tuple-element.41), channel_id=1, source_target_pairs={{0,12},{2,14},{4,0},{6,2},{8,4},{10,6},{12,8},{14,10},{1,13},{3,15... | collective-permute-start | bytes 786440 | tf_op jit(solution)/shard_map/ppermute | solution.py:429
  23.3 1.6 %copy-start = (f32[16,2,128,128]{3,2,1,0:T(8,128)S(1)}, f32[16,2,128,128]{3,2,1,0:T(8,128)}, u32[]{:S(2)}) copy-start(f32[16,2,128,128]{3,2,1,0:T(8,128)} %get-tuple-element.23.rotation_ref.own_ref) | copy-start | bytes 6291460
  24.9 2.2 %copy-start.2 = (f32[16,2,2,128,128]{4,3,2,1,0:T(8,128)S(1)}, f32[16,2,2,128,128]{4,3,2,1,0:T(8,128)}, u32[]{:S(2)}) copy-start(f32[16,2,2,128,128]{4,3,2,1,0:T(8,128)} %correlation_ref.1) | copy-start | bytes 12582916
  29.6 6.8 %copy-start.1 = (f32[16,2,128,128]{3,2,1,0:T(8,128)S(1)}, f32[16,2,128,128]{3,2,1,0:T(8,128)}, u32[]{:S(2)}) copy-start(f32[16,2,128,128]{3,2,1,0:T(8,128)} %get-tuple-element.23.rotation_ref.own_ref) | copy-start | bytes 6291460
  52.3 3.1 %collective-permute-start.7 = (f32[2,128]{1,0:T(2,128)S(1)}, f32[2,128]{1,0:T(2,128)S(1)}, u32[]{:S(2)}, u32[]{:S(2)}) collective-permute-start(f32[2,128]{1,0:T(2,128)S(1)} %get-tuple-element.43), channel_id=1, source_target_pairs={{0,3},{1,2},{2,1},{3,0},{4,7},{5,6},{6,5},{7,4},{8,11},{9,10},{10,... | collective-permute-start | bytes 3080 | tf_op jit(solution)/shard_map/ppermute | solution.py:439
  52.4 3.6 %collective-permute-start.6 = (f32[2,128]{1,0:T(2,128)S(1)}, f32[2,128]{1,0:T(2,128)S(1)}, u32[]{:S(2)}, u32[]{:S(2)}) collective-permute-start(f32[2,128]{1,0:T(2,128)S(1)} %get-tuple-element.43), channel_id=1, source_target_pairs={{0,2},{1,3},{2,0},{3,1},{4,6},{5,7},{6,4},{7,5},{8,10},{9,11},{10,... | collective-permute-start | bytes 3080 | tf_op jit(solution)/shard_map/ppermute | solution.py:439
  53.9 2.1 %collective-permute-start.5 = (f32[2,128]{1,0:T(2,128)S(1)}, f32[2,128]{1,0:T(2,128)S(1)}, u32[]{:S(2)}, u32[]{:S(2)}) collective-permute-start(f32[2,128]{1,0:T(2,128)S(1)} %get-tuple-element.43), channel_id=1, source_target_pairs={{0,1},{1,0},{2,3},{3,2},{4,5},{5,4},{6,7},{7,6},{8,9},{9,8},{10,11... | collective-permute-start | bytes 3080 | tf_op jit(solution)/shard_map/ppermute | solution.py:439
  56.0 3.1 %collective-permute-start.8 = (f32[2,128]{1,0:T(2,128)S(1)}, f32[2,128]{1,0:T(2,128)S(1)}, u32[]{:S(2)}, u32[]{:S(2)}) collective-permute-start(f32[2,128]{1,0:T(2,128)S(1)} %add_add_fusion), channel_id=1, source_target_pairs={{0,5},{1,4},{2,7},{3,6},{4,1},{5,0},{6,3},{7,2},{8,13},{9,12},{10,... | collective-permute-start | bytes 3080 | tf_op jit(solution)/shard_map/ppermute | solution.py:439
  59.1 4.0 %collective-permute-start.9 = (f32[2,128]{1,0:T(2,128)S(1)}, f32[2,128]{1,0:T(2,128)S(1)}, u32[]{:S(2)}, u32[]{:S(2)}) collective-permute-start(f32[2,128]{1,0:T(2,128)S(1)} %add.37.first_ref), channel_id=1, source_target_pairs={{0,9},{1,8},{2,11},{3,10},{4,13},{5,12},{6,15},{7,14},{8,1},{9,0},... | collective-permute-start | bytes 3080 | tf_op jit(solution)/shard_map/ppermute | solution.py:439

commit v7 on v5

--- a/solution.py
+++ b/solution.py
@@ -255,7 +255,7 @@
         pairs = [(partner_ref[i, 0], partner_ref[i, 1]) for i in group]
         partners = polar(pairs) if raw else [jnp.concatenate(pair, 1) for pair in pairs]
         rotated = [
-            product(split(picked(i)), both(right_form, split(partner))) for i, partner in zip(group, partners)
+            product(picked(i), both(right_form, split(partner))) for i, partner in zip(group, partners)
         ]
         for i, matrix in zip(group, rotated):
             phase, rows = column_terms(matrix)
@@ -269,7 +269,7 @@
         out_ref[first + i] = matrix
         store_rows(rows_ref, first + i, rows)
 
-    total = plane_products(partner_ref, lambda i: sandwich_ref[order_ref[first + i]], True, finish)
+    total = plane_products(partner_ref, lambda i: split(sandwich_ref[order_ref[first + i]]), True, finish)
     total_ref[...] = before_ref[...]
     total_ref[0:1] = total_ref[0:1] + total
 
@@ -295,14 +295,14 @@
     order_ref, sandwich_ref, partner_ref, before_ref, slab_ref, slab_rows, _, parts_ref, total_ref, last_ref, *, first
 ):
     size = partner_ref.shape[0]
-    for i in range(last_ref.shape[0]):
-        last_ref[i] = sandwich_ref[order_ref[first + size + i]]
+    for i in range(last_ref.shape[1]):
+        last_ref[0, i], last_ref[1, i] = split(sandwich_ref[order_ref[first + size + i]])
 
     def finish(i, matrix, rows):
         k = order_ref[first + i]
         combine(parts_ref, k, (matrix, slab_ref[k]), (rows, load_rows(slab_rows, k)))
 
-    total = plane_products(partner_ref, lambda i: sandwich_ref[order_ref[first + i]], False, finish)
+    total = plane_products(partner_ref, lambda i: split(sandwich_ref[order_ref[first + i]]), False, finish)
     total_ref[...] = before_ref[...]
     total_ref[0:1] = total_ref[0:1] + total
 
@@ -317,7 +317,7 @@
         out_shape=[
             jax.ShapeDtypeStruct(parts.shape, parts.dtype),
             jax.ShapeDtypeStruct(total.shape, total.dtype),
-            jax.ShapeDtypeStruct((last, n, width), sandwich.dtype),
+            jax.ShapeDtypeStruct((2, last, n, width), jnp.bfloat16),
         ],
         input_output_aliases={6: 0},
         compiler_params=pltpu.CompilerParams(vmem_limit_bytes=VMEM),
@@ -325,18 +325,18 @@
     )(order, sandwich, partner, total, slab, slab_rows, parts)
 
 
-def last_kernel(sandwich_ref, partner_ref, before_ref, out_ref, rows_ref, total_ref):
+def last_kernel(left_ref, partner_ref, before_ref, out_ref, rows_ref, total_ref):
     def finish(i, matrix, rows):
         out_ref[i] = matrix
         store_rows(rows_ref, i, rows)
 
-    total = plane_products(partner_ref, lambda i: sandwich_ref[i], False, finish)
+    total = plane_products(partner_ref, lambda i: (left_ref[0, i], left_ref[1, i]), False, finish)
     total_ref[...] = before_ref[...]
     total_ref[0:1] = total_ref[0:1] + total
 
 
-def last_call(sandwich, partner, total):
-    size, n, width = sandwich.shape
+def last_call(left, partner, total):
+    _, size, n, width = left.shape
     whole = pl.BlockSpec(memory_space=pltpu.VMEM)
     return pl.pallas_call(
         last_kernel,
@@ -349,7 +349,7 @@
         ],
         compiler_params=pltpu.CompilerParams(vmem_limit_bytes=VMEM),
         name="last",
-    )(sandwich, partner, total)
+    )(left, partner, total)
 
 
 def combine_kernel(order_ref, plane_ref, plane_rows, slab_ref, slab_rows, _, parts_ref, *, first):

time: 65.2 us -> 65.2 us (level)
  no operation moved by 1% of the time
where the time goes in v7:
time: 65.2 us; the launch traced here: 64.8 us
  Pallas kernels  34.2 us (52%)
  waiting for transfers between devices  14.2 us (22%)
  starting transfers between devices  11.6 us (18%)
  local copies, waits for them, and re-layouts  3.79 us (6%)
  between operations  0.9 us (1%)
    pallas_call x2, Pallas kernels, polar_call(): pl.pallas_call(functools.partial(polar_kernel, carried=len(carried), chun...  14.8 us
    ppermute x5, waiting for transfers between devices, shifted(): lax.ppermute(value, axis, [(source, (source + steps) % count) for source...  9.37 us
    ppermute x5, starting transfers between devices, shifted(): lax.ppermute(value, axis, [(source, (source + steps) % count) for source...  6.52 us
    pallas_call x1, Pallas kernels, plane_call(): pl.pallas_call(functools.partial(plane_kernel, first=first), in_specs=[pl...  5.84 us
    ppermute x5, starting transfers between devices, swapped(): return lax.ppermute(value, ('kxy', 'kz'), pairs)  5.12 us
    ppermute x5, waiting for transfers between devices, swapped(): return lax.ppermute(value, ('kxy', 'kz'), pairs)  4.83 us
    pallas_call x1, Pallas kernels, slab_call(): pl.pallas_call(functools.partial(slab_kernel, pieces=len(pieces)), in_spe...  4.73 us
    unnamed x8, local copies, waits for them, and re-layouts  3.78 us
  transfers between devices with their start and end apart: 10, of which 7 were waited for; matrix products, arithmetic and copies ran while one was open for 0% of the time, Pallas kernels for 48%

profile of v7, /device:TPU:0, one launch (start us, length us, event | category | flops | bytes accessed | tf_op | source)
XLA Modules:
  0.0 64.8 jit_solution(8097890283693690970)
XLA Ops:
  0.6 1.2 %take.1 = f32[8,2,128,128]{3,2,1,0:T(8,128)S(1)} custom-call(f32[16,2,128,128]{3,2,1,0:T(8,128)} %start_ref.5), custom_call_target="tpu_custom_call" | custom-call | tf_op jit(solution)/shard_map/take/pallas_call | solution.py:114
  1.9 5.1 %collective-permute-start.1 = (f32[8,2,128,128]{3,2,1,0:T(8,128)S(1)}, f32[8,2,128,128]{3,2,1,0:T(8,128)S(1)}, u32[]{:S(2)}, u32[]{:S(2)}) collective-permute-start(f32[8,2,128,128]{3,2,1,0:T(8,128)S(1)} %take.1), channel_id=1, source_target_pairs={{0,12},{2,14},{4,0},{6,2},{8,4},{10,6},{12,8},{14,10},{1,13},{3,15... | collective-permute-start | bytes 3145736 | tf_op jit(solution)/shard_map/ppermute | solution.py:429
  7.0 7.6 %polar.2 = (f32[16,2,128,128]{3,2,1,0:T(8,128)}, f32[8,2,128,128]{3,2,1,0:T(8,128)}, f32[6,2,128,128]{3,2,1,0:T(8,128)}, f32[2,2,128,128]{3,2,1,0:T(8,128)}) custom-call(f32[16,2,128,128]{3,2,1,0:T(8,128)} %start_ref.5), custom_call_target="tpu_custom_call" | custom-call | tf_op jit(solution)/shard_map/polar/pallas_call | solution.py:94
  14.6 7.2 %polar.3 = (f32[16,2,128,128]{3,2,1,0:T(8,128)}, f32[8,2,128,128]{3,2,1,0:T(8,128)}) custom-call(f32[16,2,128,128]{3,2,1,0:T(8,128)} %start_ref.5, f32[16,2,128,128]{3,2,1,0:T(8,128)} %get-tuple-element.26.refs_0_), custom_call_target="tpu_custom_call", output_to_operand_aliasing={{0}: (1, {})} | custom-call | tf_op jit(solution)/shard_map/polar/pallas_call | solution.py:94
  21.8 0.5 collective-permute-start.3
  22.8 0.5 collective-permute-start.4
  23.3 1.6 %copy-done = f32[16,2,128,128]{3,2,1,0:T(8,128)S(1)} copy-done((f32[16,2,128,128]{3,2,1,0:T(8,128)S(1)}, f32[16,2,128,128]{3,2,1,0:T(8,128)}, u32[]{:S(2)}) %copy-start) | copy-done | bytes 2097176
  24.9 2.2 %copy-done.2 = f32[16,2,2,128,128]{4,3,2,1,0:T(8,128)S(1)} copy-done((f32[16,2,2,128,128]{4,3,2,1,0:T(8,128)S(1)}, f32[16,2,2,128,128]{4,3,2,1,0:T(8,128)}, u32[]{:S(2)}) %copy-start.2) | copy-done | bytes 4194328
  27.1 2.5 %sandwich.1 = (f32[16,128,256]{2,1,0:T(8,128)S(1)}, f32[16,128,256]{2,1,0:T(8,128)S(1)}) custom-call(f32[16,2,128,128]{3,2,1,0:T(8,128)S(1)} %copy-done, f32[16,2,2,128,128]{4,3,2,1,0:T(8,128)S(1)} %copy-done.2), custom_call_target="tpu_custom_call" | custom-call | tf_op jit(solution)/shard_map/sandwich/pallas_call | solution.py:135
  29.7 0.9 %collective-permute-done.1.partner_ref = f32[8,2,128,128]{3,2,1,0:T(8,128)S(1)} collective-permute-done((f32[8,2,128,128]{3,2,1,0:T(8,128)S(1)}, f32[8,2,128,128]{3,2,1,0:T(8,128)S(1)}, u32[]{:S(2)}, u32[]{:S(2)}) %collective-permute-start.1) | collective-permute-done | bytes 1048608 | tf_op jit(solution)/shard_map/ppermute | solution.py:429
  30.5 5.8 %plane.1 = (f32[8,128,256]{2,1,0:T(8,128)S(1)}, f32[8,8,128]{2,1,0:T(8,128)S(1)}, f32[2,128]{1,0:T(2,128)S(1)}) custom-call(s32[16]{0:T(128)S(1)} %select_reduce_fusion.order_ref, f32[16,128,256]{2,1,0:T(8,128)S(1)} %get-tuple-element.28.sandwich_ref, f32[8,2,128,128]{3,2,1,0:T(8,128)S(1)} %collective-permute-done.1.partner_ref, ...), custom_call_target="tpu_custom_call" | custom-call | tf_op jit(solution)/shard_map/plane/pallas_call | solution.py:280
  36.4 4.7 %slab.1 = (f32[16,128,256]{2,1,0:T(8,128)S(1)}, f32[16,8,128]{2,1,0:T(8,128)S(1)}, f32[16,10,128,128]{3,2,1,0:T(8,128)S(1)}, f32[2,128]{1,0:T(2,128)S(1)}) custom-call(s32[16]{0:T(128)S(1)} %select_reduce_fusion.order_ref, s32[16]{0:T(128)S(1)} %fusion.slots_ref, f32[2,128]{1,0:T(2,128)S(1)} %get-tuple-element.30.before_ref, ...), custom_call_target="tpu_custom_call" | custom-call | tf_op jit(solution)/shard_map/slab/pallas_call | solution.py:234
  41.2 6.3 %collective-permute-done.partner_ref = f32[6,2,128,128]{3,2,1,0:T(8,128)} collective-permute-done((f32[6,2,128,128]{3,2,1,0:T(8,128)}, f32[6,2,128,128]{3,2,1,0:T(8,128)}, u32[]{:S(2)}, u32[]{:S(2)}) %collective-permute-start) | collective-permute-done | bytes 786464 | tf_op jit(solution)/shard_map/ppermute | solution.py:429
  47.5 2.3 %middle.1 = (f32[16,10,128,128]{3,2,1,0:T(8,128)S(1)}, f32[2,128]{1,0:T(2,128)S(1)}, bf16[2,2,128,256]{3,2,1,0:T(8,128)(2,1)S(1)}) custom-call(s32[16]{0:T(128)S(1)} %select_reduce_fusion.order_ref, f32[16,128,256]{2,1,0:T(8,128)S(1)} %get-tuple-element.28.sandwich_ref, ...), custom_call_target="tpu_custom_call", output_to_operand_aliasing={{0}: (6, {})} | custom-call | tf_op jit(solution)/shard_map/middle/pallas_call | solution.py:313
  49.8 2.2 %collective-permute-done.4.partner_ref = f32[2,2,128,128]{3,2,1,0:T(8,128)S(1)} collective-permute-done((f32[2,2,128,128]{3,2,1,0:T(8,128)}, f32[2,2,128,128]{3,2,1,0:T(8,128)S(1)}, u32[]{:S(2)}, u32[]{:S(2)}) %collective-permute-start.4) | collective-permute-done | bytes 262176 | tf_op jit(solution)/shard_map/ppermute | solution.py:429
  52.4 1.5 %collective-permute-start.6 = (f32[2,128]{1,0:T(2,128)S(1)}, f32[2,128]{1,0:T(2,128)S(1)}, u32[]{:S(2)}, u32[]{:S(2)}) collective-permute-start(f32[2,128]{1,0:T(2,128)S(1)} %get-tuple-element.43), channel_id=1, source_target_pairs={{0,2},{1,3},{2,0},{3,1},{4,6},{5,7},{6,4},{7,5},{8,10},{9,11},{10,... | collective-permute-start | bytes 3080 | tf_op jit(solution)/shard_map/ppermute | solution.py:439
  54.2 1.1 %collective-permute-done.7 = f32[2,128]{1,0:T(2,128)S(1)} collective-permute-done((f32[2,128]{1,0:T(2,128)S(1)}, f32[2,128]{1,0:T(2,128)S(1)}, u32[]{:S(2)}, u32[]{:S(2)}) %collective-permute-start.7) | collective-permute-done | bytes 1056 | tf_op jit(solution)/shard_map/ppermute | solution.py:439
  55.4 0.7 %collective-permute-done.6 = f32[2,128]{1,0:T(2,128)S(1)} collective-permute-done((f32[2,128]{1,0:T(2,128)S(1)}, f32[2,128]{1,0:T(2,128)S(1)}, u32[]{:S(2)}, u32[]{:S(2)}) %collective-permute-start.6) | collective-permute-done | bytes 1056 | tf_op jit(solution)/shard_map/ppermute | solution.py:439
  56.0 1.4 %collective-permute-start.8 = (f32[2,128]{1,0:T(2,128)S(1)}, f32[2,128]{1,0:T(2,128)S(1)}, u32[]{:S(2)}, u32[]{:S(2)}) collective-permute-start(f32[2,128]{1,0:T(2,128)S(1)} %add_add_fusion), channel_id=1, source_target_pairs={{0,9},{1,8},{2,11},{3,10},{4,13},{5,12},{6,15},{7,14},{8,1},{9,0},... | collective-permute-start | bytes 3080 | tf_op jit(solution)/shard_map/ppermute | solution.py:439
  57.4 2.6 %collective-permute-done.8 = f32[2,128]{1,0:T(2,128)S(1)} collective-permute-done((f32[2,128]{1,0:T(2,128)S(1)}, f32[2,128]{1,0:T(2,128)S(1)}, u32[]{:S(2)}, u32[]{:S(2)}) %collective-permute-start.8) | collective-permute-done | bytes 1056 | tf_op jit(solution)/shard_map/ppermute | solution.py:439
  60.0 1.8 %collective-permute-start.9 = (f32[2,128]{1,0:T(2,128)S(1)}, f32[2,128]{1,0:T(2,128)S(1)}, u32[]{:S(2)}, u32[]{:S(2)}) collective-permute-start(f32[2,128]{1,0:T(2,128)S(1)} %add.37.first_ref), channel_id=1, source_target_pairs={{0,5},{1,4},{2,7},{3,6},{4,1},{5,0},{6,3},{7,2},{8,13},{9,12},{10,... | collective-permute-start | bytes 3080 | tf_op jit(solution)/shard_map/ppermute | solution.py:439
  61.8 0.8 %combine.1.parts_ref = f32[16,10,128,128]{3,2,1,0:T(8,128)S(1)} custom-call(s32[16]{0:T(128)S(1)} %select_reduce_fusion.order_ref, f32[2,128,256]{2,1,0:T(8,128)S(1)} %get-tuple-element.44.plane_ref, f32[2,8,128]{2,1,0:T(8,128)S(1)} %get-tuple-element.45.plane_rows, f32[16,128,256]{2,1,0:T(8,128)S(1)} %get-tuple-element.37.slab_ref, ...), custom_call_target="tpu_custom_call", output_to_operand_aliasing={{}: (5, {})} | custom-call | tf_op jit(solution)/shard_map/combine/pallas_call | solution.py:365
  62.6 0.5 collective-permute-done.9.second_ref
  63.1 1.6 %gradient.1 = (f32[16,2,128,128]{3,2,1,0:T(8,128)}, f32[2,128]{1,0:T(2,128)}) custom-call(f32[2,128]{1,0:T(2,128)S(1)} %add.37.first_ref, f32[2,128]{1,0:T(2,128)S(1)} %collective-permute-done.9.second_ref, f32[16,10,128,128]{3,2,1,0:T(8,128)S(1)} %combine.1.parts_ref), custom_call_target="tpu_custom_call" | custom-call | tf_op jit(solution)/shard_map/gradient/pallas_call | solution.py:408
  (20 shorter events, 1.3 us)
Async XLA Ops:
  1.9 28.7 %collective-permute-start.1 = (f32[8,2,128,128]{3,2,1,0:T(8,128)S(1)}, f32[8,2,128,128]{3,2,1,0:T(8,128)S(1)}, u32[]{:S(2)}, u32[]{:S(2)}) collective-permute-start(f32[8,2,128,128]{3,2,1,0:T(8,128)S(1)} %take.1), channel_id=1, source_target_pairs={{0,12},{2,14},{4,0},{6,2},{8,4},{10,6},{12,8},{14,10},{1,13},{3,15... | collective-permute-start | bytes 3145736 | tf_op jit(solution)/shard_map/ppermute | solution.py:429
  14.6 8.6 %copy-start.3 = (s32[16,2]{0,1:T(2,128)S(1)}, s32[16,2]{0,1:T(2,128)}, u32[]{:S(2)}) copy-start(s32[16,2]{0,1:T(2,128)} %param.5) | copy-start | bytes 388
  21.8 14.6 %collective-permute-start.2 = (f32[8,2,128,128]{3,2,1,0:T(8,128)}, f32[8,2,128,128]{3,2,1,0:T(8,128)S(1)}, u32[]{:S(2)}, u32[]{:S(2)}) collective-permute-start(f32[8,2,128,128]{3,2,1,0:T(8,128)} %get-tuple-element.34), channel_id=1, source_target_pairs={{0,1},{1,0},{2,3},{3,2},{4,5},{5,4},{6,7},{7,6},{8,9},{9,8},{10,11... | collective-permute-start | bytes 3145736 | tf_op jit(solution)/shard_map/ppermute | solution.py:429
  21.8 14.6 %collective-permute-start.3 = (f32[8,2,128,128]{3,2,1,0:T(8,128)}, f32[8,2,128,128]{3,2,1,0:T(8,128)}, u32[]{:S(2)}, u32[]{:S(2)}) collective-permute-start(f32[8,2,128,128]{3,2,1,0:T(8,128)} %get-tuple-element.35), channel_id=1, source_target_pairs={{0,1},{1,0},{2,3},{3,2},{4,5},{5,4},{6,7},{7,6},{8,9},{9,8},{10,11... | collective-permute-start | bytes 3145736 | tf_op jit(solution)/shard_map/ppermute | solution.py:429
  22.3 25.2 %collective-permute-start = (f32[6,2,128,128]{3,2,1,0:T(8,128)}, f32[6,2,128,128]{3,2,1,0:T(8,128)}, u32[]{:S(2)}, u32[]{:S(2)}) collective-permute-start(f32[6,2,128,128]{3,2,1,0:T(8,128)} %get-tuple-element.29), channel_id=1, source_target_pairs={{0,12},{2,14},{4,0},{6,2},{8,4},{10,6},{12,8},{14,10},{1,13},{3,15... | collective-permute-start | bytes 2359304 | tf_op jit(solution)/shard_map/ppermute | solution.py:429
  22.8 29.2 %collective-permute-start.4 = (f32[2,2,128,128]{3,2,1,0:T(8,128)}, f32[2,2,128,128]{3,2,1,0:T(8,128)S(1)}, u32[]{:S(2)}, u32[]{:S(2)}) collective-permute-start(f32[2,2,128,128]{3,2,1,0:T(8,128)} %get-tuple-element.41), channel_id=1, source_target_pairs={{0,12},{2,14},{4,0},{6,2},{8,4},{10,6},{12,8},{14,10},{1,13},{3,15... | collective-permute-start | bytes 786440 | tf_op jit(solution)/shard_map/ppermute | solution.py:429
  23.3 1.6 %copy-start = (f32[16,2,128,128]{3,2,1,0:T(8,128)S(1)}, f32[16,2,128,128]{3,2,1,0:T(8,128)}, u32[]{:S(2)}) copy-start(f32[16,2,128,128]{3,2,1,0:T(8,128)} %get-tuple-element.23.rotation_ref.own_ref) | copy-start | bytes 6291460
  24.9 2.2 %copy-start.2 = (f32[16,2,2,128,128]{4,3,2,1,0:T(8,128)S(1)}, f32[16,2,2,128,128]{4,3,2,1,0:T(8,128)}, u32[]{:S(2)}) copy-start(f32[16,2,2,128,128]{4,3,2,1,0:T(8,128)} %correlation_ref.1) | copy-start | bytes 12582916
  29.6 6.8 %copy-start.1 = (f32[16,2,128,128]{3,2,1,0:T(8,128)S(1)}, f32[16,2,128,128]{3,2,1,0:T(8,128)}, u32[]{:S(2)}) copy-start(f32[16,2,128,128]{3,2,1,0:T(8,128)} %get-tuple-element.23.rotation_ref.own_ref) | copy-start | bytes 6291460
  52.3 3.1 %collective-permute-start.7 = (f32[2,128]{1,0:T(2,128)S(1)}, f32[2,128]{1,0:T(2,128)S(1)}, u32[]{:S(2)}, u32[]{:S(2)}) collective-permute-start(f32[2,128]{1,0:T(2,128)S(1)} %get-tuple-element.43), channel_id=1, source_target_pairs={{0,3},{1,2},{2,1},{3,0},{4,7},{5,6},{6,5},{7,4},{8,11},{9,10},{10,... | collective-permute-start | bytes 3080 | tf_op jit(solution)/shard_map/ppermute | solution.py:439
  52.4 3.6 %collective-permute-start.6 = (f32[2,128]{1,0:T(2,128)S(1)}, f32[2,128]{1,0:T(2,128)S(1)}, u32[]{:S(2)}, u32[]{:S(2)}) collective-permute-start(f32[2,128]{1,0:T(2,128)S(1)} %get-tuple-element.43), channel_id=1, source_target_pairs={{0,2},{1,3},{2,0},{3,1},{4,6},{5,7},{6,4},{7,5},{8,10},{9,11},{10,... | collective-permute-start | bytes 3080 | tf_op jit(solution)/shard_map/ppermute | solution.py:439
  53.9 2.1 %collective-permute-start.5 = (f32[2,128]{1,0:T(2,128)S(1)}, f32[2,128]{1,0:T(2,128)S(1)}, u32[]{:S(2)}, u32[]{:S(2)}) collective-permute-start(f32[2,128]{1,0:T(2,128)S(1)} %get-tuple-element.43), channel_id=1, source_target_pairs={{0,1},{1,0},{2,3},{3,2},{4,5},{5,4},{6,7},{7,6},{8,9},{9,8},{10,11... | collective-permute-start | bytes 3080 | tf_op jit(solution)/shard_map/ppermute | solution.py:439
  56.0 4.0 %collective-permute-start.8 = (f32[2,128]{1,0:T(2,128)S(1)}, f32[2,128]{1,0:T(2,128)S(1)}, u32[]{:S(2)}, u32[]{:S(2)}) collective-permute-start(f32[2,128]{1,0:T(2,128)S(1)} %add_add_fusion), channel_id=1, source_target_pairs={{0,9},{1,8},{2,11},{3,10},{4,13},{5,12},{6,15},{7,14},{8,1},{9,0},... | collective-permute-start | bytes 3080 | tf_op jit(solution)/shard_map/ppermute | solution.py:439
  60.0 3.1 %collective-permute-start.9 = (f32[2,128]{1,0:T(2,128)S(1)}, f32[2,128]{1,0:T(2,128)S(1)}, u32[]{:S(2)}, u32[]{:S(2)}) collective-permute-start(f32[2,128]{1,0:T(2,128)S(1)} %add.37.first_ref), channel_id=1, source_target_pairs={{0,5},{1,4},{2,7},{3,6},{4,1},{5,0},{6,3},{7,2},{8,13},{9,12},{10,... | collective-permute-start | bytes 3080 | tf_op jit(solution)/shard_map/ppermute | solution.py:439
